TPU v7x, 32 devices: a whole 2x2x4 slice. The times are simulated.
32 devices in a mesh: seq: 16 (over z, x, core), res: 2 (over y).
Axes of the slice: x: 2, y: 2, z: 4, core: 2. Of those that a mesh axis runs over, the one named last changes fastest.
Arguments:
- embedded_aligned_rows: bfloat16 [48, 256, 768], P('seq', 'res'), may hold values from -12 to 12
- norm_multiplier: float32 [768], replicated, may hold values from 0.1 to 1.9
- asker_projector: bfloat16 [768, 768], replicated, may hold values from -1 to 1
- matcher_projector: bfloat16 [768, 768], replicated, may hold values from -1 to 1
- content_projector: bfloat16 [768, 768], replicated, may hold values from -0.21875 to 0.21875
- final_projector: bfloat16 [768, 768], replicated, may hold values from -0.21875 to 0.21875
Outputs:
- mixed: bfloat16 [48, 256, 768], P('seq', 'res')
All inputs are finite; a program needn't handle non-finite values.
Results may differ from a plain program's by a relative error of at most 0.01.
Values may be sent and summed in bfloat16 or wider, within the bound.
No kernel may reach another device: no remote copies, remote signals or barrier semaphores. Data moves between devices by JAX's collectives and lax.ppermute only.
A program may use at most 64 MiB of HBM per device.

v0:
```python
import jax
import jax.numpy as jnp
from jax import lax
from jax.sharding import PartitionSpec as P

HEADS = 12


def standardize_rows(embedded_aligned_rows, norm_multiplier):
    content_array = embedded_aligned_rows.astype(jnp.float32)
    center = content_array - jnp.mean(content_array, axis=-1, keepdims=True)
    spread = jnp.mean(center * center, axis=-1, keepdims=True)
    return (center / jnp.sqrt(spread + 1e-05) * norm_multiplier).astype(jnp.bfloat16)


def body(
    embedded_aligned_rows,
    norm_multiplier,
    asker_projector,
    matcher_projector,
    content_projector,
    final_projector,
):
    row_portion, column_portion, embedding_dimension = embedded_aligned_rows.shape
    heads = HEADS
    hsize = embedding_dimension // heads
    unrolled_array = standardize_rows(embedded_aligned_rows, norm_multiplier).reshape(
        row_portion * column_portion, embedding_dimension
    )
    query = jnp.dot(unrolled_array, asker_projector, preferred_element_type=jnp.float32).astype(
        jnp.bfloat16
    )
    query = query.reshape(row_portion, column_portion, heads, hsize)
    key_local = jnp.dot(
        unrolled_array, matcher_projector, preferred_element_type=jnp.float32
    ).astype(jnp.bfloat16)
    key_local = key_local.reshape(row_portion, column_portion, embedding_dimension)
    value_local = jnp.dot(
        unrolled_array, content_projector, preferred_element_type=jnp.float32
    ).astype(jnp.bfloat16)
    value_local = value_local.reshape(row_portion, column_portion, embedding_dimension)
    total_seqs = row_portion * lax.axis_size("seq")
    scale = 1.0 / (jnp.sqrt(jnp.float32(hsize)) * jnp.sqrt(jnp.float32(total_seqs)))
    key_all, value_all = (
        lax.all_gather(key_local, "res", axis=1, tiled=True),
        lax.all_gather(value_local, "res", axis=1, tiled=True),
    )
    keys = key_all.reshape(row_portion, key_all.shape[1], heads, hsize)
    logits = jnp.einsum("sihe,sjhe->hij", query, keys, preferred_element_type=jnp.float32)
    share = lax.psum_scatter(logits, "seq", scatter_dimension=1, tiled=True)
    share_probs = jax.nn.softmax(share * scale, axis=-1).astype(jnp.bfloat16)
    probs = lax.all_gather(share_probs, "seq", axis=1, tiled=True)
    content_array = value_all.reshape(row_portion, value_all.shape[1], heads, hsize)
    attended = jnp.einsum(
        "hij,sjhe->sihe", probs, content_array, preferred_element_type=jnp.float32
    )
    attended = attended.astype(jnp.bfloat16).reshape(
        row_portion * column_portion, embedding_dimension
    )
    mixed = jnp.dot(attended, final_projector, preferred_element_type=jnp.float32).astype(
        jnp.bfloat16
    )
    return mixed.reshape(row_portion, column_portion, embedding_dimension)


def solution(mesh):
    placed = (P("seq", "res", None), P(), P(), P(), P(), P())
    return jax.shard_map(
        body, mesh=mesh, in_specs=placed, out_specs=P("seq", "res", None), check_vma=False
    )
```

profile of v0, /device:TPU:0, one launch (start us, length us, event | category | flops | bytes accessed | tf_op | source)
XLA Modules:
  0.0 134.4 jit_solution(8885785728018542669)
XLA Ops:
  6.5 1.4 %convert_reduce_fusion = f32[3,128]{1,0:T(4,128)S(1)} fusion(bf16[3,128,768]{2,1,0:T(8,128)(2,1)} %param.6), kind=kLoop, calls=%fused_computation.4 | loop fusion | flops 589440 | bytes 591360 | tf_op jit(solution)/shard_map/reduce_sum | solution.py:11
  7.9 1.4 %fusion.5 = f32[3,128]{1,0:T(4,128)S(1)} fusion(bf16[3,128,768]{2,1,0:T(8,128)(2,1)} %param.6, f32[3,128]{1,0:T(4,128)S(1)} %broadcast_multiply_fusion), kind=kLoop, calls=%fused_computation.13 | loop fusion | flops 1179264 | bytes 592896 | tf_op jit(solution)/shard_map/reduce_sum | solution.py:12
  9.3 0.2 fusion.7
  9.6 0.6 convolution_convert_fusion.2
  10.2 1.1 copy.10
  11.3 0.0 all-gather.5.cloned.1.call-update
  11.3 0.0 reduce-scatter.2.cloned.1.call-start
  11.3 0.3 copy-done.3
  11.7 1.4 %convolution_convert_fusion.3 = bf16[384,768]{1,0:T(8,128)(2,1)} fusion(bf16[384,768]{1,0:T(8,128)(2,1)S(1)} %bitcast.33, bf16[768,768]{1,0:T(8,128)(2,1)S(1)} %copy-done.3), kind=kOutput, calls=%fused_computation.10 | convolution fusion | flops 453279744 | bytes 2359296 | tf_op jit(solution)/shard_map/dot_general | solution.py:30
  13.1 1.9 %reshape.49 = bf16[3,128,12,64]{3,2,1,0:T(8,128)(2,1)S(1)} reshape(bf16[384,768]{1,0:T(8,128)(2,1)} %convolution_convert_fusion.3) | data formatting | bytes 1179648 | tf_op jit(solution)/shard_map/reshape | solution.py:33
  15.1 21.8 %all-gather.5.cloned.1.call-done = bf16[3,256,768]{1,2,0:T(8,128)(2,1)} async-done(((bf16[3,128,768]{1,2,0:T(8,128)(2,1)}), bf16[3,256,768]{1,2,0:T(8,128)(2,1)}) %all-gather.5.cloned.1.call-update) | async-done | bytes 1179664 | tf_op jit(solution)/shard_map/all_gather | solution.py:45
  36.9 2.9 %convolution_bitcast_fusion = f32[12,128,256]{2,1,0:T(8,128)} fusion(bf16[3,128,12,64]{3,2,1,0:T(8,128)(2,1)S(1)} %reshape.49, bf16[3,256,12,64]{1,3,2,0:T(8,128)(2,1)} %bitcast.30), kind=kOutput, calls=%fused_computation.2 | convolution fusion | flops 150994944 | bytes 3342336 | tf_op jit(solution)/shard_map/sihe,sjhe->hij/dot_general | solution.py:49
  39.8 0.0 all-gather.3.cloned.1.call-start
  39.9 1.2 copy-done.4
  41.1 0.6 convolution_convert_fusion.4
  41.7 1.1 copy.8
  42.8 57.4 %reduce-scatter.2.cloned.1.call-done = f32[12,8,256]{2,1,0:T(8,128)} async-done(((f32[12,128,256]{2,1,0:T(8,128)}), f32[12,8,256]{2,1,0:T(8,128)}) %reduce-scatter.2.cloned.1.call-update) | async-done | bytes 98320 | tf_op jit(solution)/shard_map/reduce_scatter | solution.py:50
  100.1 1.1 fusion.14
  101.2 21.5 %all_gather.11 = bf16[12,128,256]{2,1,0:T(8,128)(2,1)S(1)} all-gather(bf16[12,8,256]{2,1,0:T(8,128)(2,1)S(1)} %fusion.14), channel_id=1, replica_groups=mesh['seq'=16,'res'=2] {'seq'}, dimensions={1}, use_global_device_ids=true | all-gather | bytes 835584 | tf_op jit(solution)/shard_map/all_gather | solution.py:52
  122.7 0.7 all-gather.3.cloned.1.call-done
  123.4 1.7 %fusion.4 = bf16[3,128,12,64]{1,3,0,2:T(8,128)(2,1)S(1)} fusion(bf16[3,256,12,64]{1,3,2,0:T(8,128)(2,1)} %bitcast.37, bf16[12,128,256]{2,1,0:T(8,128)(2,1)S(1)} %all_gather.11), kind=kOutput, calls=%fused_computation.12 | convolution fusion | flops 151289856 | bytes 2555904 | tf_op jit(solution)/shard_map/hij,sjhe->sihe/dot_general | solution.py:54
  125.2 0.5 copy.14
  125.7 0.7 copy-done.5
  126.4 1.5 %convolution_convert_fusion = bf16[384,768]{1,0:T(8,128)(2,1)} fusion(bf16[768,768]{1,0:T(8,128)(2,1)S(1)} %copy-done.5, bf16[96,8,3,128]{3,2,1,0:T(4,128)(2,1)S(1)} %bitcast.31), kind=kOutput, calls=%fused_computation.7 | convolution fusion | flops 453279744 | bytes 2359296 | tf_op jit(solution)/shard_map/dot_general | solution.py:60
  (14 shorter events, 0.1 us)
Async XLA Ops:
  6.5 3.0 %copy-start = (bf16[768,768]{1,0:T(8,128)(2,1)S(1)}, bf16[768,768]{1,0:T(8,128)(2,1)}, u32[]{:S(2)}) copy-start(bf16[768,768]{1,0:T(8,128)(2,1)} %param.9) | copy-start | bytes 3538948
  6.5 2.8 %copy-start.1 = (bf16[3,128,768]{2,1,0:T(8,128)(2,1)S(1)}, bf16[3,128,768]{2,1,0:T(8,128)(2,1)}, u32[]{:S(2)}) copy-start(bf16[3,128,768]{2,1,0:T(8,128)(2,1)} %param.6) | copy-start | bytes 1769476
  6.5 2.8 %copy-start.2 = (f32[768]{0:T(1024)S(1)}, f32[768]{0:T(1024)}, u32[]{:S(2)}) copy-start(f32[768]{0:T(1024)} %param.7) | copy-start | bytes 9220
  6.5 30.4 %all-gather.5.cloned.1.call-start = ((), (), s32[]{:S(2)}) async-start(), calls=%async_computation.2 | async-start | bytes 1769472 | tf_op jit(solution)/shard_map/all_gather | solution.py:45
  10.2 1.5 %copy-start.3 = (bf16[768,768]{1,0:T(8,128)(2,1)S(1)}, bf16[768,768]{1,0:T(8,128)(2,1)}, u32[]{:S(2)}) copy-start(bf16[768,768]{1,0:T(8,128)(2,1)} %param.8) | copy-start | bytes 3538948
  11.3 88.8 %reduce-scatter.2.cloned.1.call-start = ((), (), s32[]{:S(2)}) async-start(), calls=%async_computation.3 | async-start | bytes 1671168 | tf_op jit(solution)/shard_map/reduce_scatter | solution.py:50
  39.8 1.3 copy-start.4
  39.8 83.6 %all-gather.3.cloned.1.call-start = ((), (), s32[]{:S(2)}) async-start(), calls=%async_computation.1 | async-start | bytes 1769472 | tf_op jit(solution)/shard_map/all_gather | solution.py:46
  125.2 1.3 copy-start.5
Sparse Core Ops, SparseCore 0:
  11.4 25.4 all-gather.4
  40.6 59.5 reduce-scatter.1
  101.7 21.6 all-gather.2
where the time goes:
time: 135 us; the launch traced here: 134 us
  waiting for transfers between devices  79.9 us (59%)
  blocking collectives  21.5 us (16%)
  between operations  13.2 us (10%)
  matrix products  8.81 us (7%)
  local copies, waits for them, and re-layouts  6.86 us (5%)
  other arithmetic  4.05 us (3%)
    reduce_scatter x1, waiting for transfers between devices, body(): share = lax.psum_scatter(logits, 'seq', scatter_dimension=1, tiled=True)  57.4 us
    all_gather x1, waiting for transfers between devices, body(): lax.all_gather(key_local, 'res', axis=1, tiled=True)  21.8 us
    all_gather x1, blocking collectives, body(): probs = lax.all_gather(share_probs, 'seq', axis=1, tiled=True)  21.5 us
    dot_general x1, matrix products, body(): jnp.einsum('sihe,sjhe->hij', query, keys, preferred_element_type=jnp.floa...  2.9 us
  transfers between devices with their start and end apart: 3, of which 3 were waited for; matrix products, arithmetic and copies ran while one was open for 5% of the time, Pallas kernels for 0%

commit v1 on v0

v1 whole, which is shorter than its diff:
```python
import functools

import jax
import jax.numpy as jnp
from jax import lax
from jax.experimental import pallas as pl
from jax.experimental.pallas import tpu as pltpu
from jax.sharding import PartitionSpec as P

HEADS = 12
LANES = 128
CORES = 2

VMEM = pl.BlockSpec(memory_space=pltpu.VMEM)
SMEM = pl.BlockSpec(memory_space=pltpu.SMEM)
PARAMS = pltpu.CompilerParams(vmem_limit_bytes=48 << 20)


def standardize(x, gain):
    x = x.astype(jnp.float32)
    center = x - jnp.mean(x, axis=-1, keepdims=True)
    spread = jnp.mean(center * center, axis=-1, keepdims=True)
    return (center * (1.0 / jnp.sqrt(spread + 1e-05)) * gain).astype(jnp.bfloat16)


def rows_of(x_ref, gain_ref):
    s, r, d = x_ref.shape
    return standardize(x_ref[...].reshape(s * r, d), gain_ref[...])


def project(rows, w_ref):
    return jnp.dot(rows, w_ref[...], preferred_element_type=jnp.float32).astype(jnp.bfloat16)


def lane_group(y, s, r, group):
    return jnp.concatenate(
        [y[i * r : (i + 1) * r, group * LANES : (group + 1) * LANES] for i in range(s)], axis=1
    )


def write_scores(core, q_ref, k_ref, send_ref, keep_ref):
    groups, packed, _ = q_ref.shape
    blocks, heads, share, cols = keep_ref.shape
    per_core = groups // CORES
    pack = heads // per_core
    r = packed // pack
    for out_ref, side in ((send_ref, 1 - core), (keep_ref, core)):
        for t in range(per_core):
            g = side * per_core + t
            part = lax.dot_general(
                q_ref[g], k_ref[g], (((1,), (1,)), ((), ())), preferred_element_type=jnp.float32
            )
            for h in range(pack):
                out_ref[:, t * pack + h] = part[h * r : (h + 1) * r].reshape(blocks, share, cols)


def own_kernel(ids, x_ref, gain_ref, wq_ref, wk_ref, q_ref, send_ref, keep_ref, k_scr):
    s, r, d = x_ref.shape
    groups = d // LANES
    hsize = d // HEADS
    rows = rows_of(x_ref, gain_ref)
    q = project(rows, wq_ref)
    k = project(rows, wk_ref)
    lane = lax.broadcasted_iota(jnp.int32, (r, s * LANES), 1) % LANES // hsize
    for g in range(groups):
        k_scr[g] = lane_group(k, s, r, g)
        both = lane_group(q, s, r, g)
        for h in range(LANES // hsize):
            q_ref[g, h * r : (h + 1) * r] = jnp.where(lane == h, both, jnp.zeros_like(both))
    write_scores(ids[0], q_ref, k_scr, send_ref, keep_ref)


def other_kernel(ids, x_ref, gain_ref, wk_ref, q_ref, send_ref, keep_ref, k_scr):
    s, r, d = x_ref.shape
    k = project(rows_of(x_ref, gain_ref), wk_ref)
    for g in range(d // LANES):
        k_scr[g] = lane_group(k, s, r, g)
    write_scores(ids[0], q_ref, k_scr, send_ref, keep_ref)


def value_kernel(x_ref, gain_ref, wv_ref, v_ref):
    s, r, d = x_ref.shape
    v = project(rows_of(x_ref, gain_ref), wv_ref)
    for g in range(d // LANES):
        v_ref[g] = lane_group(v, s, r, g)


def merge_kernel(n, *refs):
    keep, got, out_ref = refs[:n], refs[n : 2 * n], refs[2 * n]
    for h in range(out_ref.shape[1]):
        total = jnp.concatenate([a[:, h] + b[:, h] for a, b in zip(keep, got)], axis=-1)
        total = total - jnp.max(total, axis=-1, keepdims=True)
        out_ref[:, h] = total.astype(out_ref.dtype)


def softmax_kernel(scale, parts_ref, out_ref):
    blocks = parts_ref.shape[0]
    for h in range(parts_ref.shape[1]):
        logits = jnp.sum(parts_ref[:, h].astype(jnp.float32), axis=0) * scale
        p = jnp.exp(logits - jnp.max(logits, axis=-1, keepdims=True))
        p = (p / jnp.sum(p, axis=-1, keepdims=True)).astype(out_ref.dtype)
        for b in range(blocks):
            out_ref[b, h] = p


def mix_kernel(n, ids, *refs):
    mine_ref, got_ref = refs[:2]
    v_refs = refs[2 : 2 + n]
    wf_ref, out_ref, att_scr = refs[2 + n :]
    s, r, d = out_ref.shape
    groups = d // LANES
    hsize = d // HEADS
    pack = LANES // hsize
    blocks, heads, share, cols = mine_ref.shape
    per_core = groups // CORES
    lane = lax.broadcasted_iota(jnp.int32, (r, s * LANES), 1) % LANES // hsize
    for p_ref, side in ((mine_ref, ids[0]), (got_ref, 1 - ids[0])):
        for t in range(per_core):
            g = side * per_core + t
            p = jnp.concatenate(
                [p_ref[:, t * pack + h].reshape(r, cols) for h in range(pack)], axis=0
            )
            v = jnp.concatenate([v_ref[g] for v_ref in v_refs], axis=0)
            both = jnp.dot(p, v, preferred_element_type=jnp.float32)
            got = both[:r]
            for h in range(1, pack):
                got = jnp.where(lane == h, both[h * r : (h + 1) * r], got)
            att_scr[g] = got.astype(jnp.bfloat16)
    rows = jnp.concatenate(
        [
            jnp.concatenate(
                [att_scr[g, :, i * LANES : (i + 1) * LANES] for g in range(groups)], axis=1
            )
            for i in range(s)
        ],
        axis=0,
    )
    mixed = jnp.dot(rows, wf_ref[...], preferred_element_type=jnp.float32)
    out_ref[...] = mixed.astype(out_ref.dtype).reshape(s, r, d)


def call(kernel, out_shape, args, ids=None, scratch=(), flops=0, name=None):
    ins = ((ids,) if ids is not None else ()) + tuple(args)
    specs = ([SMEM] if ids is not None else []) + [VMEM] * len(args)
    moved = sum(a.size * a.dtype.itemsize for a in args)
    return pl.pallas_call(
        kernel,
        out_shape=out_shape,
        in_specs=specs,
        out_specs=jax.tree.map(lambda _: VMEM, out_shape),
        scratch_shapes=list(scratch),
        compiler_params=PARAMS,
        cost_estimate=pl.CostEstimate(flops=flops, bytes_accessed=moved, transcendentals=0),
        name=name,
    )(*ins)


def body(n_seq, n_res, x, gain, wq, wk, wv, wf):
    s, r, d = x.shape
    groups = d // LANES
    hsize = d // HEADS
    pack = LANES // hsize
    blocks = n_seq // CORES
    share = r // blocks
    heads = HEADS // CORES
    f32, bf16 = jnp.float32, jnp.bfloat16
    shape = jax.ShapeDtypeStruct

    gain = gain.reshape(1, d)
    core = lax.axis_index("seq") % CORES
    ids = core.astype(jnp.int32).reshape(1)
    swap = [(i, i ^ 1) for i in range(n_seq)]
    peers = [[b * CORES + c for b in range(blocks)] for c in range(CORES)]

    def exchange(y):
        return lax.all_to_all(y, "seq", 0, 0, tiled=True, axis_index_groups=peers)

    others = [
        lax.ppermute(x, "res", [(i, (i + k) % n_res) for i in range(n_res)])
        for k in range(1, n_res)
    ]
    part = shape((blocks, heads, share, r), f32)
    dots = 2 * s * r * d
    q, send, keep = call(
        own_kernel,
        (shape((groups, pack * r, s * LANES), bf16), part, part),
        (x, gain, wq, wk),
        ids,
        scratch=[pltpu.VMEM((groups, r, s * LANES), bf16)],
        flops=dots * (2 * d + r),
        name="own_scores",
    )
    keeps, gots = [keep], [lax.ppermute(send, "seq", swap)]
    for other in others:
        send, keep = call(
            other_kernel,
            (part, part),
            (other, gain, wk, q),
            ids,
            scratch=[pltpu.VMEM((groups, r, s * LANES), bf16)],
            flops=dots * (d + r),
            name="other_scores",
        )
        keeps.append(keep)
        gots.append(lax.ppermute(send, "seq", swap))
    values = [
        call(
            value_kernel,
            shape((groups, r, s * LANES), bf16),
            (block, gain, wv),
            flops=dots * d,
            name="values",
        )
        for block in [x] + others
    ]
    cols = r * n_res
    pieces = shape((blocks, heads, share, cols), bf16)
    partial = call(
        functools.partial(merge_kernel, n_res), pieces, (*keeps, *gots), name="merge_scores"
    )
    scale = float(hsize * s * n_seq) ** -0.5
    probs = call(
        functools.partial(softmax_kernel, scale), pieces, (exchange(partial),), name="softmax"
    )
    mine = exchange(probs)
    got = lax.ppermute(mine, "seq", swap)
    return call(
        functools.partial(mix_kernel, n_res),
        shape((s, r, d), bf16),
        (mine, got, *values, wf),
        ids,
        scratch=[pltpu.VMEM((groups, r, s * LANES), bf16)],
        flops=dots * (d + cols),
        name="mix",
    )


def solution(mesh):
    placed = (P("seq", "res", None), P(), P(), P(), P(), P())
    return jax.shard_map(
        functools.partial(body, mesh.shape["seq"], mesh.shape["res"]),
        mesh=mesh,
        in_specs=placed,
        out_specs=P("seq", "res", None),
        check_vma=False,
    )
```

time: 135 us -> 58.3 us (0.43)
  waiting for transfers between devices: 79.9 us -> 8.98 us
  between operations: 13.2 us -> 0.1 us
  blocking collectives: 21.5 us -> 33.3 us
  matrix products: 8.81 us -> 0 us
  Pallas kernels: 0 us -> 7.8 us
  other arithmetic: 4.05 us -> 0 us
  starting transfers between devices: 0.09 us -> 3.14 us
  local copies, waits for them, and re-layouts: 6.86 us -> 4.65 us
    reduce_scatter x1 -> x0, waiting for transfers between devices: 57.4 us -> none  [body(): share = lax.psum_scatter(logits, 'seq', scatter_dimension=1, tiled=True)]
    all_to_all x0 -> x2, blocking collectives: none -> 33.3 us  [exchange(): return lax.all_to_all(y, 'seq', 0, 0, tiled=True, axis_index_groups=peers)]
    all_gather x2 -> x0, waiting for transfers between devices: 22.5 us -> none  [the longest x1 21.8 us: body(): lax.all_gather(key_local, 'res', axis=1, tiled=True)]
    all_gather x1 -> x0, blocking collectives: 21.5 us -> none  [body(): probs = lax.all_gather(share_probs, 'seq', axis=1, tiled=True)]
    ppermute x0 -> x4, waiting for transfers between devices: none -> 8.98 us  [the longest x1 7.27 us: body(): lax.ppermute(x, 'res', [(i, (i + k) % n_res) for i in range(n_res)])]
    dot_general x6 -> x0, matrix products: 8.81 us -> none  [the longest x1 2.9 us: body(): jnp.einsum('sihe,sjhe->hij', query, keys, preferred_element_type=jnp.floa...]
    pallas_call x0 -> x7, Pallas kernels: none -> 7.8 us  [call(): pl.pallas_call(kernel, out_shape=out_shape, in_specs=specs, out_specs=jax...]
    reshape x3 -> x1, local copies, waits for them, and re-layouts: 4.04 us -> 0.69 us  [body(): gain = gain.reshape(1, d)]
  transfers between devices with their start and end apart: 3 -> 4, of which waited for: 3 -> 2; matrix products, arithmetic and copies ran while one was open for 5% -> 1% of each run, Pallas kernels for 0% -> 9%
where the time goes in v1:
time: 58.3 us; the launch traced here: 58 us
  blocking collectives  33.3 us (57%)
  waiting for transfers between devices  8.98 us (15%)
  Pallas kernels  7.8 us (13%)
  local copies, waits for them, and re-layouts  4.65 us (8%)
  starting transfers between devices  3.14 us (5%)
    all_to_all x2, blocking collectives, exchange(): return lax.all_to_all(y, 'seq', 0, 0, tiled=True, axis_index_groups=peers)  33.3 us
    pallas_call x7, Pallas kernels, call(): pl.pallas_call(kernel, out_shape=out_shape, in_specs=specs, out_specs=jax...  7.8 us
    ppermute x1, waiting for transfers between devices, body(): lax.ppermute(x, 'res', [(i, (i + k) % n_res) for i in range(n_res)])  7.27 us
    unnamed x14, local copies, waits for them, and re-layouts  3.96 us
    ppermute x1, starting transfers between devices, body(): lax.ppermute(x, 'res', [(i, (i + k) % n_res) for i in range(n_res)])  3 us
    ppermute x1, waiting for transfers between devices, body(): gots.append(lax.ppermute(send, 'seq', swap))  1.7 us
  transfers between devices with their start and end apart: 4, of which 2 were waited for; matrix products, arithmetic and copies ran while one was open for 1% of the time, Pallas kernels for 9%

profile of v1, /device:TPU:0, one launch (start us, length us, event | category | flops | bytes accessed | tf_op | source)
XLA Modules:
  0.0 58.0 jit_solution(17703828361432376208)
XLA Ops:
  0.0 3.0 %collective-permute-start = (bf16[3,128,768]{2,1,0:T(8,128)(2,1)}, bf16[3,128,768]{2,1,0:T(8,128)(2,1)S(1)}, u32[]{:S(2)}, u32[]{:S(2)}) collective-permute-start(bf16[3,128,768]{2,1,0:T(8,128)(2,1)} %x_ref.3), channel_id=1, source_target_pairs={{0,1},{1,0},{2,3},{3,2},{4,5},{5,4},{6,7},{7,6},{8,9},{9,8},{10,11... | collective-permute-start | bytes 1769480 | tf_op jit(solution)/shard_map/ppermute | solution.py:179
  3.0 0.7 %reshape.7.gain_ref = f32[1,768]{1,0:T(1,128)S(1)} reshape(f32[768]{0:T(1024)} %param.7) | data formatting | bytes 6144 | tf_op jit(solution)/shard_map/reshape | solution.py:169
  3.7 1.3 %copy-done.1 = bf16[768,768]{1,0:T(8,128)(2,1)S(1)} copy-done((bf16[768,768]{1,0:T(8,128)(2,1)S(1)}, bf16[768,768]{1,0:T(8,128)(2,1)}, u32[]{:S(2)}) %copy-start.1) | copy-done | bytes 1179672
  5.0 1.1 %copy-done.4 = bf16[3,128,768]{2,1,0:T(8,128)(2,1)S(1)} copy-done((bf16[3,128,768]{2,1,0:T(8,128)(2,1)S(1)}, bf16[3,128,768]{2,1,0:T(8,128)(2,1)}, u32[]{:S(2)}) %copy-start.4) | copy-done | bytes 589848
  6.0 1.3 %copy-done.6 = bf16[768,768]{1,0:T(8,128)(2,1)S(1)} copy-done((bf16[768,768]{1,0:T(8,128)(2,1)S(1)}, bf16[768,768]{1,0:T(8,128)(2,1)}, u32[]{:S(2)}) %copy-start.6) | copy-done | bytes 1179672
  7.3 1.9 %own_scores.1 = (bf16[6,256,384]{2,1,0:T(8,128)(2,1)S(1)}, f32[8,6,16,128]{3,2,1,0:T(8,128)S(1)}, f32[8,6,16,128]{3,2,1,0:T(8,128)S(1)}) custom-call(s32[1]{0:T(128)} %bitcast.ids, bf16[3,128,768]{2,1,0:T(8,128)(2,1)S(1)} %copy-done.4, f32[1,768]{1,0:T(1,128)S(1)} %reshape.7.gain_ref, bf16[768,768]{1,0:T(8,128)(2,1)S(1)} %copy-done.6, ...), custom_call_target="tpu_custom_call" | custom-call | flops 981467136 | bytes 2952192 | tf_op jit(solution)/shard_map/own_scores/pallas_call | solution.py:146
  9.2 0.1 collective-permute-start.1
  9.3 7.3 %collective-permute-done.x_ref = bf16[3,128,768]{2,1,0:T(8,128)(2,1)S(1)} collective-permute-done((bf16[3,128,768]{2,1,0:T(8,128)(2,1)}, bf16[3,128,768]{2,1,0:T(8,128)(2,1)S(1)}, u32[]{:S(2)}, u32[]{:S(2)}) %collective-permute-start) | collective-permute-done | bytes 589856 | tf_op jit(solution)/shard_map/ppermute | solution.py:179
  16.5 1.7 %other_scores.1 = (f32[8,6,16,128]{3,2,1,0:T(8,128)S(1)}, f32[8,6,16,128]{3,2,1,0:T(8,128)S(1)}) custom-call(s32[1]{0:T(128)} %bitcast.ids, bf16[3,128,768]{2,1,0:T(8,128)(2,1)S(1)} %collective-permute-done.x_ref, f32[1,768]{1,0:T(1,128)S(1)} %reshape.7.gain_ref, bf16[768,768]{1,0:T(8,128)(2,1)S(1)} %copy-done.2, ...), custom_call_target="tpu_custom_call" | custom-call | flops 528482304 | bytes 2952192 | tf_op jit(solution)/shard_map/other_scores/pallas_call | solution.py:146
  18.2 0.1 collective-permute-start.2
  18.3 0.0 collective-permute-done.1.refs_2_
  18.3 1.7 %collective-permute-done.2.refs_3_ = f32[8,6,16,128]{3,2,1,0:T(8,128)S(1)} collective-permute-done((f32[8,6,16,128]{3,2,1,0:T(8,128)S(1)}, f32[8,6,16,128]{3,2,1,0:T(8,128)S(1)}, u32[]{:S(2)}, u32[]{:S(2)}) %collective-permute-start.2) | collective-permute-done | bytes 393248 | tf_op jit(solution)/shard_map/ppermute | solution.py:205
  20.0 0.2 merge_scores.1
  20.2 0.0 copy-start
  20.2 0.0 copy-start.5
  20.2 18.3 %all_to_all.10.parts_ref = bf16[8,6,16,256]{3,2,1,0:T(8,128)(2,1)S(1)} all-to-all(bf16[8,6,16,256]{3,2,1,0:T(8,128)(2,1)S(1)} %merge_scores.1), channel_id=1, replica_groups={{0,4,8,12,16,20,24,28},{2,6,10,14,18,22,26,30},{1,5,9,13,17,21,25,29},{..., dimensions={0} | all-to-all | bytes 786432 | tf_op jit(solution)/shard_map/all_to_all | solution.py:176
  38.5 0.2 softmax.1
  38.8 15.0 %all_to_all.11.refs_0_ = bf16[8,6,16,256]{3,2,1,0:T(8,128)(2,1)S(1)} all-to-all(bf16[8,6,16,256]{3,2,1,0:T(8,128)(2,1)S(1)} %softmax.1), channel_id=1, replica_groups={{0,4,8,12,16,20,24,28},{2,6,10,14,18,22,26,30},{1,5,9,13,17,21,25,29},{..., dimensions={0} | all-to-all | bytes 786432 | tf_op jit(solution)/shard_map/all_to_all | solution.py:176
  53.7 0.0 collective-permute-start.3
  53.8 0.9 %values.2.refs_2_ = bf16[6,128,384]{2,1,0:T(8,128)(2,1)S(1)} custom-call(bf16[3,128,768]{2,1,0:T(8,128)(2,1)S(1)} %copy-done.5, f32[1,768]{1,0:T(1,128)S(1)} %reshape.7.gain_ref, bf16[768,768]{1,0:T(8,128)(2,1)S(1)} %copy-done), custom_call_target="tpu_custom_call" | custom-call | flops 452984832 | bytes 1772544 | tf_op jit(solution)/shard_map/values/pallas_call | solution.py:146
  54.7 0.0 copy-start.3
  54.7 0.9 %values.3.refs_3_ = bf16[6,128,384]{2,1,0:T(8,128)(2,1)S(1)} custom-call(bf16[3,128,768]{2,1,0:T(8,128)(2,1)S(1)} %collective-permute-done.x_ref, f32[1,768]{1,0:T(1,128)S(1)} %reshape.7.gain_ref, bf16[768,768]{1,0:T(8,128)(2,1)S(1)} %copy-done), custom_call_target="tpu_custom_call" | custom-call | flops 452984832 | bytes 1772544 | tf_op jit(solution)/shard_map/values/pallas_call | solution.py:146
  55.6 0.3 copy-done.3
  56.0 2.0 %mix.1 = bf16[3,128,768]{2,1,0:T(8,128)(2,1)} custom-call(s32[1]{0:T(128)} %bitcast.ids, bf16[8,6,16,256]{3,2,1,0:T(8,128)(2,1)S(1)} %all_to_all.11.refs_0_, bf16[8,6,16,256]{3,2,1,0:T(8,128)(2,1)S(1)} %collective-permute-done.3.refs_1_, bf16[6,128,384]{2,1,0:T(8,128)(2,1)S(1)} %values.2.refs_2_, bf16[6,128,384]{2,1,0:T(8,128)(2,1)S(1)} %values.3.refs_3_, ...), custom_call_target="tpu_custom_call" | custom-call | flops 603979776 | bytes 3145728 | tf_op jit(solution)/shard_map/mix/pallas_call | solution.py:146
  (8 shorter events, 0.0 us)
Async XLA Ops:
  0.0 16.5 %collective-permute-start = (bf16[3,128,768]{2,1,0:T(8,128)(2,1)}, bf16[3,128,768]{2,1,0:T(8,128)(2,1)S(1)}, u32[]{:S(2)}, u32[]{:S(2)}) collective-permute-start(bf16[3,128,768]{2,1,0:T(8,128)(2,1)} %x_ref.3), channel_id=1, source_target_pairs={{0,1},{1,0},{2,3},{3,2},{4,5},{5,4},{6,7},{7,6},{8,9},{9,8},{10,11... | collective-permute-start | bytes 1769480 | tf_op jit(solution)/shard_map/ppermute | solution.py:179
  3.7 1.3 %copy-start.1 = (bf16[768,768]{1,0:T(8,128)(2,1)S(1)}, bf16[768,768]{1,0:T(8,128)(2,1)}, u32[]{:S(2)}) copy-start(bf16[768,768]{1,0:T(8,128)(2,1)} %wk_ref.3) | copy-start | bytes 3538948
  5.0 1.1 %copy-start.4 = (bf16[3,128,768]{2,1,0:T(8,128)(2,1)S(1)}, bf16[3,128,768]{2,1,0:T(8,128)(2,1)}, u32[]{:S(2)}) copy-start(bf16[3,128,768]{2,1,0:T(8,128)(2,1)} %x_ref.3) | copy-start | bytes 1769476
  6.0 1.3 %copy-start.6 = (bf16[768,768]{1,0:T(8,128)(2,1)S(1)}, bf16[768,768]{1,0:T(8,128)(2,1)}, u32[]{:S(2)}) copy-start(bf16[768,768]{1,0:T(8,128)(2,1)} %wq_ref.1) | copy-start | bytes 3538948
  7.3 9.2 %copy-start.2 = (bf16[768,768]{1,0:T(8,128)(2,1)S(1)}, bf16[768,768]{1,0:T(8,128)(2,1)}, u32[]{:S(2)}) copy-start(bf16[768,768]{1,0:T(8,128)(2,1)} %wk_ref.3) | copy-start | bytes 3538948
  9.2 9.1 %collective-permute-start.1 = (f32[8,6,16,128]{3,2,1,0:T(8,128)S(1)}, f32[8,6,16,128]{3,2,1,0:T(8,128)S(1)}, u32[]{:S(2)}, u32[]{:S(2)}) collective-permute-start(f32[8,6,16,128]{3,2,1,0:T(8,128)S(1)} %get-tuple-element.13), channel_id=1, source_target_pairs={{0,2},{2,0},{4,6},{6,4},{8,10},{10,8},{12,14},{14,12},{16,18},{18,... | collective-permute-start | bytes 1179656 | tf_op jit(solution)/shard_map/ppermute | solution.py:193
  18.2 1.8 %collective-permute-start.2 = (f32[8,6,16,128]{3,2,1,0:T(8,128)S(1)}, f32[8,6,16,128]{3,2,1,0:T(8,128)S(1)}, u32[]{:S(2)}, u32[]{:S(2)}) collective-permute-start(f32[8,6,16,128]{3,2,1,0:T(8,128)S(1)} %get-tuple-element.14), channel_id=1, source_target_pairs={{0,2},{2,0},{4,6},{6,4},{8,10},{10,8},{12,14},{14,12},{16,18},{18,... | collective-permute-start | bytes 1179656 | tf_op jit(solution)/shard_map/ppermute | solution.py:205
  20.2 33.5 %copy-start = (bf16[768,768]{1,0:T(8,128)(2,1)S(1)}, bf16[768,768]{1,0:T(8,128)(2,1)}, u32[]{:S(2)}) copy-start(bf16[768,768]{1,0:T(8,128)(2,1)} %wv_ref.3) | copy-start | bytes 3538948
  20.2 33.5 %copy-start.5 = (bf16[3,128,768]{2,1,0:T(8,128)(2,1)S(1)}, bf16[3,128,768]{2,1,0:T(8,128)(2,1)}, u32[]{:S(2)}) copy-start(bf16[3,128,768]{2,1,0:T(8,128)(2,1)} %x_ref.3) | copy-start | bytes 1769476
  53.7 1.9 %collective-permute-start.3 = (bf16[8,6,16,256]{3,2,1,0:T(8,128)(2,1)S(1)}, bf16[8,6,16,256]{3,2,1,0:T(8,128)(2,1)S(1)}, u32[]{:S(2)}, u32[]{:S(2)}) collective-permute-start(bf16[8,6,16,256]{3,2,1,0:T(8,128)(2,1)S(1)} %all_to_all.11.refs_0_), channel_id=1, source_target_pairs={{0,2},{2,0},{4,6},{6,4},{8,10},{10,8},{12,14},{14,12},{16,18},{18,... | collective-permute-start | bytes 1179656 | tf_op jit(solution)/shard_map/ppermute | solution.py:226
  54.7 1.3 %copy-start.3 = (bf16[768,768]{1,0:T(8,128)(2,1)S(1)}, bf16[768,768]{1,0:T(8,128)(2,1)}, u32[]{:S(2)}) copy-start(bf16[768,768]{1,0:T(8,128)(2,1)} %refs_4_.1) | copy-start | bytes 3538948

commit v2 on v0

v2 whole, which is shorter than its diff:
```python
import functools

import jax
import jax.numpy as jnp
from jax import lax
from jax.experimental import pallas as pl
from jax.experimental.pallas import tpu as pltpu
from jax.sharding import PartitionSpec as P

HEADS = 12
LANES = 128
CORES = 2


VMEM = pl.BlockSpec(memory_space=pltpu.VMEM)
ANY = pl.BlockSpec(memory_space=pl.ANY)
HBM = pl.BlockSpec(memory_space=pltpu.HBM)
PARAMS = pltpu.CompilerParams(vmem_limit_bytes=48 << 20)


def spot(inner):
    place = lax.axis_index("seq")
    return place & (CORES - 1), (place >> 1) & (inner - 1)


def standardize(x, gain):
    x = x.astype(jnp.float32)
    center = x - jnp.mean(x, axis=-1, keepdims=True)
    spread = jnp.mean(center * center, axis=-1, keepdims=True)
    return (center * (1.0 / jnp.sqrt(spread + 1e-05)) * gain).astype(jnp.bfloat16)


def rows_of(x_ref, gain_ref):
    s, r, d = x_ref.shape
    return standardize(x_ref[...].reshape(s * r, d), gain_ref[...].reshape(1, d))


def project(rows, w_ref):
    return jnp.dot(rows, w_ref[...], preferred_element_type=jnp.float32).astype(jnp.bfloat16)


def lane_group(y, s, r, group):
    return jnp.concatenate(
        [y[i * r : (i + 1) * r, group * LANES : (group + 1) * LANES] for i in range(s)], axis=1
    )


def half_of(w_ref, side):
    half = w_ref.shape[1] // CORES
    return w_ref.at[:, pl.ds(pl.multiple_of(side * half, half), half)]


def write_keys(rows, w_ref, s, k_scr):
    k = project(rows, w_ref)
    for g in range(k_scr.shape[0]):
        k_scr[g] = lane_group(k, s, k_scr.shape[1], g)


def write_queries(rows, w_ref, s, hsize, q_ref):
    q = project(rows, w_ref)
    pack = LANES // hsize
    r = q_ref.shape[1] // pack
    lane = lax.broadcasted_iota(jnp.int32, (r, s * LANES), 1) % LANES // hsize
    for g in range(q_ref.shape[0]):
        both = lane_group(q, s, r, g)
        for h in range(pack):
            q_ref[g, h * r : (h + 1) * r] = jnp.where(lane == h, both, jnp.zeros_like(both))


def write_scores(q_ref, k_ref, out_ref):
    blocks, heads, share, cols = out_ref.shape
    pack = heads // q_ref.shape[0]
    r = blocks * share
    for t in range(q_ref.shape[0]):
        part = lax.dot_general(
            q_ref[t], k_ref[t], (((1,), (1,)), ((), ())), preferred_element_type=jnp.float32
        )
        for h in range(pack):
            out_ref[:, t * pack + h] = part[h * r : (h + 1) * r].reshape(blocks, share, cols)


def load(pairs, sems):
    copies = [pltpu.make_async_copy(a, b, sems.at[i]) for i, (a, b) in enumerate(pairs)]
    for copy in copies:
        copy.start()
    return copies


def own_send_kernel(
    x_hbm, gain_hbm, wk_hbm, wq_hbm,
    rows_ref, q_ref, send_ref,
    x_ref, gain_ref, wk_ref, wq_ref, k_scr, sems,
):
    side = 1 - spot(1)[0]
    copies = load(
        (
            (x_hbm, x_ref),
            (gain_hbm, gain_ref),
            (half_of(wk_hbm, side), wk_ref),
            (half_of(wq_hbm, side), wq_ref),
        ),
        sems,
    )
    s, _, d = x_ref.shape
    copies[0].wait()
    copies[1].wait()
    rows_ref[...] = rows_of(x_ref, gain_ref)
    copies[2].wait()
    write_keys(rows_ref[...], wk_ref, s, k_scr)
    copies[3].wait()
    write_queries(rows_ref[...], wq_ref, s, d // HEADS, q_ref)
    write_scores(q_ref, k_scr, send_ref)


def own_keep_kernel(
    rows_ref, wk_hbm, wq_hbm, after_ref, q_ref, keep_ref, wk_ref, wq_ref, k_scr, sems
):
    side = spot(1)[0]
    copies = load(((half_of(wk_hbm, side), wk_ref), (half_of(wq_hbm, side), wq_ref)), sems)
    d = rows_ref.shape[1]
    s = rows_ref.shape[0] // k_scr.shape[1]
    copies[0].wait()
    write_keys(rows_ref[...], wk_ref, s, k_scr)
    copies[1].wait()
    write_queries(rows_ref[...], wq_ref, s, d // HEADS, q_ref)
    write_scores(q_ref, k_scr, keep_ref)


def send_kernel(x_ref, gain_ref, wk_ref, q_ref, after_ref, rows_ref, send_ref, k_scr):
    rows_ref[...] = rows_of(x_ref, gain_ref)
    write_keys(rows_ref[...], half_of(wk_ref, 1 - spot(1)[0]), x_ref.shape[0], k_scr)
    write_scores(q_ref, k_scr, send_ref)


def keep_kernel(rows_ref, wk_ref, q_ref, after_ref, keep_ref, k_scr):
    s = rows_ref.shape[0] // k_scr.shape[1]
    write_keys(rows_ref[...], half_of(wk_ref, spot(1)[0]), s, k_scr)
    write_scores(q_ref, k_scr, keep_ref)


def value_kernel(rows_ref, wv_hbm, after_ref, v_ref, wv_ref, sems):
    groups, r, width = v_ref.shape
    for copy in load(((wv_hbm, wv_ref),), sems):
        copy.wait()
    v = project(rows_ref[...], wv_ref)
    for g in range(groups):
        v_ref[g] = lane_group(v, width // LANES, r, g)


def steps(inner):
    return sorted(range(inner), key=lambda k: (k > 0, -k.bit_count(), k))


def merge_kernel(keep_ref, got_ref, *refs):
    inner = keep_ref.shape[0]
    outs = refs[-inner:]
    _, chip = spot(inner)
    for k, out_ref in zip(steps(inner), outs):
        b = chip ^ k
        out_ref[...] = keep_ref[b] + got_ref[b]


def sum_kernel(n, *refs):
    total = refs[0][...]
    for part in refs[1:n]:
        total = total + part[...]
    refs[-1][...] = total


def own_softmax_kernel(scale, mine_ref, other_ref, after_ref, p_ref, top_ref, sum_ref):
    logits = (mine_ref[...] + other_ref[...]) * scale
    top = jnp.max(logits, axis=-1, keepdims=True)
    p = jnp.exp(logits - top)
    p_ref[...] = p.astype(p_ref.dtype)
    top_ref[...] = jnp.broadcast_to(top, top_ref.shape)
    sum_ref[...] = jnp.broadcast_to(jnp.sum(p, axis=-1, keepdims=True), sum_ref.shape)


def softmax_kernel(scale, n, *refs):
    mine, other, (own_top_ref, own_sum_ref, out_ref) = refs[:n], refs[n : 2 * n], refs[2 * n :]
    logits = jnp.concatenate([a[...] + b[...] for a, b in zip(mine, other)], axis=-1) * scale
    heads, share, cols = logits.shape
    own_top = own_top_ref[...][..., :1]
    top = jnp.maximum(own_top, jnp.max(logits, axis=-1, keepdims=True))
    p = jnp.exp(logits - top)
    factor = jnp.exp(own_top - top)
    total = own_sum_ref[...][..., :1] * factor + jnp.sum(p, axis=-1, keepdims=True)
    out_ref[:heads] = (p / total).astype(out_ref.dtype)
    factor = factor / total
    high = factor.astype(out_ref.dtype).astype(jnp.float32)
    low = factor - high
    lane = lax.broadcasted_iota(jnp.int32, (share, cols), 1)
    packed = jnp.zeros((share, cols), jnp.float32)
    for h in range(heads):
        packed = jnp.where(lane == h, high[h], packed)
        packed = jnp.where(lane == heads + h, low[h], packed)
    out_ref[heads] = packed.astype(out_ref.dtype)


def pack_kernel(n, *refs):
    for k in range(n):
        refs[-1][k] = refs[k][...]


def weighted(p_ref, v_refs, g, t, hsize):
    pieces, _, share, _ = p_ref.shape
    pack = LANES // hsize
    r = pieces * share
    p = jnp.concatenate(
        [p_ref[:, t * pack + h].reshape(r, p_ref.shape[-1]) for h in range(pack)], axis=0
    )
    v = jnp.concatenate([v_ref[g] for v_ref in v_refs], axis=0)
    both = jnp.dot(p, v, preferred_element_type=jnp.float32)
    return pick([both[h * r : (h + 1) * r] for h in range(pack)], both.shape[1], hsize)


def pick(per_head, width, hsize):
    r = per_head[0].shape[0]
    lane = lax.broadcasted_iota(jnp.int32, (r, width), 1) % LANES // hsize
    got = jnp.broadcast_to(per_head[0], (r, width))
    for h in range(1, len(per_head)):
        got = jnp.where(lane == h, per_head[h], got)
    return got


def own_attend_kernel(hsize, mine_ref, got_ref, v_ref, out_ref):
    core = spot(mine_ref.shape[0])[0]
    per_core = v_ref.shape[0] // CORES
    for p_ref, side in ((mine_ref, core), (got_ref, 1 - core)):
        for t in range(per_core):
            g = side * per_core + t
            out_ref[g] = weighted(p_ref, (v_ref,), g, t, hsize)


def attended(p_ref, v_refs, own_ref, side, hsize):
    pieces, heads, share, _ = p_ref.shape
    heads -= 1
    pack = LANES // hsize
    per_core = heads // pack
    width = own_ref.shape[-1]
    groups = []
    for t in range(per_core):
        g = side * per_core + t
        factors = []
        for h in range(t * pack, (t + 1) * pack):
            packed = p_ref[:, heads].reshape(pieces * share, -1).astype(jnp.float32)
            factors.append(packed[:, h : h + 1] + packed[:, heads + h : heads + h + 1])
        own = own_ref[g] * pick(factors, width, hsize)
        groups.append((own + weighted(p_ref, v_refs, g, t, hsize)).astype(jnp.bfloat16))
    return jnp.concatenate(
        [
            jnp.concatenate([g[:, i : i + LANES] for g in groups], axis=1)
            for i in range(0, width, LANES)
        ],
        axis=0,
    )


def half_rows(w_ref, side):
    half = w_ref.shape[0] // CORES
    return w_ref[pl.ds(pl.multiple_of(side * half, half), half)]


def half_mix_kernel(hsize, n, p_ref, *refs):
    v_refs, (own_ref, wf_ref, out_ref) = refs[:n], refs[n:]
    side = spot(p_ref.shape[0])[0]
    rows = attended(p_ref, v_refs, own_ref, side, hsize)
    out_ref[...] = jnp.dot(rows, half_rows(wf_ref, side), preferred_element_type=jnp.float32)


def mix_kernel(hsize, n, p_ref, *refs):
    v_refs, (own_ref, half_ref, wf_ref, out_hbm, out_ref, sems) = refs[:n], refs[n:]
    pieces = p_ref.shape[0]
    s, r, _ = out_ref.shape
    share = r // pieces
    core, chip = spot(pieces)
    rows = attended(p_ref, v_refs, own_ref, 1 - core, hsize)
    w = half_rows(wf_ref, 1 - core)
    copies = []
    for i in range(s):
        part = slice(i * r, (i + 1) * r)
        mixed = half_ref[part] + jnp.dot(rows[part], w, preferred_element_type=jnp.float32)
        mixed = mixed.astype(out_ref.dtype)
        for n, k in enumerate(steps(pieces)):
            start = pl.multiple_of((chip ^ k) * share, share)
            out_ref[i, pl.ds(start, share)] = mixed[n * share : (n + 1) * share]
        copies.append(pltpu.make_async_copy(out_ref.at[i], out_hbm.at[i], sems.at[i]))
        copies[-1].start()
    for copy in copies:
        copy.wait()


def call(kernel, out_shape, args, order=(), hbm=(), scratch=(), flops=0, out_space=VMEM):
    ins = (*args, *(pltpu.with_memory_space_constraint(a, pltpu.HBM) for a in hbm), *order)
    specs = [VMEM] * len(args) + [HBM] * len(hbm) + [ANY] * len(order)
    moved = sum(a.size * a.dtype.itemsize for a in args)
    return pl.pallas_call(
        kernel,
        out_shape=out_shape,
        in_specs=specs,
        out_specs=jax.tree.map(lambda _: out_space, out_shape),
        scratch_shapes=list(scratch),
        compiler_params=PARAMS,
        cost_estimate=pl.CostEstimate(flops=flops, bytes_accessed=moved, transcendentals=0),
    )(*ins)


def body(n_seq, n_res, x, gain, wq, wk, wv, wf):
    s, r, d = x.shape
    groups = d // LANES
    hsize = d // HEADS
    pack = LANES // hsize
    heads = HEADS // CORES
    blocks = n_seq // CORES
    inner = blocks // 2
    share = r // inner
    cols = r * n_res
    f32, bf16 = jnp.float32, jnp.bfloat16
    shape = jax.ShapeDtypeStruct

    part = shape((inner, heads, share, r), f32)
    piece = shape((heads, share, r), f32)
    normed = shape((s * r, d), bf16)
    grouped = shape((groups, r, s * LANES), bf16)
    queries = shape((groups // CORES, pack * r, s * LANES), bf16)
    keys = pltpu.VMEM((groups // CORES, r, s * LANES), bf16)
    half = pltpu.VMEM((d, d // CORES), bf16)
    dots = 2 * s * r * d

    def hop(y, k):
        return lax.ppermute(y, "seq", [(i, i ^ k) for i in range(n_seq)])

    def values_of(rows, order):
        return call(
            value_kernel,
            grouped,
            (rows,),
            hbm=(wv,),
            order=order,
            scratch=[pltpu.VMEM(wv.shape, bf16), pltpu.SemaphoreType.DMA((1,))],
            flops=dots * d,
        )

    def split(keep, got, order=()):
        return call(merge_kernel, (piece,) * inner, (keep, got), order=order)

    def reduce(own, *sent, order=()):
        parts = [hop(y, CORES * k) for k, y in zip(steps(inner)[1:], sent)]
        total = call(functools.partial(sum_kernel, inner), piece, (own, *parts), order=order)
        return total, hop(total, CORES * inner)

    others = [
        lax.ppermute(x, "res", [(i, (i + k) % n_res) for i in range(n_res)])
        for k in range(1, n_res)
    ]
    rows, q_send, send = call(
        own_send_kernel,
        (normed, queries, part),
        (),
        hbm=(x, gain, wk, wq),
        scratch=[
            pltpu.VMEM(x.shape, bf16),
            pltpu.VMEM(gain.shape, f32),
            half,
            half,
            keys,
            pltpu.SemaphoreType.DMA((4,)),
        ],
        flops=dots * (d + r // 2),
    )
    got = hop(send, 1)
    q_keep, keep = call(
        own_keep_kernel,
        (queries, part),
        (rows,),
        hbm=(wk, wq),
        order=(send,),
        scratch=[half, half, keys, pltpu.SemaphoreType.DMA((2,))],
        flops=dots * (d + r // 2),
    )
    pieces = split(keep, got)
    values = [values_of(rows, pieces[:1])]
    reduced = [reduce(*pieces, order=values)]
    for other in others:
        rows, send = call(
            send_kernel,
            (normed, part),
            (other, gain, wk, q_send),
            order=(reduced[0][0],),
            scratch=[keys],
            flops=dots * (d // 2 + r // 2),
        )
        got = hop(send, 1)
        keep = call(
            keep_kernel,
            part,
            (rows, wk, q_keep),
            order=(send,),
            scratch=[keys],
            flops=dots * (d // 2 + r // 2),
        )
        pieces = split(keep, got)
        values.append(values_of(rows, pieces[:1]))
        reduced.append(reduce(*pieces, order=values[-1:]))
    scale = float(hsize * s * n_seq) ** -0.5

    def gather(y, order=()):
        mine = [y] + [hop(y, CORES * k) for k in steps(inner)[1:]]
        mine = call(
            functools.partial(pack_kernel, inner), shape((inner, *y.shape), bf16), mine, order=order
        )
        return mine, hop(mine, 1)

    own_probs, own_top, own_sum = call(
        functools.partial(own_softmax_kernel, scale),
        (shape(piece.shape, bf16), piece, piece),
        reduced[0],
        order=(reduced[-1][0],),
    )
    probs = call(
        functools.partial(softmax_kernel, scale, n_res - 1),
        shape((heads + 1, share, cols - r), bf16),
        (*(a for a, _ in reduced[1:]), *(b for _, b in reduced[1:]), own_top, own_sum),
    )
    own_mine, own_got = gather(own_probs, order=(probs,))
    own_part = call(
        functools.partial(own_attend_kernel, hsize),
        shape(grouped.shape, f32),
        (own_mine, own_got, values[0]),
        flops=dots * r,
    )
    mine, got = gather(probs, order=(own_part,))
    half_mix = call(
        functools.partial(half_mix_kernel, hsize, n_res - 1),
        shape((s * r, d), f32),
        (mine, *values[1:], own_part, wf),
        flops=dots * (d + cols) // 2,
    )
    return call(
        functools.partial(mix_kernel, hsize, n_res - 1),
        shape((s, r, d), bf16),
        (got, *values[1:], own_part, half_mix, wf),
        scratch=[pltpu.VMEM(x.shape, bf16), pltpu.SemaphoreType.DMA((s,))],
        flops=dots * (d + cols) // 2,
        out_space=HBM,
    )


def solution(mesh):
    n_seq, n_res = mesh.shape["seq"], mesh.shape["res"]

    def program(*args):
        return body(n_seq, n_res, *args)

    placed = (P("seq", "res", None), P(), P(), P(), P(), P())
    return jax.shard_map(
        program, mesh=mesh, in_specs=placed, out_specs=P("seq", "res", None), check_vma=False
    )
```

time: 135 us -> 49.2 us (0.36)
  waiting for transfers between devices: 79.9 us -> 12.6 us
  starting transfers between devices: 0.09 us -> 22 us
  blocking collectives: 21.5 us -> 0 us
  Pallas kernels: 0 us -> 14.2 us
  between operations: 13.2 us -> 0.18 us
  matrix products: 8.81 us -> 0 us
  local copies, waits for them, and re-layouts: 6.86 us -> 0.01 us
  other arithmetic: 4.05 us -> 0 us
    reduce_scatter x1 -> x0, waiting for transfers between devices: 57.4 us -> none  [body(): share = lax.psum_scatter(logits, 'seq', scatter_dimension=1, tiled=True)]
    all_gather x2 -> x0, waiting for transfers between devices: 22.5 us -> none  [the longest x1 21.8 us: body(): lax.all_gather(key_local, 'res', axis=1, tiled=True)]
    ppermute x0 -> x19, starting transfers between devices: none -> 22 us  [the longest x18 19 us: hop(): return lax.ppermute(y, 'seq', [(i, i ^ k) for i in range(n_seq)])]
    all_gather x1 -> x0, blocking collectives: 21.5 us -> none  [body(): probs = lax.all_gather(share_probs, 'seq', axis=1, tiled=True)]
    pallas_call x0 -> x17, Pallas kernels: none -> 14.2 us  [call(): pl.pallas_call(kernel, out_shape=out_shape, in_specs=specs, out_specs=jax...]
    ppermute x0 -> x19, waiting for transfers between devices: none -> 12.6 us  [the longest x18 12.6 us: hop(): return lax.ppermute(y, 'seq', [(i, i ^ k) for i in range(n_seq)])]
    dot_general x6 -> x0, matrix products: 8.81 us -> none  [the longest x1 2.9 us: body(): jnp.einsum('sihe,sjhe->hij', query, keys, preferred_element_type=jnp.floa...]
    reshape x3 -> x0, local copies, waits for them, and re-layouts: 4.04 us -> none  [the longest x1 1.93 us: body(): query = query.reshape(row_portion, column_portion, heads, hsize)]
  transfers between devices with their start and end apart: 3 -> 19, of which waited for: 3 -> 11; matrix products, arithmetic and copies ran while one was open for 5% -> 0% of each run, Pallas kernels for 0% -> 24%
where the time goes in v2:
time: 49.2 us; the launch traced here: 49 us
  starting transfers between devices  22 us (45%)
  Pallas kernels  14.2 us (29%)
  waiting for transfers between devices  12.6 us (26%)
    ppermute x18, starting transfers between devices, hop(): return lax.ppermute(y, 'seq', [(i, i ^ k) for i in range(n_seq)])  19 us
    pallas_call x17, Pallas kernels, call(): pl.pallas_call(kernel, out_shape=out_shape, in_specs=specs, out_specs=jax...  14.2 us
    ppermute x18, waiting for transfers between devices, hop(): return lax.ppermute(y, 'seq', [(i, i ^ k) for i in range(n_seq)])  12.6 us
    ppermute x1, starting transfers between devices, body(): lax.ppermute(x, 'res', [(i, (i + k) % n_res) for i in range(n_res)])  3 us
  transfers between devices with their start and end apart: 19, of which 11 were waited for; matrix products, arithmetic and copies ran while one was open for 0% of the time, Pallas kernels for 24%

profile of v2, /device:TPU:0, one launch (start us, length us, event | category | flops | bytes accessed | tf_op | source)
XLA Modules:
  0.0 49.0 jit_solution(7120221204318218572)
XLA Ops:
  0.0 3.0 %collective-permute-start = (bf16[3,128,768]{2,1,0:T(8,128)(2,1)}, bf16[3,128,768]{2,1,0:T(8,128)(2,1)S(1)}, u32[]{:S(2)}, u32[]{:S(2)}) collective-permute-start(bf16[3,128,768]{2,1,0:T(8,128)(2,1)} %x_hbm.1), channel_id=1, source_target_pairs={{0,1},{1,0},{2,3},{3,2},{4,5},{5,4},{6,7},{7,6},{8,9},{9,8},{10,11... | collective-permute-start | bytes 1769480 | tf_op jit(solution)/shard_map/ppermute | solution.py:353
  3.0 2.7 %shard_map.64 = (bf16[384,768]{1,0:T(8,128)(2,1)S(1)}, bf16[3,256,384]{2,1,0:T(8,128)(2,1)S(1)}, f32[4,6,32,128]{3,2,1,0:T(8,128)S(1)}) custom-call(bf16[3,128,768]{2,1,0:T(8,128)(2,1)} %x_hbm.1, f32[768]{0:T(1024)} %gain_ref.1, bf16[768,768]{1,0:T(8,128)(2,1)} %wk_ref.3, bf16[768,768]{1,0:T(8,128)(2,1)} %wq_hbm.3), custom_call_target="tpu_custom_call" | custom-call | flops 490733568 | tf_op jit(solution)/shard_map/pallas_call | solution.py:297
  5.8 2.3 %shard_map.65 = (bf16[3,256,384]{2,1,0:T(8,128)(2,1)S(1)}, f32[4,6,32,128]{3,2,1,0:T(8,128)S(1)}) custom-call(bf16[384,768]{1,0:T(8,128)(2,1)S(1)} %get-tuple-element.24.rows_ref, bf16[768,768]{1,0:T(8,128)(2,1)} %wk_ref.3, bf16[768,768]{1,0:T(8,128)(2,1)} %wq_hbm.3, f32[4,6,32,128]{3,2,1,0:T(8,128)S(1)} %get-tuple-element.25.after_ref), custom_call_target="tpu_custom_call" | custom-call | flops 490733568 | bytes 589824 | tf_op jit(solution)/shard_map/pallas_call | solution.py:297
  8.2 2.6 %collective-permute-start.2 = (f32[6,32,128]{2,1,0:T(8,128)S(1)}, f32[6,32,128]{2,1,0:T(8,128)S(1)}, u32[]{:S(2)}, u32[]{:S(2)}) collective-permute-start(f32[6,32,128]{2,1,0:T(8,128)S(1)} %get-tuple-element.28), channel_id=1, source_target_pairs={{0,12},{2,14},{4,8},{6,10},{8,4},{10,6},{12,0},{14,2},{16,28},{18,... | collective-permute-start | bytes 294920 | tf_op jit(solution)/shard_map/ppermute | solution.py:331
  11.8 2.0 %shard_map.67.refs_4_.v_ref = bf16[6,128,384]{2,1,0:T(8,128)(2,1)S(1)} custom-call(bf16[384,768]{1,0:T(8,128)(2,1)S(1)} %get-tuple-element.24.rows_ref, bf16[768,768]{1,0:T(8,128)(2,1)} %wv_hbm.3, f32[6,32,128]{2,1,0:T(8,128)S(1)} %get-tuple-element.27.after_ref.refs_0_), custom_call_target="tpu_custom_call" | custom-call | flops 452984832 | bytes 589824 | tf_op jit(solution)/shard_map/pallas_call | solution.py:297
  14.4 2.0 %collective-permute-done.3.refs_2_ = f32[6,32,128]{2,1,0:T(8,128)S(1)} collective-permute-done((f32[6,32,128]{2,1,0:T(8,128)S(1)}, f32[6,32,128]{2,1,0:T(8,128)S(1)}, u32[]{:S(2)}, u32[]{:S(2)}) %collective-permute-start.3) | collective-permute-done | bytes 98336 | tf_op jit(solution)/shard_map/ppermute | solution.py:331
  16.5 1.0 %shard_map.69 = (bf16[384,768]{1,0:T(8,128)(2,1)S(1)}, f32[4,6,32,128]{3,2,1,0:T(8,128)S(1)}) custom-call(bf16[3,128,768]{2,1,0:T(8,128)(2,1)S(1)} %collective-permute-done.x_ref, f32[768]{0:T(1024)S(1)} %copy-done.2, bf16[768,768]{1,0:T(8,128)(2,1)S(1)} %copy-done, bf16[3,256,384]{2,1,0:T(8,128)(2,1)S(1)} %get-tuple-element.23.q_ref, ...), custom_call_target="tpu_custom_call" | custom-call | flops 264241152 | bytes 2362368 | tf_op jit(solution)/shard_map/pallas_call | solution.py:297
  17.7 0.8 %shard_map.70.keep_ref = f32[4,6,32,128]{3,2,1,0:T(8,128)S(1)} custom-call(bf16[384,768]{1,0:T(8,128)(2,1)S(1)} %get-tuple-element.31.rows_ref, bf16[768,768]{1,0:T(8,128)(2,1)S(1)} %copy-done, bf16[3,256,384]{2,1,0:T(8,128)(2,1)S(1)} %get-tuple-element.32.q_ref, f32[4,6,32,128]{3,2,1,0:T(8,128)S(1)} %get-tuple-element.33.after_ref), custom_call_target="tpu_custom_call" | custom-call | flops 264241152 | bytes 2359296 | tf_op jit(solution)/shard_map/pallas_call | solution.py:297
  18.4 0.9 %collective-permute-done.5.got_ref = f32[4,6,32,128]{3,2,1,0:T(8,128)S(1)} collective-permute-done((f32[4,6,32,128]{3,2,1,0:T(8,128)S(1)}, f32[4,6,32,128]{3,2,1,0:T(8,128)S(1)}, u32[]{:S(2)}, u32[]{:S(2)}) %collective-permute-start.5) | collective-permute-done | bytes 393248 | tf_op jit(solution)/shard_map/ppermute | solution.py:331
  19.4 2.8 %collective-permute-start.6 = (f32[6,32,128]{2,1,0:T(8,128)S(1)}, f32[6,32,128]{2,1,0:T(8,128)S(1)}, u32[]{:S(2)}, u32[]{:S(2)}) collective-permute-start(f32[6,32,128]{2,1,0:T(8,128)S(1)} %get-tuple-element.35), channel_id=1, source_target_pairs={{0,12},{2,14},{4,8},{6,10},{8,4},{10,6},{12,0},{14,2},{16,28},{18,... | collective-permute-start | bytes 294920 | tf_op jit(solution)/shard_map/ppermute | solution.py:331
  23.0 2.8 %collective-permute-start.10 = (f32[6,32,128]{2,1,0:T(8,128)S(1)}, f32[6,32,128]{2,1,0:T(8,128)S(1)}, u32[]{:S(2)}, u32[]{:S(2)}) collective-permute-start(f32[6,32,128]{2,1,0:T(8,128)S(1)} %shard_map.68.after_ref.mine_ref), channel_id=1, source_target_pairs={{0,16},{2,18},{4,20},{6,22},{8,24},{10,26},{12,28},{14,30},{16,0},... | collective-permute-start | bytes 294920 | tf_op jit(solution)/shard_map/ppermute | solution.py:331
  25.8 1.9 %shard_map.72.refs_4_.refs_0_ = bf16[6,128,384]{2,1,0:T(8,128)(2,1)S(1)} custom-call(bf16[384,768]{1,0:T(8,128)(2,1)S(1)} %get-tuple-element.31.rows_ref, bf16[768,768]{1,0:T(8,128)(2,1)} %wv_hbm.3, f32[6,32,128]{2,1,0:T(8,128)S(1)} %get-tuple-element.34.after_ref.refs_0_), custom_call_target="tpu_custom_call" | custom-call | flops 452984832 | bytes 589824 | tf_op jit(solution)/shard_map/pallas_call | solution.py:297
  27.7 1.9 %collective-permute-done.8.refs_3_ = f32[6,32,128]{2,1,0:T(8,128)S(1)} collective-permute-done((f32[6,32,128]{2,1,0:T(8,128)S(1)}, f32[6,32,128]{2,1,0:T(8,128)S(1)}, u32[]{:S(2)}, u32[]{:S(2)}) %collective-permute-start.8) | collective-permute-done | bytes 98336 | tf_op jit(solution)/shard_map/ppermute | solution.py:331
  29.7 1.4 %collective-permute-start.9 = (f32[6,32,128]{2,1,0:T(8,128)S(1)}, f32[6,32,128]{2,1,0:T(8,128)S(1)}, u32[]{:S(2)}, u32[]{:S(2)}) collective-permute-start(f32[6,32,128]{2,1,0:T(8,128)S(1)} %shard_map.73.after_ref.refs_0_), channel_id=1, source_target_pairs={{0,16},{2,18},{4,20},{6,22},{8,24},{10,26},{12,28},{14,30},{16,0},... | collective-permute-start | bytes 294920 | tf_op jit(solution)/shard_map/ppermute | solution.py:331
  31.3 2.3 %collective-permute-start.16 = (bf16[6,32,128]{2,1,0:T(8,128)(2,1)S(1)}, bf16[6,32,128]{2,1,0:T(8,128)(2,1)S(1)}, u32[]{:S(2)}, u32[]{:S(2)}) collective-permute-start(bf16[6,32,128]{2,1,0:T(8,128)(2,1)S(1)} %get-tuple-element.40.refs_0_), channel_id=1, source_target_pairs={{0,8},{2,10},{4,12},{6,14},{8,0},{10,2},{12,4},{14,6},{16,24},{18,... | collective-permute-start | bytes 147464 | tf_op jit(solution)/shard_map/ppermute | solution.py:331
  33.6 1.5 %collective-permute-start.14 = (bf16[6,32,128]{2,1,0:T(8,128)(2,1)S(1)}, bf16[6,32,128]{2,1,0:T(8,128)(2,1)S(1)}, u32[]{:S(2)}, u32[]{:S(2)}) collective-permute-start(bf16[6,32,128]{2,1,0:T(8,128)(2,1)S(1)} %get-tuple-element.40.refs_0_), channel_id=1, source_target_pairs={{0,12},{2,14},{4,8},{6,10},{8,4},{10,6},{12,0},{14,2},{16,28},{18,... | collective-permute-start | bytes 147464 | tf_op jit(solution)/shard_map/ppermute | solution.py:331
  35.1 1.9 %collective-permute-done.9.refs_1_ = f32[6,32,128]{2,1,0:T(8,128)S(1)} collective-permute-done((f32[6,32,128]{2,1,0:T(8,128)S(1)}, f32[6,32,128]{2,1,0:T(8,128)S(1)}, u32[]{:S(2)}, u32[]{:S(2)}) %collective-permute-start.9) | collective-permute-done | bytes 98336 | tf_op jit(solution)/shard_map/ppermute | solution.py:331
  37.8 0.8 %collective-permute-done.14.refs_1_ = bf16[6,32,128]{2,1,0:T(8,128)(2,1)S(1)} collective-permute-done((bf16[6,32,128]{2,1,0:T(8,128)(2,1)S(1)}, bf16[6,32,128]{2,1,0:T(8,128)(2,1)S(1)}, u32[]{:S(2)}, u32[]{:S(2)}) %collective-permute-start.14) | collective-permute-done | bytes 49184 | tf_op jit(solution)/shard_map/ppermute | solution.py:331
  38.7 1.0 %collective-permute-start.13 = (bf16[7,32,128]{2,1,0:T(8,128)(2,1)S(1)}, bf16[7,32,128]{2,1,0:T(8,128)(2,1)S(1)}, u32[]{:S(2)}, u32[]{:S(2)}) collective-permute-start(bf16[7,32,128]{2,1,0:T(8,128)(2,1)S(1)} %shard_map.75.refs_4_.refs_0_), channel_id=1, source_target_pairs={{0,8},{2,10},{4,12},{6,14},{8,0},{10,2},{12,4},{14,6},{16,24},{18,... | collective-permute-start | bytes 172040 | tf_op jit(solution)/shard_map/ppermute | solution.py:331
  39.7 1.1 %collective-permute-start.12 = (bf16[7,32,128]{2,1,0:T(8,128)(2,1)S(1)}, bf16[7,32,128]{2,1,0:T(8,128)(2,1)S(1)}, u32[]{:S(2)}, u32[]{:S(2)}) collective-permute-start(bf16[7,32,128]{2,1,0:T(8,128)(2,1)S(1)} %shard_map.75.refs_4_.refs_0_), channel_id=1, source_target_pairs={{0,4},{2,6},{4,0},{6,2},{8,12},{10,14},{12,8},{14,10},{16,20},{18,... | collective-permute-start | bytes 172040 | tf_op jit(solution)/shard_map/ppermute | solution.py:331
  40.8 1.4 %collective-permute-start.11 = (bf16[7,32,128]{2,1,0:T(8,128)(2,1)S(1)}, bf16[7,32,128]{2,1,0:T(8,128)(2,1)S(1)}, u32[]{:S(2)}, u32[]{:S(2)}) collective-permute-start(bf16[7,32,128]{2,1,0:T(8,128)(2,1)S(1)} %shard_map.75.refs_4_.refs_0_), channel_id=1, source_target_pairs={{0,12},{2,14},{4,8},{6,10},{8,4},{10,6},{12,0},{14,2},{16,28},{18,... | collective-permute-start | bytes 172040 | tf_op jit(solution)/shard_map/ppermute | solution.py:331
  43.0 0.9 %collective-permute-done.12.refs_2_ = bf16[7,32,128]{2,1,0:T(8,128)(2,1)S(1)} collective-permute-done((bf16[7,32,128]{2,1,0:T(8,128)(2,1)S(1)}, bf16[7,32,128]{2,1,0:T(8,128)(2,1)S(1)}, u32[]{:S(2)}, u32[]{:S(2)}) %collective-permute-start.12) | collective-permute-done | bytes 57376 | tf_op jit(solution)/shard_map/ppermute | solution.py:331
  43.9 2.0 %collective-permute-done.11.refs_1_ = bf16[7,32,128]{2,1,0:T(8,128)(2,1)S(1)} collective-permute-done((bf16[7,32,128]{2,1,0:T(8,128)(2,1)S(1)}, bf16[7,32,128]{2,1,0:T(8,128)(2,1)S(1)}, u32[]{:S(2)}, u32[]{:S(2)}) %collective-permute-start.11) | collective-permute-done | bytes 57376 | tf_op jit(solution)/shard_map/ppermute | solution.py:331
  47.5 1.5 %shard_map.80 = bf16[3,128,768]{2,1,0:T(8,128)(2,1)} custom-call(bf16[4,7,32,128]{3,2,1,0:T(8,128)(2,1)S(1)} %collective-permute-done.18.p_ref, bf16[6,128,384]{2,1,0:T(8,128)(2,1)S(1)} %shard_map.72.refs_4_.refs_0_, f32[6,128,384]{2,1,0:T(8,128)S(1)} %shard_map.77.refs_4_.refs_1_, f32[384,768]{1,0:T(8,128)S(1)} %shard_map.79.refs_2_, ...), custom_call_target="tpu_custom_call" | custom-call | flops 301989888 | bytes 4358144 | tf_op jit(solution)/shard_map/pallas_call | solution.py:297
  (37 shorter events, 6.1 us)
Async XLA Ops:
  0.0 16.5 %collective-permute-start = (bf16[3,128,768]{2,1,0:T(8,128)(2,1)}, bf16[3,128,768]{2,1,0:T(8,128)(2,1)S(1)}, u32[]{:S(2)}, u32[]{:S(2)}) collective-permute-start(bf16[3,128,768]{2,1,0:T(8,128)(2,1)} %x_hbm.1), channel_id=1, source_target_pairs={{0,1},{1,0},{2,3},{3,2},{4,5},{5,4},{6,7},{7,6},{8,9},{9,8},{10,11... | collective-permute-start | bytes 1769480 | tf_op jit(solution)/shard_map/ppermute | solution.py:353
  5.7 2.4 %collective-permute-start.1 = (f32[4,6,32,128]{3,2,1,0:T(8,128)S(1)}, f32[4,6,32,128]{3,2,1,0:T(8,128)S(1)}, u32[]{:S(2)}, u32[]{:S(2)}) collective-permute-start(f32[4,6,32,128]{3,2,1,0:T(8,128)S(1)} %get-tuple-element.25.after_ref), channel_id=1, source_target_pairs={{0,2},{2,0},{4,6},{6,4},{8,10},{10,8},{12,14},{14,12},{16,18},{18,... | collective-permute-start | bytes 1179656 | tf_op jit(solution)/shard_map/ppermute | solution.py:331
  8.2 6.2 %collective-permute-start.2 = (f32[6,32,128]{2,1,0:T(8,128)S(1)}, f32[6,32,128]{2,1,0:T(8,128)S(1)}, u32[]{:S(2)}, u32[]{:S(2)}) collective-permute-start(f32[6,32,128]{2,1,0:T(8,128)S(1)} %get-tuple-element.28), channel_id=1, source_target_pairs={{0,12},{2,14},{4,8},{6,10},{8,4},{10,6},{12,0},{14,2},{16,28},{18,... | collective-permute-start | bytes 294920 | tf_op jit(solution)/shard_map/ppermute | solution.py:331
  10.8 5.7 %collective-permute-start.3 = (f32[6,32,128]{2,1,0:T(8,128)S(1)}, f32[6,32,128]{2,1,0:T(8,128)S(1)}, u32[]{:S(2)}, u32[]{:S(2)}) collective-permute-start(f32[6,32,128]{2,1,0:T(8,128)S(1)} %get-tuple-element.29), channel_id=1, source_target_pairs={{0,4},{2,6},{4,0},{6,2},{8,12},{10,14},{12,8},{14,10},{16,20},{18,... | collective-permute-start | bytes 294920 | tf_op jit(solution)/shard_map/ppermute | solution.py:331
  11.3 5.2 %collective-permute-start.4 = (f32[6,32,128]{2,1,0:T(8,128)S(1)}, f32[6,32,128]{2,1,0:T(8,128)S(1)}, u32[]{:S(2)}, u32[]{:S(2)}) collective-permute-start(f32[6,32,128]{2,1,0:T(8,128)S(1)} %get-tuple-element.30), channel_id=1, source_target_pairs={{0,8},{2,10},{4,12},{6,14},{8,0},{10,2},{12,4},{14,6},{16,24},{18,... | collective-permute-start | bytes 294920 | tf_op jit(solution)/shard_map/ppermute | solution.py:331
  11.7 4.8 %copy-start = (bf16[768,768]{1,0:T(8,128)(2,1)S(1)}, bf16[768,768]{1,0:T(8,128)(2,1)}, u32[]{:S(2)}) copy-start(bf16[768,768]{1,0:T(8,128)(2,1)} %wk_ref.3) | copy-start | bytes 3538948
  11.8 4.8 %copy-start.2 = (f32[768]{0:T(1024)S(1)}, f32[768]{0:T(1024)}, u32[]{:S(2)}) copy-start(f32[768]{0:T(1024)} %gain_ref.1) | copy-start | bytes 9220
  17.6 1.8 %collective-permute-start.5 = (f32[4,6,32,128]{3,2,1,0:T(8,128)S(1)}, f32[4,6,32,128]{3,2,1,0:T(8,128)S(1)}, u32[]{:S(2)}, u32[]{:S(2)}) collective-permute-start(f32[4,6,32,128]{3,2,1,0:T(8,128)S(1)} %get-tuple-element.33.after_ref), channel_id=1, source_target_pairs={{0,2},{2,0},{4,6},{6,4},{8,10},{10,8},{12,14},{14,12},{16,18},{18,... | collective-permute-start | bytes 1179656 | tf_op jit(solution)/shard_map/ppermute | solution.py:331
  19.4 8.3 %collective-permute-start.6 = (f32[6,32,128]{2,1,0:T(8,128)S(1)}, f32[6,32,128]{2,1,0:T(8,128)S(1)}, u32[]{:S(2)}, u32[]{:S(2)}) collective-permute-start(f32[6,32,128]{2,1,0:T(8,128)S(1)} %get-tuple-element.35), channel_id=1, source_target_pairs={{0,12},{2,14},{4,8},{6,10},{8,4},{10,6},{12,0},{14,2},{16,28},{18,... | collective-permute-start | bytes 294920 | tf_op jit(solution)/shard_map/ppermute | solution.py:331
  22.2 5.5 %collective-permute-start.7 = (f32[6,32,128]{2,1,0:T(8,128)S(1)}, f32[6,32,128]{2,1,0:T(8,128)S(1)}, u32[]{:S(2)}, u32[]{:S(2)}) collective-permute-start(f32[6,32,128]{2,1,0:T(8,128)S(1)} %get-tuple-element.36), channel_id=1, source_target_pairs={{0,4},{2,6},{4,0},{6,2},{8,12},{10,14},{12,8},{14,10},{16,20},{18,... | collective-permute-start | bytes 294920 | tf_op jit(solution)/shard_map/ppermute | solution.py:331
  22.7 6.9 %collective-permute-start.8 = (f32[6,32,128]{2,1,0:T(8,128)S(1)}, f32[6,32,128]{2,1,0:T(8,128)S(1)}, u32[]{:S(2)}, u32[]{:S(2)}) collective-permute-start(f32[6,32,128]{2,1,0:T(8,128)S(1)} %get-tuple-element.37), channel_id=1, source_target_pairs={{0,8},{2,10},{4,12},{6,14},{8,0},{10,2},{12,4},{14,6},{16,24},{18,... | collective-permute-start | bytes 294920 | tf_op jit(solution)/shard_map/ppermute | solution.py:331
  23.0 8.1 %collective-permute-start.10 = (f32[6,32,128]{2,1,0:T(8,128)S(1)}, f32[6,32,128]{2,1,0:T(8,128)S(1)}, u32[]{:S(2)}, u32[]{:S(2)}) collective-permute-start(f32[6,32,128]{2,1,0:T(8,128)S(1)} %shard_map.68.after_ref.mine_ref), channel_id=1, source_target_pairs={{0,16},{2,18},{4,20},{6,22},{8,24},{10,26},{12,28},{14,30},{16,0},... | collective-permute-start | bytes 294920 | tf_op jit(solution)/shard_map/ppermute | solution.py:331
  29.7 7.3 %collective-permute-start.9 = (f32[6,32,128]{2,1,0:T(8,128)S(1)}, f32[6,32,128]{2,1,0:T(8,128)S(1)}, u32[]{:S(2)}, u32[]{:S(2)}) collective-permute-start(f32[6,32,128]{2,1,0:T(8,128)S(1)} %shard_map.73.after_ref.refs_0_), channel_id=1, source_target_pairs={{0,16},{2,18},{4,20},{6,22},{8,24},{10,26},{12,28},{14,30},{16,0},... | collective-permute-start | bytes 294920 | tf_op jit(solution)/shard_map/ppermute | solution.py:331
  31.3 6.1 %collective-permute-start.16 = (bf16[6,32,128]{2,1,0:T(8,128)(2,1)S(1)}, bf16[6,32,128]{2,1,0:T(8,128)(2,1)S(1)}, u32[]{:S(2)}, u32[]{:S(2)}) collective-permute-start(bf16[6,32,128]{2,1,0:T(8,128)(2,1)S(1)} %get-tuple-element.40.refs_0_), channel_id=1, source_target_pairs={{0,8},{2,10},{4,12},{6,14},{8,0},{10,2},{12,4},{14,6},{16,24},{18,... | collective-permute-start | bytes 147464 | tf_op jit(solution)/shard_map/ppermute | solution.py:331
  33.6 4.2 %collective-permute-start.15 = (bf16[6,32,128]{2,1,0:T(8,128)(2,1)S(1)}, bf16[6,32,128]{2,1,0:T(8,128)(2,1)S(1)}, u32[]{:S(2)}, u32[]{:S(2)}) collective-permute-start(bf16[6,32,128]{2,1,0:T(8,128)(2,1)S(1)} %get-tuple-element.40.refs_0_), channel_id=1, source_target_pairs={{0,4},{2,6},{4,0},{6,2},{8,12},{10,14},{12,8},{14,10},{16,20},{18,... | collective-permute-start | bytes 147464 | tf_op jit(solution)/shard_map/ppermute | solution.py:331
  33.6 5.0 %collective-permute-start.14 = (bf16[6,32,128]{2,1,0:T(8,128)(2,1)S(1)}, bf16[6,32,128]{2,1,0:T(8,128)(2,1)S(1)}, u32[]{:S(2)}, u32[]{:S(2)}) collective-permute-start(bf16[6,32,128]{2,1,0:T(8,128)(2,1)S(1)} %get-tuple-element.40.refs_0_), channel_id=1, source_target_pairs={{0,12},{2,14},{4,8},{6,10},{8,4},{10,6},{12,0},{14,2},{16,28},{18,... | collective-permute-start | bytes 147464 | tf_op jit(solution)/shard_map/ppermute | solution.py:331
  38.6 3.6 %collective-permute-start.17 = (bf16[4,6,32,128]{3,2,1,0:T(8,128)(2,1)S(1)}, bf16[4,6,32,128]{3,2,1,0:T(8,128)(2,1)S(1)}, u32[]{:S(2)}, u32[]{:S(2)}) collective-permute-start(bf16[4,6,32,128]{3,2,1,0:T(8,128)(2,1)S(1)} %shard_map.76.mine_ref), channel_id=1, source_target_pairs={{0,2},{2,0},{4,6},{6,4},{8,10},{10,8},{12,14},{14,12},{16,18},{18,... | collective-permute-start | bytes 589832 | tf_op jit(solution)/shard_map/ppermute | solution.py:331
  38.7 4.3 %collective-permute-start.13 = (bf16[7,32,128]{2,1,0:T(8,128)(2,1)S(1)}, bf16[7,32,128]{2,1,0:T(8,128)(2,1)S(1)}, u32[]{:S(2)}, u32[]{:S(2)}) collective-permute-start(bf16[7,32,128]{2,1,0:T(8,128)(2,1)S(1)} %shard_map.75.refs_4_.refs_0_), channel_id=1, source_target_pairs={{0,8},{2,10},{4,12},{6,14},{8,0},{10,2},{12,4},{14,6},{16,24},{18,... | collective-permute-start | bytes 172040 | tf_op jit(solution)/shard_map/ppermute | solution.py:331
  39.7 4.2 %collective-permute-start.12 = (bf16[7,32,128]{2,1,0:T(8,128)(2,1)S(1)}, bf16[7,32,128]{2,1,0:T(8,128)(2,1)S(1)}, u32[]{:S(2)}, u32[]{:S(2)}) collective-permute-start(bf16[7,32,128]{2,1,0:T(8,128)(2,1)S(1)} %shard_map.75.refs_4_.refs_0_), channel_id=1, source_target_pairs={{0,4},{2,6},{4,0},{6,2},{8,12},{10,14},{12,8},{14,10},{16,20},{18,... | collective-permute-start | bytes 172040 | tf_op jit(solution)/shard_map/ppermute | solution.py:331
  40.8 5.1 %collective-permute-start.11 = (bf16[7,32,128]{2,1,0:T(8,128)(2,1)S(1)}, bf16[7,32,128]{2,1,0:T(8,128)(2,1)S(1)}, u32[]{:S(2)}, u32[]{:S(2)}) collective-permute-start(bf16[7,32,128]{2,1,0:T(8,128)(2,1)S(1)} %shard_map.75.refs_4_.refs_0_), channel_id=1, source_target_pairs={{0,12},{2,14},{4,8},{6,10},{8,4},{10,6},{12,0},{14,2},{16,28},{18,... | collective-permute-start | bytes 172040 | tf_op jit(solution)/shard_map/ppermute | solution.py:331
  42.7 3.3 %copy-start.1 = (bf16[768,768]{1,0:T(8,128)(2,1)S(1)}, bf16[768,768]{1,0:T(8,128)(2,1)}, u32[]{:S(2)}) copy-start(bf16[768,768]{1,0:T(8,128)(2,1)} %refs_3_.1) | copy-start | bytes 3538948
  45.9 1.6 %collective-permute-start.18 = (bf16[4,7,32,128]{3,2,1,0:T(8,128)(2,1)S(1)}, bf16[4,7,32,128]{3,2,1,0:T(8,128)(2,1)S(1)}, u32[]{:S(2)}, u32[]{:S(2)}) collective-permute-start(bf16[4,7,32,128]{3,2,1,0:T(8,128)(2,1)S(1)} %shard_map.78.p_ref), channel_id=1, source_target_pairs={{0,2},{2,0},{4,6},{6,4},{8,10},{10,8},{12,14},{14,12},{16,18},{18,... | collective-permute-start | bytes 688136 | tf_op jit(solution)/shard_map/ppermute | solution.py:331

commit v3 on v2

--- a/solution.py
+++ b/solution.py
@@ -10,6 +10,9 @@
 HEADS = 12
 LANES = 128
 CORES = 2
+
+UNIT = 0.5
+CODED = 80.0
 
 
 VMEM = pl.BlockSpec(memory_space=pltpu.VMEM)
@@ -138,37 +141,74 @@
     write_scores(q_ref, k_scr, keep_ref)
 
 
-def value_kernel(rows_ref, wv_hbm, after_ref, v_ref, wv_ref, sems):
+def write_values(rows, wv, v_ref):
     groups, r, width = v_ref.shape
-    for copy in load(((wv_hbm, wv_ref),), sems):
-        copy.wait()
-    v = project(rows_ref[...], wv_ref)
+    v = project(rows, wv)
     for g in range(groups):
         v_ref[g] = lane_group(v, width // LANES, r, g)
 
 
+def own_value_kernel(rows_ref, wv_hbm, wf_hbm, after_ref, v_ref, wv_ref, wf_ref, sems):
+    copies = load(((wv_hbm, wv_ref), (wf_hbm, wf_ref)), sems)
+    copies[0].wait()
+    write_values(rows_ref[...], wv_ref, v_ref)
+    copies[1].wait()
+
+
+def value_kernel(rows_ref, wv_ref, after_ref, v_ref):
+    write_values(rows_ref[...], wv_ref, v_ref)
+
+
+def encode(u):
+    near = jnp.exp(jnp.clip(u, -CODED, CODED))
+    far = jnp.where(u < 0, u, -1.0 / u)
+    return jnp.where(jnp.abs(u) < CODED, near, far).astype(jnp.bfloat16)
+
+
+def decode(y):
+    y = y.astype(jnp.float32)
+    near = jnp.log(jnp.abs(y))
+    far = jnp.where(y < -1.0, y, -1.0 / y)
+    return jnp.where(y > 0, near, far)
+
+
 def steps(inner):
     return sorted(range(inner), key=lambda k: (k > 0, -k.bit_count(), k))
 
 
-def merge_kernel(keep_ref, got_ref, *refs):
+def merge_kernel(factor, keep_ref, got_ref, *refs):
     inner = keep_ref.shape[0]
-    outs = refs[-inner:]
+    if refs[-1].shape == keep_ref.shape:
+        outs, top_out, top_ref = refs[:-1], refs[-1], None
+    else:
+        outs, top_out, top_ref = refs[1:], None, refs[0]
     _, chip = spot(inner)
     for k, out_ref in zip(steps(inner), outs):
         b = chip ^ k
-        out_ref[...] = keep_ref[b] + got_ref[b]
-
-
-def sum_kernel(n, *refs):
-    total = refs[0][...]
-    for part in refs[1:n]:
-        total = total + part[...]
-    refs[-1][...] = total
-
-
-def own_softmax_kernel(scale, mine_ref, other_ref, after_ref, p_ref, top_ref, sum_ref):
-    logits = (mine_ref[...] + other_ref[...]) * scale
+        u = (keep_ref[b] + got_ref[b]) * factor
+        if top_out is None:
+            top = top_ref[b]
+        else:
+            top = jnp.broadcast_to(jnp.max(u, axis=-1, keepdims=True), u.shape)
+            top_out[b] = top
+        u = u - top
+        out_ref[...] = encode(u) if k else u
+
+
+def sum_kernel(n, own_ref, *refs):
+    total = own_ref[...]
+    for part in refs[: n - 1]:
+        total = total + decode(part[...])
+    refs[-2][...] = total
+    refs[-1][...] = encode(total * 0.5)
+
+
+def logits_of(mine_ref, other_ref):
+    return (mine_ref[...] + 2.0 * decode(other_ref[...])) * UNIT
+
+
+def own_softmax_kernel(mine_ref, other_ref, after_ref, p_ref, top_ref, sum_ref):
+    logits = logits_of(mine_ref, other_ref)
     top = jnp.max(logits, axis=-1, keepdims=True)
     p = jnp.exp(logits - top)
     p_ref[...] = p.astype(p_ref.dtype)
@@ -176,9 +216,9 @@
     sum_ref[...] = jnp.broadcast_to(jnp.sum(p, axis=-1, keepdims=True), sum_ref.shape)
 
 
-def softmax_kernel(scale, n, *refs):
+def softmax_kernel(n, *refs):
     mine, other, (own_top_ref, own_sum_ref, out_ref) = refs[:n], refs[n : 2 * n], refs[2 * n :]
-    logits = jnp.concatenate([a[...] + b[...] for a, b in zip(mine, other)], axis=-1) * scale
+    logits = jnp.concatenate([logits_of(a, b) for a, b in zip(mine, other)], axis=-1)
     heads, share, cols = logits.shape
     own_top = own_top_ref[...][..., :1]
     top = jnp.maximum(own_top, jnp.max(logits, axis=-1, keepdims=True))
@@ -330,24 +370,16 @@
     def hop(y, k):
         return lax.ppermute(y, "seq", [(i, i ^ k) for i in range(n_seq)])
 
-    def values_of(rows, order):
-        return call(
-            value_kernel,
-            grouped,
-            (rows,),
-            hbm=(wv,),
-            order=order,
-            scratch=[pltpu.VMEM(wv.shape, bf16), pltpu.SemaphoreType.DMA((1,))],
-            flops=dots * d,
-        )
-
-    def split(keep, got, order=()):
-        return call(merge_kernel, (piece,) * inner, (keep, got), order=order)
+    coded = shape((heads, share, r), bf16)
+    scale = float(hsize * s * n_seq) ** -0.5
+    merge = functools.partial(merge_kernel, scale / UNIT)
 
     def reduce(own, *sent, order=()):
         parts = [hop(y, CORES * k) for k, y in zip(steps(inner)[1:], sent)]
-        total = call(functools.partial(sum_kernel, inner), piece, (own, *parts), order=order)
-        return total, hop(total, CORES * inner)
+        total, half = call(
+            functools.partial(sum_kernel, inner), (piece, coded), (own, *parts), order=order
+        )
+        return total, hop(half, CORES * inner)
 
     others = [
         lax.ppermute(x, "res", [(i, (i + k) % n_res) for i in range(n_res)])
@@ -378,8 +410,17 @@
         scratch=[half, half, keys, pltpu.SemaphoreType.DMA((2,))],
         flops=dots * (d + r // 2),
     )
-    pieces = split(keep, got)
-    values = [values_of(rows, pieces[:1])]
+    *pieces, top = call(merge, (piece, *[coded] * (inner - 1), part), (keep, got))
+    value, wv, wf = call(
+        own_value_kernel,
+        (grouped, shape(wv.shape, bf16), shape(wf.shape, bf16)),
+        (rows,),
+        hbm=(wv, wf),
+        order=pieces[:1],
+        scratch=[pltpu.SemaphoreType.DMA((2,))],
+        flops=dots * d,
+    )
+    values = [value]
     reduced = [reduce(*pieces, order=values)]
     for other in others:
         rows, send = call(
@@ -399,10 +440,9 @@
             scratch=[keys],
             flops=dots * (d // 2 + r // 2),
         )
-        pieces = split(keep, got)
-        values.append(values_of(rows, pieces[:1]))
+        pieces = call(merge, (piece, *[coded] * (inner - 1)), (keep, got, top))
+        values.append(call(value_kernel, grouped, (rows, wv), order=pieces[:1], flops=dots * d))
         reduced.append(reduce(*pieces, order=values[-1:]))
-    scale = float(hsize * s * n_seq) ** -0.5
 
     def gather(y, order=()):
         mine = [y] + [hop(y, CORES * k) for k in steps(inner)[1:]]
@@ -412,13 +452,13 @@
         return mine, hop(mine, 1)
 
     own_probs, own_top, own_sum = call(
-        functools.partial(own_softmax_kernel, scale),
+        own_softmax_kernel,
         (shape(piece.shape, bf16), piece, piece),
         reduced[0],
         order=(reduced[-1][0],),
     )
     probs = call(
-        functools.partial(softmax_kernel, scale, n_res - 1),
+        functools.partial(softmax_kernel, n_res - 1),
         shape((heads + 1, share, cols - r), bf16),
         (*(a for a, _ in reduced[1:]), *(b for _, b in reduced[1:]), own_top, own_sum),
     )

time: 49.2 us -> 47.5 us (0.965)
  waiting for transfers between devices: 12.6 us -> 10.9 us
  starting transfers between devices: 22 us -> 22.8 us
  Pallas kernels: 14.2 us -> 13.5 us
    ppermute x18, waiting for transfers between devices: 12.6 us -> 10.1 us  [hop(): return lax.ppermute(y, 'seq', [(i, i ^ k) for i in range(n_seq)])]
    ppermute x18, starting transfers between devices: 19 us -> 19.8 us  [hop(): return lax.ppermute(y, 'seq', [(i, i ^ k) for i in range(n_seq)])]
    ppermute x1, waiting for transfers between devices: 0.03 us -> 0.79 us  [body(): lax.ppermute(x, 'res', [(i, (i + k) % n_res) for i in range(n_res)])]
    pallas_call x17, Pallas kernels: 14.2 us -> 13.5 us  [call(): pl.pallas_call(kernel, out_shape=out_shape, in_specs=specs, out_specs=jax...]
  transfers between devices with their start and end apart: 19 -> 19, of which waited for: 11 -> 12; matrix products, arithmetic and copies ran while one was open for 0% -> 0% of each run, Pallas kernels for 24% -> 23%
where the time goes in v3:
time: 47.5 us; the launch traced here: 47.4 us
  starting transfers between devices  22.8 us (48%)
  Pallas kernels  13.5 us (28%)
  waiting for transfers between devices  10.9 us (23%)
    ppermute x18, starting transfers between devices, hop(): return lax.ppermute(y, 'seq', [(i, i ^ k) for i in range(n_seq)])  19.8 us
    pallas_call x17, Pallas kernels, call(): pl.pallas_call(kernel, out_shape=out_shape, in_specs=specs, out_specs=jax...  13.5 us
    ppermute x18, waiting for transfers between devices, hop(): return lax.ppermute(y, 'seq', [(i, i ^ k) for i in range(n_seq)])  10.1 us
    ppermute x1, starting transfers between devices, body(): lax.ppermute(x, 'res', [(i, (i + k) % n_res) for i in range(n_res)])  3 us
  transfers between devices with their start and end apart: 19, of which 12 were waited for; matrix products, arithmetic and copies ran while one was open for 0% of the time, Pallas kernels for 23%

profile of v3, /device:TPU:0, one launch (start us, length us, event | category | flops | bytes accessed | tf_op | source)
XLA Modules:
  0.0 47.4 jit_solution(11872904235745293784)
XLA Ops:
  0.0 3.0 %collective-permute-start = (bf16[3,128,768]{2,1,0:T(8,128)(2,1)}, bf16[3,128,768]{2,1,0:T(8,128)(2,1)S(1)}, u32[]{:S(2)}, u32[]{:S(2)}) collective-permute-start(bf16[3,128,768]{2,1,0:T(8,128)(2,1)} %x_hbm.1), channel_id=1, source_target_pairs={{0,1},{1,0},{2,3},{3,2},{4,5},{5,4},{6,7},{7,6},{8,9},{9,8},{10,11... | collective-permute-start | bytes 1769480 | tf_op jit(solution)/shard_map/ppermute | solution.py:385
  3.0 2.7 %shard_map.64 = (bf16[384,768]{1,0:T(8,128)(2,1)S(1)}, bf16[3,256,384]{2,1,0:T(8,128)(2,1)S(1)}, f32[4,6,32,128]{3,2,1,0:T(8,128)S(1)}) custom-call(bf16[3,128,768]{2,1,0:T(8,128)(2,1)} %x_hbm.1, f32[768]{0:T(1024)} %gain_ref.1, bf16[768,768]{1,0:T(8,128)(2,1)} %wk_ref.3, bf16[768,768]{1,0:T(8,128)(2,1)} %wq_hbm.3), custom_call_target="tpu_custom_call" | custom-call | flops 490733568 | tf_op jit(solution)/shard_map/pallas_call | solution.py:337
  5.8 2.3 %shard_map.65 = (bf16[3,256,384]{2,1,0:T(8,128)(2,1)S(1)}, f32[4,6,32,128]{3,2,1,0:T(8,128)S(1)}) custom-call(bf16[384,768]{1,0:T(8,128)(2,1)S(1)} %get-tuple-element.32.rows_ref, bf16[768,768]{1,0:T(8,128)(2,1)} %wk_ref.3, bf16[768,768]{1,0:T(8,128)(2,1)} %wq_hbm.3, f32[4,6,32,128]{3,2,1,0:T(8,128)S(1)} %get-tuple-element.33.after_ref), custom_call_target="tpu_custom_call" | custom-call | flops 490733568 | bytes 589824 | tf_op jit(solution)/shard_map/pallas_call | solution.py:337
  8.4 2.6 %collective-permute-start.2 = (bf16[6,32,128]{2,1,0:T(8,128)(2,1)S(1)}, bf16[6,32,128]{2,1,0:T(8,128)(2,1)S(1)}, u32[]{:S(2)}, u32[]{:S(2)}) collective-permute-start(bf16[6,32,128]{2,1,0:T(8,128)(2,1)S(1)} %get-tuple-element.36), channel_id=1, source_target_pairs={{0,12},{2,14},{4,8},{6,10},{8,4},{10,6},{12,0},{14,2},{16,28},{18,... | collective-permute-start | bytes 147464 | tf_op jit(solution)/shard_map/ppermute | solution.py:371
  11.9 2.0 %shard_map.67 = (bf16[6,128,384]{2,1,0:T(8,128)(2,1)S(1)}, bf16[768,768]{1,0:T(8,128)(2,1)S(1)}, bf16[768,768]{1,0:T(8,128)(2,1)S(1)}) custom-call(bf16[384,768]{1,0:T(8,128)(2,1)S(1)} %get-tuple-element.32.rows_ref, bf16[768,768]{1,0:T(8,128)(2,1)} %wv_hbm.1, bf16[768,768]{1,0:T(8,128)(2,1)} %wf_hbm.1, f32[6,32,128]{2,1,0:T(8,128)S(1)} %get-tuple-element.35.after_ref.own_ref), custom_call_target="tpu_custom_call" | custom-call | flops 452984832 | bytes 589824 | tf_op jit(solution)/shard_map/pallas_call | solution.py:337
  14.0 1.1 %collective-permute-done.3.refs_1_ = bf16[6,32,128]{2,1,0:T(8,128)(2,1)S(1)} collective-permute-done((bf16[6,32,128]{2,1,0:T(8,128)(2,1)S(1)}, bf16[6,32,128]{2,1,0:T(8,128)(2,1)S(1)}, u32[]{:S(2)}, u32[]{:S(2)}) %collective-permute-start.3) | collective-permute-done | bytes 49184 | tf_op jit(solution)/shard_map/ppermute | solution.py:371
  15.7 0.8 %collective-permute-done.x_ref = bf16[3,128,768]{2,1,0:T(8,128)(2,1)S(1)} collective-permute-done((bf16[3,128,768]{2,1,0:T(8,128)(2,1)}, bf16[3,128,768]{2,1,0:T(8,128)(2,1)S(1)}, u32[]{:S(2)}, u32[]{:S(2)}) %collective-permute-start) | collective-permute-done | bytes 589856 | tf_op jit(solution)/shard_map/ppermute | solution.py:385
  16.5 1.0 %shard_map.69 = (bf16[384,768]{1,0:T(8,128)(2,1)S(1)}, f32[4,6,32,128]{3,2,1,0:T(8,128)S(1)}) custom-call(bf16[3,128,768]{2,1,0:T(8,128)(2,1)S(1)} %collective-permute-done.x_ref, f32[768]{0:T(1024)S(1)} %copy-done.1, bf16[768,768]{1,0:T(8,128)(2,1)S(1)} %copy-done, bf16[3,256,384]{2,1,0:T(8,128)(2,1)S(1)} %get-tuple-element.31.q_ref, ...), custom_call_target="tpu_custom_call" | custom-call | flops 264241152 | bytes 2362368 | tf_op jit(solution)/shard_map/pallas_call | solution.py:337
  17.7 0.8 %shard_map.70.keep_ref = f32[4,6,32,128]{3,2,1,0:T(8,128)S(1)} custom-call(bf16[384,768]{1,0:T(8,128)(2,1)S(1)} %get-tuple-element.41.rows_ref, bf16[768,768]{1,0:T(8,128)(2,1)S(1)} %copy-done, bf16[3,256,384]{2,1,0:T(8,128)(2,1)S(1)} %get-tuple-element.42.q_ref, f32[4,6,32,128]{3,2,1,0:T(8,128)S(1)} %get-tuple-element.43.after_ref), custom_call_target="tpu_custom_call" | custom-call | flops 264241152 | bytes 2359296 | tf_op jit(solution)/shard_map/pallas_call | solution.py:337
  18.4 0.9 %collective-permute-done.5.got_ref = f32[4,6,32,128]{3,2,1,0:T(8,128)S(1)} collective-permute-done((f32[4,6,32,128]{3,2,1,0:T(8,128)S(1)}, f32[4,6,32,128]{3,2,1,0:T(8,128)S(1)}, u32[]{:S(2)}, u32[]{:S(2)}) %collective-permute-start.5) | collective-permute-done | bytes 393248 | tf_op jit(solution)/shard_map/ppermute | solution.py:371
  19.5 2.8 %collective-permute-start.6 = (bf16[6,32,128]{2,1,0:T(8,128)(2,1)S(1)}, bf16[6,32,128]{2,1,0:T(8,128)(2,1)S(1)}, u32[]{:S(2)}, u32[]{:S(2)}) collective-permute-start(bf16[6,32,128]{2,1,0:T(8,128)(2,1)S(1)} %get-tuple-element.46), channel_id=1, source_target_pairs={{0,12},{2,14},{4,8},{6,10},{8,4},{10,6},{12,0},{14,2},{16,28},{18,... | collective-permute-start | bytes 147464 | tf_op jit(solution)/shard_map/ppermute | solution.py:371
  23.1 2.8 %collective-permute-start.10 = (bf16[6,32,128]{2,1,0:T(8,128)(2,1)S(1)}, bf16[6,32,128]{2,1,0:T(8,128)(2,1)S(1)}, u32[]{:S(2)}, u32[]{:S(2)}) collective-permute-start(bf16[6,32,128]{2,1,0:T(8,128)(2,1)S(1)} %get-tuple-element.52), channel_id=1, source_target_pairs={{0,16},{2,18},{4,20},{6,22},{8,24},{10,26},{12,28},{14,30},{16,0},... | collective-permute-start | bytes 147464 | tf_op jit(solution)/shard_map/ppermute | solution.py:371
  25.9 0.6 %shard_map.72.refs_3_.refs_0_ = bf16[6,128,384]{2,1,0:T(8,128)(2,1)S(1)} custom-call(bf16[384,768]{1,0:T(8,128)(2,1)S(1)} %get-tuple-element.41.rows_ref, bf16[768,768]{1,0:T(8,128)(2,1)S(1)} %get-tuple-element.49.wv_ref, f32[6,32,128]{2,1,0:T(8,128)S(1)} %get-tuple-element.45.after_ref.own_ref), custom_call_target="tpu_custom_call" | custom-call | flops 452984832 | bytes 1769472 | tf_op jit(solution)/shard_map/pallas_call | solution.py:337
  27.2 2.5 %collective-permute-start.9 = (bf16[6,32,128]{2,1,0:T(8,128)(2,1)S(1)}, bf16[6,32,128]{2,1,0:T(8,128)(2,1)S(1)}, u32[]{:S(2)}, u32[]{:S(2)}) collective-permute-start(bf16[6,32,128]{2,1,0:T(8,128)(2,1)S(1)} %get-tuple-element.51), channel_id=1, source_target_pairs={{0,16},{2,18},{4,20},{6,22},{8,24},{10,26},{12,28},{14,30},{16,0},... | collective-permute-start | bytes 147464 | tf_op jit(solution)/shard_map/ppermute | solution.py:371
  30.5 1.5 %collective-permute-start.15 = (bf16[6,32,128]{2,1,0:T(8,128)(2,1)S(1)}, bf16[6,32,128]{2,1,0:T(8,128)(2,1)S(1)}, u32[]{:S(2)}, u32[]{:S(2)}) collective-permute-start(bf16[6,32,128]{2,1,0:T(8,128)(2,1)S(1)} %get-tuple-element.55.refs_0_), channel_id=1, source_target_pairs={{0,4},{2,6},{4,0},{6,2},{8,12},{10,14},{12,8},{14,10},{16,20},{18,... | collective-permute-start | bytes 147464 | tf_op jit(solution)/shard_map/ppermute | solution.py:371
  32.0 1.6 %collective-permute-start.14 = (bf16[6,32,128]{2,1,0:T(8,128)(2,1)S(1)}, bf16[6,32,128]{2,1,0:T(8,128)(2,1)S(1)}, u32[]{:S(2)}, u32[]{:S(2)}) collective-permute-start(bf16[6,32,128]{2,1,0:T(8,128)(2,1)S(1)} %get-tuple-element.55.refs_0_), channel_id=1, source_target_pairs={{0,12},{2,14},{4,8},{6,10},{8,4},{10,6},{12,0},{14,2},{16,28},{18,... | collective-permute-start | bytes 147464 | tf_op jit(solution)/shard_map/ppermute | solution.py:371
  34.6 2.4 %collective-permute-done.14.refs_1_ = bf16[6,32,128]{2,1,0:T(8,128)(2,1)S(1)} collective-permute-done((bf16[6,32,128]{2,1,0:T(8,128)(2,1)S(1)}, bf16[6,32,128]{2,1,0:T(8,128)(2,1)S(1)}, u32[]{:S(2)}, u32[]{:S(2)}) %collective-permute-start.14) | collective-permute-done | bytes 49184 | tf_op jit(solution)/shard_map/ppermute | solution.py:371
  37.1 1.6 %collective-permute-start.13 = (bf16[7,32,128]{2,1,0:T(8,128)(2,1)S(1)}, bf16[7,32,128]{2,1,0:T(8,128)(2,1)S(1)}, u32[]{:S(2)}, u32[]{:S(2)}) collective-permute-start(bf16[7,32,128]{2,1,0:T(8,128)(2,1)S(1)} %shard_map.75.refs_4_.refs_0_), channel_id=1, source_target_pairs={{0,8},{2,10},{4,12},{6,14},{8,0},{10,2},{12,4},{14,6},{16,24},{18,... | collective-permute-start | bytes 172040 | tf_op jit(solution)/shard_map/ppermute | solution.py:371
  39.2 1.4 %collective-permute-start.11 = (bf16[7,32,128]{2,1,0:T(8,128)(2,1)S(1)}, bf16[7,32,128]{2,1,0:T(8,128)(2,1)S(1)}, u32[]{:S(2)}, u32[]{:S(2)}) collective-permute-start(bf16[7,32,128]{2,1,0:T(8,128)(2,1)S(1)} %shard_map.75.refs_4_.refs_0_), channel_id=1, source_target_pairs={{0,12},{2,14},{4,8},{6,10},{8,4},{10,6},{12,0},{14,2},{16,28},{18,... | collective-permute-start | bytes 172040 | tf_op jit(solution)/shard_map/ppermute | solution.py:371
  41.4 2.1 %collective-permute-done.12.refs_2_ = bf16[7,32,128]{2,1,0:T(8,128)(2,1)S(1)} collective-permute-done((bf16[7,32,128]{2,1,0:T(8,128)(2,1)S(1)}, bf16[7,32,128]{2,1,0:T(8,128)(2,1)S(1)}, u32[]{:S(2)}, u32[]{:S(2)}) %collective-permute-start.12) | collective-permute-done | bytes 57376 | tf_op jit(solution)/shard_map/ppermute | solution.py:371
  43.5 0.8 %collective-permute-done.11.refs_1_ = bf16[7,32,128]{2,1,0:T(8,128)(2,1)S(1)} collective-permute-done((bf16[7,32,128]{2,1,0:T(8,128)(2,1)S(1)}, bf16[7,32,128]{2,1,0:T(8,128)(2,1)S(1)}, u32[]{:S(2)}, u32[]{:S(2)}) %collective-permute-start.11) | collective-permute-done | bytes 57376 | tf_op jit(solution)/shard_map/ppermute | solution.py:371
  44.4 0.7 %shard_map.79.refs_2_ = f32[384,768]{1,0:T(8,128)S(1)} custom-call(bf16[4,7,32,128]{3,2,1,0:T(8,128)(2,1)S(1)} %shard_map.78.p_ref, bf16[6,128,384]{2,1,0:T(8,128)(2,1)S(1)} %shard_map.72.refs_3_.refs_0_, f32[6,128,384]{2,1,0:T(8,128)S(1)} %shard_map.77.refs_4_.refs_1_, bf16[768,768]{1,0:T(8,128)(2,1)S(1)} %get-tuple-element.56.refs_2_.refs_3_), custom_call_target="tpu_custom_call" | custom-call | flops 301989888 | bytes 3178496 | tf_op jit(solution)/shard_map/pallas_call | solution.py:337
  45.1 0.7 %collective-permute-done.18.p_ref = bf16[4,7,32,128]{3,2,1,0:T(8,128)(2,1)S(1)} collective-permute-done((bf16[4,7,32,128]{3,2,1,0:T(8,128)(2,1)S(1)}, bf16[4,7,32,128]{3,2,1,0:T(8,128)(2,1)S(1)}, u32[]{:S(2)}, u32[]{:S(2)}) %collective-permute-start.18) | collective-permute-done | bytes 229408 | tf_op jit(solution)/shard_map/ppermute | solution.py:371
  45.9 1.5 %shard_map.80 = bf16[3,128,768]{2,1,0:T(8,128)(2,1)} custom-call(bf16[4,7,32,128]{3,2,1,0:T(8,128)(2,1)S(1)} %collective-permute-done.18.p_ref, bf16[6,128,384]{2,1,0:T(8,128)(2,1)S(1)} %shard_map.72.refs_3_.refs_0_, f32[6,128,384]{2,1,0:T(8,128)S(1)} %shard_map.77.refs_4_.refs_1_, f32[384,768]{1,0:T(8,128)S(1)} %shard_map.79.refs_2_, ...), custom_call_target="tpu_custom_call" | custom-call | flops 301989888 | bytes 4358144 | tf_op jit(solution)/shard_map/pallas_call | solution.py:337
  (35 shorter events, 6.9 us)
Async XLA Ops:
  0.0 16.5 %collective-permute-start = (bf16[3,128,768]{2,1,0:T(8,128)(2,1)}, bf16[3,128,768]{2,1,0:T(8,128)(2,1)S(1)}, u32[]{:S(2)}, u32[]{:S(2)}) collective-permute-start(bf16[3,128,768]{2,1,0:T(8,128)(2,1)} %x_hbm.1), channel_id=1, source_target_pairs={{0,1},{1,0},{2,3},{3,2},{4,5},{5,4},{6,7},{7,6},{8,9},{9,8},{10,11... | collective-permute-start | bytes 1769480 | tf_op jit(solution)/shard_map/ppermute | solution.py:385
  5.7 2.4 %collective-permute-start.1 = (f32[4,6,32,128]{3,2,1,0:T(8,128)S(1)}, f32[4,6,32,128]{3,2,1,0:T(8,128)S(1)}, u32[]{:S(2)}, u32[]{:S(2)}) collective-permute-start(f32[4,6,32,128]{3,2,1,0:T(8,128)S(1)} %get-tuple-element.33.after_ref), channel_id=1, source_target_pairs={{0,2},{2,0},{4,6},{6,4},{8,10},{10,8},{12,14},{14,12},{16,18},{18,... | collective-permute-start | bytes 1179656 | tf_op jit(solution)/shard_map/ppermute | solution.py:371
  8.4 5.6 %collective-permute-start.2 = (bf16[6,32,128]{2,1,0:T(8,128)(2,1)S(1)}, bf16[6,32,128]{2,1,0:T(8,128)(2,1)S(1)}, u32[]{:S(2)}, u32[]{:S(2)}) collective-permute-start(bf16[6,32,128]{2,1,0:T(8,128)(2,1)S(1)} %get-tuple-element.36), channel_id=1, source_target_pairs={{0,12},{2,14},{4,8},{6,10},{8,4},{10,6},{12,0},{14,2},{16,28},{18,... | collective-permute-start | bytes 147464 | tf_op jit(solution)/shard_map/ppermute | solution.py:371
  11.0 4.1 %collective-permute-start.3 = (bf16[6,32,128]{2,1,0:T(8,128)(2,1)S(1)}, bf16[6,32,128]{2,1,0:T(8,128)(2,1)S(1)}, u32[]{:S(2)}, u32[]{:S(2)}) collective-permute-start(bf16[6,32,128]{2,1,0:T(8,128)(2,1)S(1)} %get-tuple-element.37), channel_id=1, source_target_pairs={{0,4},{2,6},{4,0},{6,2},{8,12},{10,14},{12,8},{14,10},{16,20},{18,... | collective-permute-start | bytes 147464 | tf_op jit(solution)/shard_map/ppermute | solution.py:371
  11.5 4.1 %collective-permute-start.4 = (bf16[6,32,128]{2,1,0:T(8,128)(2,1)S(1)}, bf16[6,32,128]{2,1,0:T(8,128)(2,1)S(1)}, u32[]{:S(2)}, u32[]{:S(2)}) collective-permute-start(bf16[6,32,128]{2,1,0:T(8,128)(2,1)S(1)} %get-tuple-element.38), channel_id=1, source_target_pairs={{0,8},{2,10},{4,12},{6,14},{8,0},{10,2},{12,4},{14,6},{16,24},{18,... | collective-permute-start | bytes 147464 | tf_op jit(solution)/shard_map/ppermute | solution.py:371
  11.9 4.6 %copy-start = (bf16[768,768]{1,0:T(8,128)(2,1)S(1)}, bf16[768,768]{1,0:T(8,128)(2,1)}, u32[]{:S(2)}) copy-start(bf16[768,768]{1,0:T(8,128)(2,1)} %wk_ref.3) | copy-start | bytes 3538948
  11.9 4.6 %copy-start.1 = (f32[768]{0:T(1024)S(1)}, f32[768]{0:T(1024)}, u32[]{:S(2)}) copy-start(f32[768]{0:T(1024)} %gain_ref.1) | copy-start | bytes 9220
  17.6 1.8 %collective-permute-start.5 = (f32[4,6,32,128]{3,2,1,0:T(8,128)S(1)}, f32[4,6,32,128]{3,2,1,0:T(8,128)S(1)}, u32[]{:S(2)}, u32[]{:S(2)}) collective-permute-start(f32[4,6,32,128]{3,2,1,0:T(8,128)S(1)} %get-tuple-element.43.after_ref), channel_id=1, source_target_pairs={{0,2},{2,0},{4,6},{6,4},{8,10},{10,8},{12,14},{14,12},{16,18},{18,... | collective-permute-start | bytes 1179656 | tf_op jit(solution)/shard_map/ppermute | solution.py:371
  19.5 7.0 %collective-permute-start.6 = (bf16[6,32,128]{2,1,0:T(8,128)(2,1)S(1)}, bf16[6,32,128]{2,1,0:T(8,128)(2,1)S(1)}, u32[]{:S(2)}, u32[]{:S(2)}) collective-permute-start(bf16[6,32,128]{2,1,0:T(8,128)(2,1)S(1)} %get-tuple-element.46), channel_id=1, source_target_pairs={{0,12},{2,14},{4,8},{6,10},{8,4},{10,6},{12,0},{14,2},{16,28},{18,... | collective-permute-start | bytes 147464 | tf_op jit(solution)/shard_map/ppermute | solution.py:371
  22.3 4.2 %collective-permute-start.7 = (bf16[6,32,128]{2,1,0:T(8,128)(2,1)S(1)}, bf16[6,32,128]{2,1,0:T(8,128)(2,1)S(1)}, u32[]{:S(2)}, u32[]{:S(2)}) collective-permute-start(bf16[6,32,128]{2,1,0:T(8,128)(2,1)S(1)} %get-tuple-element.47), channel_id=1, source_target_pairs={{0,4},{2,6},{4,0},{6,2},{8,12},{10,14},{12,8},{14,10},{16,20},{18,... | collective-permute-start | bytes 147464 | tf_op jit(solution)/shard_map/ppermute | solution.py:371
  22.8 4.2 %collective-permute-start.8 = (bf16[6,32,128]{2,1,0:T(8,128)(2,1)S(1)}, bf16[6,32,128]{2,1,0:T(8,128)(2,1)S(1)}, u32[]{:S(2)}, u32[]{:S(2)}) collective-permute-start(bf16[6,32,128]{2,1,0:T(8,128)(2,1)S(1)} %get-tuple-element.48), channel_id=1, source_target_pairs={{0,8},{2,10},{4,12},{6,14},{8,0},{10,2},{12,4},{14,6},{16,24},{18,... | collective-permute-start | bytes 147464 | tf_op jit(solution)/shard_map/ppermute | solution.py:371
  23.1 6.7 %collective-permute-start.10 = (bf16[6,32,128]{2,1,0:T(8,128)(2,1)S(1)}, bf16[6,32,128]{2,1,0:T(8,128)(2,1)S(1)}, u32[]{:S(2)}, u32[]{:S(2)}) collective-permute-start(bf16[6,32,128]{2,1,0:T(8,128)(2,1)S(1)} %get-tuple-element.52), channel_id=1, source_target_pairs={{0,16},{2,18},{4,20},{6,22},{8,24},{10,26},{12,28},{14,30},{16,0},... | collective-permute-start | bytes 147464 | tf_op jit(solution)/shard_map/ppermute | solution.py:371
  27.2 6.3 %collective-permute-start.9 = (bf16[6,32,128]{2,1,0:T(8,128)(2,1)S(1)}, bf16[6,32,128]{2,1,0:T(8,128)(2,1)S(1)}, u32[]{:S(2)}, u32[]{:S(2)}) collective-permute-start(bf16[6,32,128]{2,1,0:T(8,128)(2,1)S(1)} %get-tuple-element.51), channel_id=1, source_target_pairs={{0,16},{2,18},{4,20},{6,22},{8,24},{10,26},{12,28},{14,30},{16,0},... | collective-permute-start | bytes 147464 | tf_op jit(solution)/shard_map/ppermute | solution.py:371
  30.0 4.3 %collective-permute-start.16 = (bf16[6,32,128]{2,1,0:T(8,128)(2,1)S(1)}, bf16[6,32,128]{2,1,0:T(8,128)(2,1)S(1)}, u32[]{:S(2)}, u32[]{:S(2)}) collective-permute-start(bf16[6,32,128]{2,1,0:T(8,128)(2,1)S(1)} %get-tuple-element.55.refs_0_), channel_id=1, source_target_pairs={{0,8},{2,10},{4,12},{6,14},{8,0},{10,2},{12,4},{14,6},{16,24},{18,... | collective-permute-start | bytes 147464 | tf_op jit(solution)/shard_map/ppermute | solution.py:371
  30.5 4.1 %collective-permute-start.15 = (bf16[6,32,128]{2,1,0:T(8,128)(2,1)S(1)}, bf16[6,32,128]{2,1,0:T(8,128)(2,1)S(1)}, u32[]{:S(2)}, u32[]{:S(2)}) collective-permute-start(bf16[6,32,128]{2,1,0:T(8,128)(2,1)S(1)} %get-tuple-element.55.refs_0_), channel_id=1, source_target_pairs={{0,4},{2,6},{4,0},{6,2},{8,12},{10,14},{12,8},{14,10},{16,20},{18,... | collective-permute-start | bytes 147464 | tf_op jit(solution)/shard_map/ppermute | solution.py:371
  32.0 5.0 %collective-permute-start.14 = (bf16[6,32,128]{2,1,0:T(8,128)(2,1)S(1)}, bf16[6,32,128]{2,1,0:T(8,128)(2,1)S(1)}, u32[]{:S(2)}, u32[]{:S(2)}) collective-permute-start(bf16[6,32,128]{2,1,0:T(8,128)(2,1)S(1)} %get-tuple-element.55.refs_0_), channel_id=1, source_target_pairs={{0,12},{2,14},{4,8},{6,10},{8,4},{10,6},{12,0},{14,2},{16,28},{18,... | collective-permute-start | bytes 147464 | tf_op jit(solution)/shard_map/ppermute | solution.py:371
  37.0 3.6 %collective-permute-start.17 = (bf16[4,6,32,128]{3,2,1,0:T(8,128)(2,1)S(1)}, bf16[4,6,32,128]{3,2,1,0:T(8,128)(2,1)S(1)}, u32[]{:S(2)}, u32[]{:S(2)}) collective-permute-start(bf16[4,6,32,128]{3,2,1,0:T(8,128)(2,1)S(1)} %shard_map.76.mine_ref), channel_id=1, source_target_pairs={{0,2},{2,0},{4,6},{6,4},{8,10},{10,8},{12,14},{14,12},{16,18},{18,... | collective-permute-start | bytes 589832 | tf_op jit(solution)/shard_map/ppermute | solution.py:371
  37.1 4.3 %collective-permute-start.13 = (bf16[7,32,128]{2,1,0:T(8,128)(2,1)S(1)}, bf16[7,32,128]{2,1,0:T(8,128)(2,1)S(1)}, u32[]{:S(2)}, u32[]{:S(2)}) collective-permute-start(bf16[7,32,128]{2,1,0:T(8,128)(2,1)S(1)} %shard_map.75.refs_4_.refs_0_), channel_id=1, source_target_pairs={{0,8},{2,10},{4,12},{6,14},{8,0},{10,2},{12,4},{14,6},{16,24},{18,... | collective-permute-start | bytes 172040 | tf_op jit(solution)/shard_map/ppermute | solution.py:371
  38.7 4.8 %collective-permute-start.12 = (bf16[7,32,128]{2,1,0:T(8,128)(2,1)S(1)}, bf16[7,32,128]{2,1,0:T(8,128)(2,1)S(1)}, u32[]{:S(2)}, u32[]{:S(2)}) collective-permute-start(bf16[7,32,128]{2,1,0:T(8,128)(2,1)S(1)} %shard_map.75.refs_4_.refs_0_), channel_id=1, source_target_pairs={{0,4},{2,6},{4,0},{6,2},{8,12},{10,14},{12,8},{14,10},{16,20},{18,... | collective-permute-start | bytes 172040 | tf_op jit(solution)/shard_map/ppermute | solution.py:371
  39.2 5.1 %collective-permute-start.11 = (bf16[7,32,128]{2,1,0:T(8,128)(2,1)S(1)}, bf16[7,32,128]{2,1,0:T(8,128)(2,1)S(1)}, u32[]{:S(2)}, u32[]{:S(2)}) collective-permute-start(bf16[7,32,128]{2,1,0:T(8,128)(2,1)S(1)} %shard_map.75.refs_4_.refs_0_), channel_id=1, source_target_pairs={{0,12},{2,14},{4,8},{6,10},{8,4},{10,6},{12,0},{14,2},{16,28},{18,... | collective-permute-start | bytes 172040 | tf_op jit(solution)/shard_map/ppermute | solution.py:371
  44.3 1.6 %collective-permute-start.18 = (bf16[4,7,32,128]{3,2,1,0:T(8,128)(2,1)S(1)}, bf16[4,7,32,128]{3,2,1,0:T(8,128)(2,1)S(1)}, u32[]{:S(2)}, u32[]{:S(2)}) collective-permute-start(bf16[4,7,32,128]{3,2,1,0:T(8,128)(2,1)S(1)} %shard_map.78.p_ref), channel_id=1, source_target_pairs={{0,2},{2,0},{4,6},{6,4},{8,10},{10,8},{12,14},{14,12},{16,18},{18,... | collective-permute-start | bytes 688136 | tf_op jit(solution)/shard_map/ppermute | solution.py:371

commit v4 on v3

--- a/solution.py
+++ b/solution.py
@@ -91,16 +91,18 @@
 
 def own_send_kernel(
     x_hbm, gain_hbm, wk_hbm, wq_hbm,
-    rows_ref, q_ref, send_ref,
+    rows_ref, q_ref, send_ref, wk_keep_ref, wq_keep_ref,
     x_ref, gain_ref, wk_ref, wq_ref, k_scr, sems,
 ):
-    side = 1 - spot(1)[0]
+    core = spot(1)[0]
     copies = load(
         (
             (x_hbm, x_ref),
             (gain_hbm, gain_ref),
-            (half_of(wk_hbm, side), wk_ref),
-            (half_of(wq_hbm, side), wq_ref),
+            (half_of(wk_hbm, 1 - core), wk_ref),
+            (half_of(wq_hbm, 1 - core), wq_ref),
+            (half_of(wk_hbm, core), wk_keep_ref),
+            (half_of(wq_hbm, core), wq_keep_ref),
         ),
         sems,
     )
@@ -113,19 +115,14 @@
     copies[3].wait()
     write_queries(rows_ref[...], wq_ref, s, d // HEADS, q_ref)
     write_scores(q_ref, k_scr, send_ref)
-
-
-def own_keep_kernel(
-    rows_ref, wk_hbm, wq_hbm, after_ref, q_ref, keep_ref, wk_ref, wq_ref, k_scr, sems
-):
-    side = spot(1)[0]
-    copies = load(((half_of(wk_hbm, side), wk_ref), (half_of(wq_hbm, side), wq_ref)), sems)
-    d = rows_ref.shape[1]
+    copies[4].wait()
+    copies[5].wait()
+
+
+def own_keep_kernel(rows_ref, wk_ref, wq_ref, after_ref, q_ref, keep_ref, k_scr):
     s = rows_ref.shape[0] // k_scr.shape[1]
-    copies[0].wait()
     write_keys(rows_ref[...], wk_ref, s, k_scr)
-    copies[1].wait()
-    write_queries(rows_ref[...], wq_ref, s, d // HEADS, q_ref)
+    write_queries(rows_ref[...], wq_ref, s, rows_ref.shape[1] // HEADS, q_ref)
     write_scores(q_ref, k_scr, keep_ref)
 
 
@@ -263,13 +260,48 @@
     return got
 
 
-def own_attend_kernel(hsize, mine_ref, got_ref, v_ref, out_ref):
-    core = spot(mine_ref.shape[0])[0]
-    per_core = v_ref.shape[0] // CORES
-    for p_ref, side in ((mine_ref, core), (got_ref, 1 - core)):
-        for t in range(per_core):
-            g = side * per_core + t
-            out_ref[g] = weighted(p_ref, (v_ref,), g, t, hsize)
+def near(inner):
+    rest = list(range(1, inner - 1))
+    return list(zip(rest[::2], rest[1::2]))
+
+
+def share_kernel(mine_ref, got_ref, out_ref):
+    core = spot(1)[0]
+    out_ref[core] = mine_ref[...]
+    out_ref[1 - core] = got_ref[...]
+
+
+def swap_kernel(n, *refs):
+    out_ref = refs[-1]
+    for j in range(n):
+        out_ref[CORES * j : CORES * (j + 1)] = refs[j][...]
+    out_ref[CORES * n] = refs[n][...]
+
+
+def own_attend_kernel(hsize, n, share_ref, *refs):
+    near_refs, (far_ref, got_ref, v_ref, out_ref, far_scr) = refs[:n], refs[n:]
+    inner = CORES * n + 2
+    core = spot(1)[0]
+    far_scr[core] = far_ref[...]
+    far_scr[1 - core] = got_ref[CORES * n]
+    at = {k: j for j, k in enumerate(steps(inner))}
+    blocks, places = [share_ref, far_scr], [0, at[inner - 1]]
+    for j, (a, b) in enumerate(near(inner)):
+        blocks += [near_refs[j], got_ref.at[CORES * j : CORES * (j + 1)]]
+        places += [at[a] + core * (at[b] - at[a]), at[b] + core * (at[a] - at[b])]
+    heads, share, _ = share_ref.shape[1:]
+    pack = LANES // hsize
+    r = share * inner
+    for g in range(v_ref.shape[0]):
+        side, t = divmod(g, heads // pack)
+        p = jnp.concatenate(
+            [block[side, t * pack + h] for h in range(pack) for block in blocks], axis=0
+        )
+        both = jnp.dot(p, v_ref[g], preferred_element_type=jnp.float32)
+        got = pick([both[h * r : (h + 1) * r] for h in range(pack)], both.shape[1], hsize)
+        for j, place in enumerate(places):
+            rows = pl.ds(pl.multiple_of(place * share, share), share)
+            out_ref[g, rows] = got[j * share : (j + 1) * share]
 
 
 def attended(p_ref, v_refs, own_ref, side, hsize):
@@ -321,11 +353,17 @@
         part = slice(i * r, (i + 1) * r)
         mixed = half_ref[part] + jnp.dot(rows[part], w, preferred_element_type=jnp.float32)
         mixed = mixed.astype(out_ref.dtype)
+        out_ref[i] = mixed
         for n, k in enumerate(steps(pieces)):
             start = pl.multiple_of((chip ^ k) * share, share)
-            out_ref[i, pl.ds(start, share)] = mixed[n * share : (n + 1) * share]
-        copies.append(pltpu.make_async_copy(out_ref.at[i], out_hbm.at[i], sems.at[i]))
-        copies[-1].start()
+            copies.append(
+                pltpu.make_async_copy(
+                    out_ref.at[i, n * share : (n + 1) * share],
+                    out_hbm.at[i, pl.ds(start, share)],
+                    sems.at[i, n],
+                )
+            )
+            copies[-1].start()
     for copy in copies:
         copy.wait()
 
@@ -385,9 +423,10 @@
         lax.ppermute(x, "res", [(i, (i + k) % n_res) for i in range(n_res)])
         for k in range(1, n_res)
     ]
-    rows, q_send, send = call(
+    kept = shape((d, d // CORES), bf16)
+    rows, q_send, send, wk_keep, wq_keep = call(
         own_send_kernel,
-        (normed, queries, part),
+        (normed, queries, part, kept, kept),
         (),
         hbm=(x, gain, wk, wq),
         scratch=[
@@ -396,7 +435,7 @@
             half,
             half,
             keys,
-            pltpu.SemaphoreType.DMA((4,)),
+            pltpu.SemaphoreType.DMA((6,)),
         ],
         flops=dots * (d + r // 2),
     )
@@ -404,10 +443,9 @@
     q_keep, keep = call(
         own_keep_kernel,
         (queries, part),
-        (rows,),
-        hbm=(wk, wq),
+        (rows, wk_keep, wq_keep),
         order=(send,),
-        scratch=[half, half, keys, pltpu.SemaphoreType.DMA((2,))],
+        scratch=[keys],
         flops=dots * (d + r // 2),
     )
     *pieces, top = call(merge, (piece, *[coded] * (inner - 1), part), (keep, got))
@@ -462,11 +500,24 @@
         shape((heads + 1, share, cols - r), bf16),
         (*(a for a, _ in reduced[1:]), *(b for _, b in reduced[1:]), own_top, own_sum),
     )
-    own_mine, own_got = gather(own_probs, order=(probs,))
+    mate = hop(own_probs, 1)
+    far = hop(own_probs, CORES * (inner - 1))
+    both = call(share_kernel, shape((CORES, *own_probs.shape), bf16), (own_probs, mate))
+    came = []
+    for ab in near(inner):
+        pairs = [(i, i ^ (CORES * ab[i % CORES])) for i in range(n_seq)]
+        came.append(lax.ppermute(both, "seq", pairs))
+    sent = call(
+        functools.partial(swap_kernel, len(came)),
+        shape((CORES * len(came) + 1, *far.shape), bf16),
+        (*came, far),
+        order=(probs,),
+    )
     own_part = call(
-        functools.partial(own_attend_kernel, hsize),
+        functools.partial(own_attend_kernel, hsize, len(came)),
         shape(grouped.shape, f32),
-        (own_mine, own_got, values[0]),
+        (both, *came, far, hop(sent, 1), values[0]),
+        scratch=[pltpu.VMEM(both.shape, bf16)],
         flops=dots * r,
     )
     mine, got = gather(probs, order=(own_part,))
@@ -480,7 +531,7 @@
         functools.partial(mix_kernel, hsize, n_res - 1),
         shape((s, r, d), bf16),
         (got, *values[1:], own_part, half_mix, wf),
-        scratch=[pltpu.VMEM(x.shape, bf16), pltpu.SemaphoreType.DMA((s,))],
+        scratch=[pltpu.VMEM(x.shape, bf16), pltpu.SemaphoreType.DMA((s, inner))],
         flops=dots * (d + cols) // 2,
         out_space=HBM,
     )

time: 47.5 us -> 50 us (1.053)
  waiting for transfers between devices: 10.9 us -> 14.7 us
  Pallas kernels: 13.5 us -> 12.3 us
    ppermute x18 -> x17, waiting for transfers between devices: 10.1 us -> 13.3 us  [hop(): return lax.ppermute(y, 'seq', [(i, i ^ k) for i in range(n_seq)])]
    ppermute x18 -> x17, starting transfers between devices: 19.8 us -> 18 us  [hop(): return lax.ppermute(y, 'seq', [(i, i ^ k) for i in range(n_seq)])]
    ppermute x0 -> x1, starting transfers between devices: none -> 1.59 us  [body(): came.append(lax.ppermute(both, 'seq', pairs))]
    pallas_call x17 -> x18, Pallas kernels: 13.5 us -> 12.3 us  [call(): pl.pallas_call(kernel, out_shape=out_shape, in_specs=specs, out_specs=jax...]
    ppermute x1, waiting for transfers between devices: 0.79 us -> 1.39 us  [body(): lax.ppermute(x, 'res', [(i, (i + k) % n_res) for i in range(n_res)])]
  transfers between devices with their start and end apart: 19 -> 19, of which waited for: 12 -> 14; matrix products, arithmetic and copies ran while one was open for 0% -> 0% of each run, Pallas kernels for 23% -> 19%
where the time goes in v4:
time: 50 us; the launch traced here: 49.8 us
  starting transfers between devices  22.6 us (45%)
  waiting for transfers between devices  14.7 us (29%)
  Pallas kernels  12.3 us (25%)
    ppermute x17, starting transfers between devices, hop(): return lax.ppermute(y, 'seq', [(i, i ^ k) for i in range(n_seq)])  18 us
    ppermute x17, waiting for transfers between devices, hop(): return lax.ppermute(y, 'seq', [(i, i ^ k) for i in range(n_seq)])  13.3 us
    pallas_call x18, Pallas kernels, call(): pl.pallas_call(kernel, out_shape=out_shape, in_specs=specs, out_specs=jax...  12.3 us
    ppermute x1, starting transfers between devices, body(): lax.ppermute(x, 'res', [(i, (i + k) % n_res) for i in range(n_res)])  3 us
    ppermute x1, starting transfers between devices, body(): came.append(lax.ppermute(both, 'seq', pairs))  1.59 us
    ppermute x1, waiting for transfers between devices, body(): lax.ppermute(x, 'res', [(i, (i + k) % n_res) for i in range(n_res)])  1.39 us
  transfers between devices with their start and end apart: 19, of which 14 were waited for; matrix products, arithmetic and copies ran while one was open for 0% of the time, Pallas kernels for 19%

profile of v4, /device:TPU:0, one launch (start us, length us, event | category | flops | bytes accessed | tf_op | source)
XLA Modules:
  0.0 49.8 jit_solution(713312145391877812)
XLA Ops:
  0.0 3.0 %collective-permute-start = (bf16[3,128,768]{2,1,0:T(8,128)(2,1)}, bf16[3,128,768]{2,1,0:T(8,128)(2,1)S(1)}, u32[]{:S(2)}, u32[]{:S(2)}) collective-permute-start(bf16[3,128,768]{2,1,0:T(8,128)(2,1)} %x_hbm.1), channel_id=1, source_target_pairs={{0,1},{1,0},{2,3},{3,2},{4,5},{5,4},{6,7},{7,6},{8,9},{9,8},{10,11... | collective-permute-start | bytes 1769480 | tf_op jit(solution)/shard_map/ppermute | solution.py:423
  3.0 2.8 %shard_map.64 = (bf16[384,768]{1,0:T(8,128)(2,1)S(1)}, bf16[3,256,384]{2,1,0:T(8,128)(2,1)S(1)}, f32[4,6,32,128]{3,2,1,0:T(8,128)S(1)}, bf16[768,384]{1,0:T(8,128)(2,1)S(1)}, bf16[768,384]{1,0:T(8,128)(2,1)S(1)}) custom-call(bf16[3,128,768]{2,1,0:T(8,128)(2,1)} %x_hbm.1, f32[768]{0:T(1024)} %gain_ref.1, bf16[768,768]{1,0:T(8,128)(2,1)} %wk_ref.3, ...), custom_call_target="tpu_custom_call" | custom-call | flops 490733568 | tf_op jit(solution)/shard_map/pallas_call | solution.py:375
  5.8 1.0 %shard_map.65 = (bf16[3,256,384]{2,1,0:T(8,128)(2,1)S(1)}, f32[4,6,32,128]{3,2,1,0:T(8,128)S(1)}) custom-call(bf16[384,768]{1,0:T(8,128)(2,1)S(1)} %get-tuple-element.34.rows_ref, bf16[768,384]{1,0:T(8,128)(2,1)S(1)} %get-tuple-element.35.wk_ref, bf16[768,384]{1,0:T(8,128)(2,1)S(1)} %get-tuple-element.36.wq_ref, ...), custom_call_target="tpu_custom_call" | custom-call | flops 490733568 | bytes 1769472 | tf_op jit(solution)/shard_map/pallas_call | solution.py:375
  7.8 2.6 %collective-permute-start.2 = (bf16[6,32,128]{2,1,0:T(8,128)(2,1)S(1)}, bf16[6,32,128]{2,1,0:T(8,128)(2,1)S(1)}, u32[]{:S(2)}, u32[]{:S(2)}) collective-permute-start(bf16[6,32,128]{2,1,0:T(8,128)(2,1)S(1)} %get-tuple-element.40), channel_id=1, source_target_pairs={{0,12},{2,14},{4,8},{6,10},{8,4},{10,6},{12,0},{14,2},{16,28},{18,... | collective-permute-start | bytes 147464 | tf_op jit(solution)/shard_map/ppermute | solution.py:409
  11.3 2.0 %shard_map.67 = (bf16[6,128,384]{2,1,0:T(8,128)(2,1)S(1)}, bf16[768,768]{1,0:T(8,128)(2,1)S(1)}, bf16[768,768]{1,0:T(8,128)(2,1)S(1)}) custom-call(bf16[384,768]{1,0:T(8,128)(2,1)S(1)} %get-tuple-element.34.rows_ref, bf16[768,768]{1,0:T(8,128)(2,1)} %wv_hbm.1, bf16[768,768]{1,0:T(8,128)(2,1)} %wf_hbm.1, f32[6,32,128]{2,1,0:T(8,128)S(1)} %get-tuple-element.39.after_ref.own_ref), custom_call_target="tpu_custom_call" | custom-call | flops 452984832 | bytes 589824 | tf_op jit(solution)/shard_map/pallas_call | solution.py:375
  13.4 1.1 %collective-permute-done.3.refs_1_ = bf16[6,32,128]{2,1,0:T(8,128)(2,1)S(1)} collective-permute-done((bf16[6,32,128]{2,1,0:T(8,128)(2,1)S(1)}, bf16[6,32,128]{2,1,0:T(8,128)(2,1)S(1)}, u32[]{:S(2)}, u32[]{:S(2)}) %collective-permute-start.3) | collective-permute-done | bytes 49184 | tf_op jit(solution)/shard_map/ppermute | solution.py:409
  15.1 1.4 %collective-permute-done.x_ref = bf16[3,128,768]{2,1,0:T(8,128)(2,1)S(1)} collective-permute-done((bf16[3,128,768]{2,1,0:T(8,128)(2,1)}, bf16[3,128,768]{2,1,0:T(8,128)(2,1)S(1)}, u32[]{:S(2)}, u32[]{:S(2)}) %collective-permute-start) | collective-permute-done | bytes 589856 | tf_op jit(solution)/shard_map/ppermute | solution.py:423
  16.5 1.0 %shard_map.69 = (bf16[384,768]{1,0:T(8,128)(2,1)S(1)}, f32[4,6,32,128]{3,2,1,0:T(8,128)S(1)}) custom-call(bf16[3,128,768]{2,1,0:T(8,128)(2,1)S(1)} %collective-permute-done.x_ref, f32[768]{0:T(1024)S(1)} %copy-done.1, bf16[768,768]{1,0:T(8,128)(2,1)S(1)} %copy-done, bf16[3,256,384]{2,1,0:T(8,128)(2,1)S(1)} %get-tuple-element.33.q_ref, ...), custom_call_target="tpu_custom_call" | custom-call | flops 264241152 | bytes 2362368 | tf_op jit(solution)/shard_map/pallas_call | solution.py:375
  17.7 0.8 %shard_map.70.keep_ref = f32[4,6,32,128]{3,2,1,0:T(8,128)S(1)} custom-call(bf16[384,768]{1,0:T(8,128)(2,1)S(1)} %get-tuple-element.45.rows_ref, bf16[768,768]{1,0:T(8,128)(2,1)S(1)} %copy-done, bf16[3,256,384]{2,1,0:T(8,128)(2,1)S(1)} %get-tuple-element.46.q_ref, f32[4,6,32,128]{3,2,1,0:T(8,128)S(1)} %get-tuple-element.47.after_ref), custom_call_target="tpu_custom_call" | custom-call | flops 264241152 | bytes 2359296 | tf_op jit(solution)/shard_map/pallas_call | solution.py:375
  18.4 0.9 %collective-permute-done.5.got_ref = f32[4,6,32,128]{3,2,1,0:T(8,128)S(1)} collective-permute-done((f32[4,6,32,128]{3,2,1,0:T(8,128)S(1)}, f32[4,6,32,128]{3,2,1,0:T(8,128)S(1)}, u32[]{:S(2)}, u32[]{:S(2)}) %collective-permute-start.5) | collective-permute-done | bytes 393248 | tf_op jit(solution)/shard_map/ppermute | solution.py:409
  19.5 2.8 %collective-permute-start.6 = (bf16[6,32,128]{2,1,0:T(8,128)(2,1)S(1)}, bf16[6,32,128]{2,1,0:T(8,128)(2,1)S(1)}, u32[]{:S(2)}, u32[]{:S(2)}) collective-permute-start(bf16[6,32,128]{2,1,0:T(8,128)(2,1)S(1)} %get-tuple-element.50), channel_id=1, source_target_pairs={{0,12},{2,14},{4,8},{6,10},{8,4},{10,6},{12,0},{14,2},{16,28},{18,... | collective-permute-start | bytes 147464 | tf_op jit(solution)/shard_map/ppermute | solution.py:409
  23.1 2.8 %collective-permute-start.10 = (bf16[6,32,128]{2,1,0:T(8,128)(2,1)S(1)}, bf16[6,32,128]{2,1,0:T(8,128)(2,1)S(1)}, u32[]{:S(2)}, u32[]{:S(2)}) collective-permute-start(bf16[6,32,128]{2,1,0:T(8,128)(2,1)S(1)} %get-tuple-element.56), channel_id=1, source_target_pairs={{0,16},{2,18},{4,20},{6,22},{8,24},{10,26},{12,28},{14,30},{16,0},... | collective-permute-start | bytes 147464 | tf_op jit(solution)/shard_map/ppermute | solution.py:409
  27.2 1.3 %collective-permute-done.10.other_ref = bf16[6,32,128]{2,1,0:T(8,128)(2,1)S(1)} collective-permute-done((bf16[6,32,128]{2,1,0:T(8,128)(2,1)S(1)}, bf16[6,32,128]{2,1,0:T(8,128)(2,1)S(1)}, u32[]{:S(2)}, u32[]{:S(2)}) %collective-permute-start.10) | collective-permute-done | bytes 49184 | tf_op jit(solution)/shard_map/ppermute | solution.py:409
  28.9 1.2 %collective-permute-done.14.got_ref = bf16[6,32,128]{2,1,0:T(8,128)(2,1)S(1)} collective-permute-done((bf16[6,32,128]{2,1,0:T(8,128)(2,1)S(1)}, bf16[6,32,128]{2,1,0:T(8,128)(2,1)S(1)}, u32[]{:S(2)}, u32[]{:S(2)}) %collective-permute-start.14) | collective-permute-done | bytes 49184 | tf_op jit(solution)/shard_map/ppermute | solution.py:409
  30.1 1.6 %collective-permute-start.15 = (bf16[2,6,32,128]{3,2,1,0:T(8,128)(2,1)S(1)}, bf16[2,6,32,128]{3,2,1,0:T(8,128)(2,1)S(1)}, u32[]{:S(2)}, u32[]{:S(2)}) collective-permute-start(bf16[2,6,32,128]{3,2,1,0:T(8,128)(2,1)S(1)} %shard_map.76.share_ref), channel_id=1, source_target_pairs={{0,4},{2,10},{4,0},{6,14},{8,12},{10,2},{12,8},{14,6},{16,20},{18,... | collective-permute-start | bytes 294920 | tf_op jit(solution)/shard_map/ppermute | solution.py:509
  31.7 2.3 %collective-permute-start.9 = (bf16[6,32,128]{2,1,0:T(8,128)(2,1)S(1)}, bf16[6,32,128]{2,1,0:T(8,128)(2,1)S(1)}, u32[]{:S(2)}, u32[]{:S(2)}) collective-permute-start(bf16[6,32,128]{2,1,0:T(8,128)(2,1)S(1)} %get-tuple-element.55), channel_id=1, source_target_pairs={{0,16},{2,18},{4,20},{6,22},{8,24},{10,26},{12,28},{14,30},{16,0},... | collective-permute-start | bytes 147464 | tf_op jit(solution)/shard_map/ppermute | solution.py:409
  34.0 1.9 %collective-permute-start.16 = (bf16[6,32,128]{2,1,0:T(8,128)(2,1)S(1)}, bf16[6,32,128]{2,1,0:T(8,128)(2,1)S(1)}, u32[]{:S(2)}, u32[]{:S(2)}) collective-permute-start(bf16[6,32,128]{2,1,0:T(8,128)(2,1)S(1)} %get-tuple-element.59.mine_ref), channel_id=1, source_target_pairs={{0,12},{2,14},{4,8},{6,10},{8,4},{10,6},{12,0},{14,2},{16,28},{18,... | collective-permute-start | bytes 147464 | tf_op jit(solution)/shard_map/ppermute | solution.py:409
  35.9 1.1 %collective-permute-done.9.refs_1_ = bf16[6,32,128]{2,1,0:T(8,128)(2,1)S(1)} collective-permute-done((bf16[6,32,128]{2,1,0:T(8,128)(2,1)S(1)}, bf16[6,32,128]{2,1,0:T(8,128)(2,1)S(1)}, u32[]{:S(2)}, u32[]{:S(2)}) %collective-permute-start.9) | collective-permute-done | bytes 49184 | tf_op jit(solution)/shard_map/ppermute | solution.py:409
  37.4 1.6 %collective-permute-done.16.refs_1_ = bf16[6,32,128]{2,1,0:T(8,128)(2,1)S(1)} collective-permute-done((bf16[6,32,128]{2,1,0:T(8,128)(2,1)S(1)}, bf16[6,32,128]{2,1,0:T(8,128)(2,1)S(1)}, u32[]{:S(2)}, u32[]{:S(2)}) %collective-permute-start.16) | collective-permute-done | bytes 49184 | tf_op jit(solution)/shard_map/ppermute | solution.py:409
  39.1 2.0 %collective-permute-start.13 = (bf16[7,32,128]{2,1,0:T(8,128)(2,1)S(1)}, bf16[7,32,128]{2,1,0:T(8,128)(2,1)S(1)}, u32[]{:S(2)}, u32[]{:S(2)}) collective-permute-start(bf16[7,32,128]{2,1,0:T(8,128)(2,1)S(1)} %shard_map.75.refs_2_.refs_0_), channel_id=1, source_target_pairs={{0,8},{2,10},{4,12},{6,14},{8,0},{10,2},{12,4},{14,6},{16,24},{18,... | collective-permute-start | bytes 172040 | tf_op jit(solution)/shard_map/ppermute | solution.py:409
  41.6 1.0 %collective-permute-start.11 = (bf16[7,32,128]{2,1,0:T(8,128)(2,1)S(1)}, bf16[7,32,128]{2,1,0:T(8,128)(2,1)S(1)}, u32[]{:S(2)}, u32[]{:S(2)}) collective-permute-start(bf16[7,32,128]{2,1,0:T(8,128)(2,1)S(1)} %shard_map.75.refs_2_.refs_0_), channel_id=1, source_target_pairs={{0,12},{2,14},{4,8},{6,10},{8,4},{10,6},{12,0},{14,2},{16,28},{18,... | collective-permute-start | bytes 172040 | tf_op jit(solution)/shard_map/ppermute | solution.py:409
  43.6 2.3 %collective-permute-done.12.refs_2_ = bf16[7,32,128]{2,1,0:T(8,128)(2,1)S(1)} collective-permute-done((bf16[7,32,128]{2,1,0:T(8,128)(2,1)S(1)}, bf16[7,32,128]{2,1,0:T(8,128)(2,1)S(1)}, u32[]{:S(2)}, u32[]{:S(2)}) %collective-permute-start.12) | collective-permute-done | bytes 57376 | tf_op jit(solution)/shard_map/ppermute | solution.py:409
  45.9 0.8 %collective-permute-done.11.refs_1_ = bf16[7,32,128]{2,1,0:T(8,128)(2,1)S(1)} collective-permute-done((bf16[7,32,128]{2,1,0:T(8,128)(2,1)S(1)}, bf16[7,32,128]{2,1,0:T(8,128)(2,1)S(1)}, u32[]{:S(2)}, u32[]{:S(2)}) %collective-permute-start.11) | collective-permute-done | bytes 57376 | tf_op jit(solution)/shard_map/ppermute | solution.py:409
  48.3 1.5 %shard_map.81 = bf16[3,128,768]{2,1,0:T(8,128)(2,1)} custom-call(bf16[4,7,32,128]{3,2,1,0:T(8,128)(2,1)S(1)} %collective-permute-done.18.p_ref, bf16[6,128,384]{2,1,0:T(8,128)(2,1)S(1)} %shard_map.72.refs_3_.refs_0_, f32[6,128,384]{2,1,0:T(8,128)S(1)} %shard_map.78.refs_4_.refs_1_, f32[384,768]{1,0:T(8,128)S(1)} %shard_map.80.refs_2_, ...), custom_call_target="tpu_custom_call" | custom-call | flops 301989888 | bytes 4358144 | tf_op jit(solution)/shard_map/pallas_call | solution.py:375
  (36 shorter events, 8.8 us)
Async XLA Ops:
  0.0 16.5 %collective-permute-start = (bf16[3,128,768]{2,1,0:T(8,128)(2,1)}, bf16[3,128,768]{2,1,0:T(8,128)(2,1)S(1)}, u32[]{:S(2)}, u32[]{:S(2)}) collective-permute-start(bf16[3,128,768]{2,1,0:T(8,128)(2,1)} %x_hbm.1), channel_id=1, source_target_pairs={{0,1},{1,0},{2,3},{3,2},{4,5},{5,4},{6,7},{7,6},{8,9},{9,8},{10,11... | collective-permute-start | bytes 1769480 | tf_op jit(solution)/shard_map/ppermute | solution.py:423
  5.8 1.8 %collective-permute-start.1 = (f32[4,6,32,128]{3,2,1,0:T(8,128)S(1)}, f32[4,6,32,128]{3,2,1,0:T(8,128)S(1)}, u32[]{:S(2)}, u32[]{:S(2)}) collective-permute-start(f32[4,6,32,128]{3,2,1,0:T(8,128)S(1)} %get-tuple-element.37.after_ref), channel_id=1, source_target_pairs={{0,2},{2,0},{4,6},{6,4},{8,10},{10,8},{12,14},{14,12},{16,18},{18,... | collective-permute-start | bytes 1179656 | tf_op jit(solution)/shard_map/ppermute | solution.py:409
  7.8 5.6 %collective-permute-start.2 = (bf16[6,32,128]{2,1,0:T(8,128)(2,1)S(1)}, bf16[6,32,128]{2,1,0:T(8,128)(2,1)S(1)}, u32[]{:S(2)}, u32[]{:S(2)}) collective-permute-start(bf16[6,32,128]{2,1,0:T(8,128)(2,1)S(1)} %get-tuple-element.40), channel_id=1, source_target_pairs={{0,12},{2,14},{4,8},{6,10},{8,4},{10,6},{12,0},{14,2},{16,28},{18,... | collective-permute-start | bytes 147464 | tf_op jit(solution)/shard_map/ppermute | solution.py:409
  10.4 4.1 %collective-permute-start.3 = (bf16[6,32,128]{2,1,0:T(8,128)(2,1)S(1)}, bf16[6,32,128]{2,1,0:T(8,128)(2,1)S(1)}, u32[]{:S(2)}, u32[]{:S(2)}) collective-permute-start(bf16[6,32,128]{2,1,0:T(8,128)(2,1)S(1)} %get-tuple-element.41), channel_id=1, source_target_pairs={{0,4},{2,6},{4,0},{6,2},{8,12},{10,14},{12,8},{14,10},{16,20},{18,... | collective-permute-start | bytes 147464 | tf_op jit(solution)/shard_map/ppermute | solution.py:409
  10.9 4.1 %collective-permute-start.4 = (bf16[6,32,128]{2,1,0:T(8,128)(2,1)S(1)}, bf16[6,32,128]{2,1,0:T(8,128)(2,1)S(1)}, u32[]{:S(2)}, u32[]{:S(2)}) collective-permute-start(bf16[6,32,128]{2,1,0:T(8,128)(2,1)S(1)} %get-tuple-element.42), channel_id=1, source_target_pairs={{0,8},{2,10},{4,12},{6,14},{8,0},{10,2},{12,4},{14,6},{16,24},{18,... | collective-permute-start | bytes 147464 | tf_op jit(solution)/shard_map/ppermute | solution.py:409
  11.3 5.2 %copy-start = (bf16[768,768]{1,0:T(8,128)(2,1)S(1)}, bf16[768,768]{1,0:T(8,128)(2,1)}, u32[]{:S(2)}) copy-start(bf16[768,768]{1,0:T(8,128)(2,1)} %wk_ref.3) | copy-start | bytes 3538948
  11.3 5.2 %copy-start.1 = (f32[768]{0:T(1024)S(1)}, f32[768]{0:T(1024)}, u32[]{:S(2)}) copy-start(f32[768]{0:T(1024)} %gain_ref.1) | copy-start | bytes 9220
  17.6 1.8 %collective-permute-start.5 = (f32[4,6,32,128]{3,2,1,0:T(8,128)S(1)}, f32[4,6,32,128]{3,2,1,0:T(8,128)S(1)}, u32[]{:S(2)}, u32[]{:S(2)}) collective-permute-start(f32[4,6,32,128]{3,2,1,0:T(8,128)S(1)} %get-tuple-element.47.after_ref), channel_id=1, source_target_pairs={{0,2},{2,0},{4,6},{6,4},{8,10},{10,8},{12,14},{14,12},{16,18},{18,... | collective-permute-start | bytes 1179656 | tf_op jit(solution)/shard_map/ppermute | solution.py:409
  19.5 7.0 %collective-permute-start.6 = (bf16[6,32,128]{2,1,0:T(8,128)(2,1)S(1)}, bf16[6,32,128]{2,1,0:T(8,128)(2,1)S(1)}, u32[]{:S(2)}, u32[]{:S(2)}) collective-permute-start(bf16[6,32,128]{2,1,0:T(8,128)(2,1)S(1)} %get-tuple-element.50), channel_id=1, source_target_pairs={{0,12},{2,14},{4,8},{6,10},{8,4},{10,6},{12,0},{14,2},{16,28},{18,... | collective-permute-start | bytes 147464 | tf_op jit(solution)/shard_map/ppermute | solution.py:409
  22.3 4.2 %collective-permute-start.7 = (bf16[6,32,128]{2,1,0:T(8,128)(2,1)S(1)}, bf16[6,32,128]{2,1,0:T(8,128)(2,1)S(1)}, u32[]{:S(2)}, u32[]{:S(2)}) collective-permute-start(bf16[6,32,128]{2,1,0:T(8,128)(2,1)S(1)} %get-tuple-element.51), channel_id=1, source_target_pairs={{0,4},{2,6},{4,0},{6,2},{8,12},{10,14},{12,8},{14,10},{16,20},{18,... | collective-permute-start | bytes 147464 | tf_op jit(solution)/shard_map/ppermute | solution.py:409
  22.8 4.2 %collective-permute-start.8 = (bf16[6,32,128]{2,1,0:T(8,128)(2,1)S(1)}, bf16[6,32,128]{2,1,0:T(8,128)(2,1)S(1)}, u32[]{:S(2)}, u32[]{:S(2)}) collective-permute-start(bf16[6,32,128]{2,1,0:T(8,128)(2,1)S(1)} %get-tuple-element.52), channel_id=1, source_target_pairs={{0,8},{2,10},{4,12},{6,14},{8,0},{10,2},{12,4},{14,6},{16,24},{18,... | collective-permute-start | bytes 147464 | tf_op jit(solution)/shard_map/ppermute | solution.py:409
  23.1 5.5 %collective-permute-start.10 = (bf16[6,32,128]{2,1,0:T(8,128)(2,1)S(1)}, bf16[6,32,128]{2,1,0:T(8,128)(2,1)S(1)}, u32[]{:S(2)}, u32[]{:S(2)}) collective-permute-start(bf16[6,32,128]{2,1,0:T(8,128)(2,1)S(1)} %get-tuple-element.56), channel_id=1, source_target_pairs={{0,16},{2,18},{4,20},{6,22},{8,24},{10,26},{12,28},{14,30},{16,0},... | collective-permute-start | bytes 147464 | tf_op jit(solution)/shard_map/ppermute | solution.py:409
  28.8 1.3 %collective-permute-start.14 = (bf16[6,32,128]{2,1,0:T(8,128)(2,1)S(1)}, bf16[6,32,128]{2,1,0:T(8,128)(2,1)S(1)}, u32[]{:S(2)}, u32[]{:S(2)}) collective-permute-start(bf16[6,32,128]{2,1,0:T(8,128)(2,1)S(1)} %get-tuple-element.59.mine_ref), channel_id=1, source_target_pairs={{0,2},{2,0},{4,6},{6,4},{8,10},{10,8},{12,14},{14,12},{16,18},{18,... | collective-permute-start | bytes 147464 | tf_op jit(solution)/shard_map/ppermute | solution.py:409
  30.1 8.9 %collective-permute-start.15 = (bf16[2,6,32,128]{3,2,1,0:T(8,128)(2,1)S(1)}, bf16[2,6,32,128]{3,2,1,0:T(8,128)(2,1)S(1)}, u32[]{:S(2)}, u32[]{:S(2)}) collective-permute-start(bf16[2,6,32,128]{3,2,1,0:T(8,128)(2,1)S(1)} %shard_map.76.share_ref), channel_id=1, source_target_pairs={{0,4},{2,10},{4,0},{6,14},{8,12},{10,2},{12,8},{14,6},{16,20},{18,... | collective-permute-start | bytes 294920 | tf_op jit(solution)/shard_map/ppermute | solution.py:509
  31.7 5.3 %collective-permute-start.9 = (bf16[6,32,128]{2,1,0:T(8,128)(2,1)S(1)}, bf16[6,32,128]{2,1,0:T(8,128)(2,1)S(1)}, u32[]{:S(2)}, u32[]{:S(2)}) collective-permute-start(bf16[6,32,128]{2,1,0:T(8,128)(2,1)S(1)} %get-tuple-element.55), channel_id=1, source_target_pairs={{0,16},{2,18},{4,20},{6,22},{8,24},{10,26},{12,28},{14,30},{16,0},... | collective-permute-start | bytes 147464 | tf_op jit(solution)/shard_map/ppermute | solution.py:409
  34.0 5.0 %collective-permute-start.16 = (bf16[6,32,128]{2,1,0:T(8,128)(2,1)S(1)}, bf16[6,32,128]{2,1,0:T(8,128)(2,1)S(1)}, u32[]{:S(2)}, u32[]{:S(2)}) collective-permute-start(bf16[6,32,128]{2,1,0:T(8,128)(2,1)S(1)} %get-tuple-element.59.mine_ref), channel_id=1, source_target_pairs={{0,12},{2,14},{4,8},{6,10},{8,4},{10,6},{12,0},{14,2},{16,28},{18,... | collective-permute-start | bytes 147464 | tf_op jit(solution)/shard_map/ppermute | solution.py:409
  39.0 3.6 %collective-permute-start.17 = (bf16[3,6,32,128]{3,2,1,0:T(8,128)(2,1)S(1)}, bf16[3,6,32,128]{3,2,1,0:T(8,128)(2,1)S(1)}, u32[]{:S(2)}, u32[]{:S(2)}) collective-permute-start(bf16[3,6,32,128]{3,2,1,0:T(8,128)(2,1)S(1)} %shard_map.77), channel_id=1, source_target_pairs={{0,2},{2,0},{4,6},{6,4},{8,10},{10,8},{12,14},{14,12},{16,18},{18,... | collective-permute-start | bytes 442376 | tf_op jit(solution)/shard_map/ppermute | solution.py:409
  39.1 4.5 %collective-permute-start.13 = (bf16[7,32,128]{2,1,0:T(8,128)(2,1)S(1)}, bf16[7,32,128]{2,1,0:T(8,128)(2,1)S(1)}, u32[]{:S(2)}, u32[]{:S(2)}) collective-permute-start(bf16[7,32,128]{2,1,0:T(8,128)(2,1)S(1)} %shard_map.75.refs_2_.refs_0_), channel_id=1, source_target_pairs={{0,8},{2,10},{4,12},{6,14},{8,0},{10,2},{12,4},{14,6},{16,24},{18,... | collective-permute-start | bytes 172040 | tf_op jit(solution)/shard_map/ppermute | solution.py:409
  41.1 4.8 %collective-permute-start.12 = (bf16[7,32,128]{2,1,0:T(8,128)(2,1)S(1)}, bf16[7,32,128]{2,1,0:T(8,128)(2,1)S(1)}, u32[]{:S(2)}, u32[]{:S(2)}) collective-permute-start(bf16[7,32,128]{2,1,0:T(8,128)(2,1)S(1)} %shard_map.75.refs_2_.refs_0_), channel_id=1, source_target_pairs={{0,4},{2,6},{4,0},{6,2},{8,12},{10,14},{12,8},{14,10},{16,20},{18,... | collective-permute-start | bytes 172040 | tf_op jit(solution)/shard_map/ppermute | solution.py:409
  41.6 5.1 %collective-permute-start.11 = (bf16[7,32,128]{2,1,0:T(8,128)(2,1)S(1)}, bf16[7,32,128]{2,1,0:T(8,128)(2,1)S(1)}, u32[]{:S(2)}, u32[]{:S(2)}) collective-permute-start(bf16[7,32,128]{2,1,0:T(8,128)(2,1)S(1)} %shard_map.75.refs_2_.refs_0_), channel_id=1, source_target_pairs={{0,12},{2,14},{4,8},{6,10},{8,4},{10,6},{12,0},{14,2},{16,28},{18,... | collective-permute-start | bytes 172040 | tf_op jit(solution)/shard_map/ppermute | solution.py:409
  46.7 1.6 %collective-permute-start.18 = (bf16[4,7,32,128]{3,2,1,0:T(8,128)(2,1)S(1)}, bf16[4,7,32,128]{3,2,1,0:T(8,128)(2,1)S(1)}, u32[]{:S(2)}, u32[]{:S(2)}) collective-permute-start(bf16[4,7,32,128]{3,2,1,0:T(8,128)(2,1)S(1)} %shard_map.79.p_ref), channel_id=1, source_target_pairs={{0,2},{2,0},{4,6},{6,4},{8,10},{10,8},{12,14},{14,12},{16,18},{18,... | collective-permute-start | bytes 688136 | tf_op jit(solution)/shard_map/ppermute | solution.py:409

commit v5 on v4

--- a/solution.py
+++ b/solution.py
@@ -11,8 +11,9 @@
 LANES = 128
 CORES = 2
 
-UNIT = 0.5
 CODED = 80.0
+SPREAD = 32.0
+LEAST_UNIT = 0.375
 
 
 VMEM = pl.BlockSpec(memory_space=pltpu.VMEM)
@@ -162,6 +163,30 @@
     return jnp.where(jnp.abs(u) < CODED, near, far).astype(jnp.bfloat16)
 
 
+def reference_of(v):
+    top = jnp.max(v, axis=-1, keepdims=True)
+    spread = top - jnp.min(v, axis=-1, keepdims=True)
+    unit = jnp.maximum(spread * (1.0 / SPREAD), LEAST_UNIT)
+    return top, unit.astype(jnp.bfloat16).astype(jnp.float32)
+
+
+def write_with_units(out_ref, v, unit):
+    heads, share, cols = v.shape
+    out_ref[:heads] = encode(v * (1.0 / unit))
+    lane = lax.broadcasted_iota(jnp.int32, (share, cols), 1)
+    packed = jnp.zeros((share, cols), jnp.float32)
+    for h in range(heads):
+        packed = jnp.where(lane == h, unit[h], packed)
+    out_ref[heads] = packed.astype(out_ref.dtype)
+
+
+def write_units(part_ref, unit_ref):
+    heads, share, cols = unit_ref.shape
+    packed = part_ref[heads].astype(jnp.float32)
+    for h in range(heads):
+        unit_ref[h] = jnp.broadcast_to(packed[:, h : h + 1], (share, cols))
+
+
 def decode(y):
     y = y.astype(jnp.float32)
     near = jnp.log(jnp.abs(y))
@@ -173,39 +198,59 @@
     return sorted(range(inner), key=lambda k: (k > 0, -k.bit_count(), k))
 
 
-def merge_kernel(factor, keep_ref, got_ref, *refs):
+def own_merge_kernel(scale, keep_ref, got_ref, *refs):
     inner = keep_ref.shape[0]
-    if refs[-1].shape == keep_ref.shape:
-        outs, top_out, top_ref = refs[:-1], refs[-1], None
-    else:
-        outs, top_out, top_ref = refs[1:], None, refs[0]
+    outs, top_ref, inverse_ref = refs[:inner], refs[inner], refs[inner + 1]
     _, chip = spot(inner)
     for k, out_ref in zip(steps(inner), outs):
         b = chip ^ k
-        u = (keep_ref[b] + got_ref[b]) * factor
-        if top_out is None:
-            top = top_ref[b]
+        v = (keep_ref[b] + got_ref[b]) * scale
+        top, unit = reference_of(v)
+        top_ref[b] = jnp.broadcast_to(top, v.shape)
+        inverse_ref[b] = jnp.broadcast_to(1.0 / unit, v.shape)
+        if k:
+            write_with_units(out_ref, v - top, unit)
         else:
-            top = jnp.broadcast_to(jnp.max(u, axis=-1, keepdims=True), u.shape)
-            top_out[b] = top
-        u = u - top
-        out_ref[...] = encode(u) if k else u
+            out_ref[...] = v - top
+
+
+def merge_kernel(scale, keep_ref, got_ref, top_ref, inverse_ref, *outs):
+    inner = keep_ref.shape[0]
+    _, chip = spot(inner)
+    for k, out_ref in zip(steps(inner), outs):
+        b = chip ^ k
+        v = (keep_ref[b] + got_ref[b]) * scale - top_ref[b]
+        out_ref[...] = encode(v * inverse_ref[b]) if k else v
+
+
+def own_sum_kernel(n, own_ref, *refs):
+    parts, outs = refs[: n - 1], refs[-(n + 3) :]
+    total_ref, sent_ref, top_ref, inverse_ref, *unit_refs = outs
+    total = own_ref[...]
+    for part_ref, unit_ref in zip(parts, unit_refs):
+        write_units(part_ref, unit_ref)
+        total = total + unit_ref[...] * decode(part_ref[: total.shape[0]])
+    top, unit = reference_of(total)
+    total = total - top
+    total_ref[...] = total
+    write_with_units(sent_ref, total, unit)
+    top_ref[...] = jnp.broadcast_to(top, total.shape)
+    inverse_ref[...] = jnp.broadcast_to(1.0 / unit, total.shape)
 
 
 def sum_kernel(n, own_ref, *refs):
-    total = own_ref[...]
-    for part in refs[: n - 1]:
-        total = total + decode(part[...])
-    refs[-2][...] = total
-    refs[-1][...] = encode(total * 0.5)
-
-
-def logits_of(mine_ref, other_ref):
-    return (mine_ref[...] + 2.0 * decode(other_ref[...])) * UNIT
-
-
-def own_softmax_kernel(mine_ref, other_ref, after_ref, p_ref, top_ref, sum_ref):
-    logits = logits_of(mine_ref, other_ref)
+    parts, (top_ref, inverse_ref, *unit_refs) = refs[: n - 1], refs[n - 1 : 2 * n]
+    total_ref, sent_ref = refs[-2:]
+    total = own_ref[...] - top_ref[...]
+    for part_ref, unit_ref in zip(parts, unit_refs):
+        total = total + unit_ref[...] * decode(part_ref[...])
+    total_ref[...] = total
+    sent_ref[...] = encode(total * inverse_ref[...])
+
+
+def own_softmax_kernel(mine_ref, other_ref, after_ref, p_ref, top_ref, sum_ref, unit_ref):
+    write_units(other_ref, unit_ref)
+    logits = mine_ref[...] + unit_ref[...] * decode(other_ref[: mine_ref.shape[0]])
     top = jnp.max(logits, axis=-1, keepdims=True)
     p = jnp.exp(logits - top)
     p_ref[...] = p.astype(p_ref.dtype)
@@ -214,16 +259,20 @@
 
 
 def softmax_kernel(n, *refs):
-    mine, other, (own_top_ref, own_sum_ref, out_ref) = refs[:n], refs[n : 2 * n], refs[2 * n :]
-    logits = jnp.concatenate([logits_of(a, b) for a, b in zip(mine, other)], axis=-1)
+    mine, other = refs[:n], refs[n : 2 * n]
+    own_top_ref, own_sum_ref, unit_ref, out_ref = refs[2 * n :]
+    logits = jnp.concatenate(
+        [a[...] + unit_ref[...] * decode(b[...]) for a, b in zip(mine, other)], axis=-1
+    )
     heads, share, cols = logits.shape
     own_top = own_top_ref[...][..., :1]
     top = jnp.maximum(own_top, jnp.max(logits, axis=-1, keepdims=True))
     p = jnp.exp(logits - top)
     factor = jnp.exp(own_top - top)
     total = own_sum_ref[...][..., :1] * factor + jnp.sum(p, axis=-1, keepdims=True)
-    out_ref[:heads] = (p / total).astype(out_ref.dtype)
-    factor = factor / total
+    share_of = 1.0 / total
+    out_ref[:heads] = (p * share_of).astype(out_ref.dtype)
+    factor = factor * share_of
     high = factor.astype(out_ref.dtype).astype(jnp.float32)
     low = factor - high
     lane = lax.broadcasted_iota(jnp.int32, (share, cols), 1)
@@ -410,14 +459,10 @@
 
     coded = shape((heads, share, r), bf16)
     scale = float(hsize * s * n_seq) ** -0.5
-    merge = functools.partial(merge_kernel, scale / UNIT)
-
-    def reduce(own, *sent, order=()):
-        parts = [hop(y, CORES * k) for k, y in zip(steps(inner)[1:], sent)]
-        total, half = call(
-            functools.partial(sum_kernel, inner), (piece, coded), (own, *parts), order=order
-        )
-        return total, hop(half, CORES * inner)
+    united = shape((heads + 1, share, r), bf16)
+
+    def quad(sent):
+        return [hop(y, CORES * k) for k, y in zip(steps(inner)[1:], sent)]
 
     others = [
         lax.ppermute(x, "res", [(i, (i + k) % n_res) for i in range(n_res)])
@@ -448,7 +493,11 @@
         scratch=[keys],
         flops=dots * (d + r // 2),
     )
-    *pieces, top = call(merge, (piece, *[coded] * (inner - 1), part), (keep, got))
+    *pieces, top, inverse = call(
+        functools.partial(own_merge_kernel, scale),
+        (piece, *[united] * (inner - 1), part, part),
+        (keep, got),
+    )
     value, wv, wf = call(
         own_value_kernel,
         (grouped, shape(wv.shape, bf16), shape(wf.shape, bf16)),
@@ -459,7 +508,13 @@
         flops=dots * d,
     )
     values = [value]
-    reduced = [reduce(*pieces, order=values)]
+    total, half, *known = call(
+        functools.partial(own_sum_kernel, inner),
+        (piece, united, *[piece] * (inner + 1)),
+        (pieces[0], *quad(pieces[1:])),
+        order=values,
+    )
+    reduced = [(total, hop(half, CORES * inner))]
     for other in others:
         rows, send = call(
             send_kernel,
@@ -478,9 +533,19 @@
             scratch=[keys],
             flops=dots * (d // 2 + r // 2),
         )
-        pieces = call(merge, (piece, *[coded] * (inner - 1)), (keep, got, top))
+        pieces = call(
+            functools.partial(merge_kernel, scale),
+            (piece, *[coded] * (inner - 1)),
+            (keep, got, top, inverse),
+        )
         values.append(call(value_kernel, grouped, (rows, wv), order=pieces[:1], flops=dots * d))
-        reduced.append(reduce(*pieces, order=values[-1:]))
+        total, half = call(
+            functools.partial(sum_kernel, inner),
+            (piece, coded),
+            (pieces[0], *quad(pieces[1:]), *known),
+            order=values[-1:],
+        )
+        reduced.append((total, hop(half, CORES * inner)))
 
     def gather(y, order=()):
         mine = [y] + [hop(y, CORES * k) for k in steps(inner)[1:]]
@@ -489,16 +554,16 @@
         )
         return mine, hop(mine, 1)
 
-    own_probs, own_top, own_sum = call(
+    own_probs, own_top, own_sum, own_unit = call(
         own_softmax_kernel,
-        (shape(piece.shape, bf16), piece, piece),
+        (shape(piece.shape, bf16), piece, piece, piece),
         reduced[0],
         order=(reduced[-1][0],),
     )
     probs = call(
         functools.partial(softmax_kernel, n_res - 1),
         shape((heads + 1, share, cols - r), bf16),
-        (*(a for a, _ in reduced[1:]), *(b for _, b in reduced[1:]), own_top, own_sum),
+        (*(a for a, _ in reduced[1:]), *(b for _, b in reduced[1:]), own_top, own_sum, own_unit),
     )
     mate = hop(own_probs, 1)
     far = hop(own_probs, CORES * (inner - 1))

time: 50 us -> 47.9 us (0.958)
  starting transfers between devices: 22.6 us -> 20.2 us
    ppermute x17, starting transfers between devices: 18 us -> 15.7 us  [hop(): return lax.ppermute(y, 'seq', [(i, i ^ k) for i in range(n_seq)])]
  transfers between devices with their start and end apart: 19 -> 19, of which waited for: 14 -> 13; matrix products, arithmetic and copies ran while one was open for 0% -> 0% of each run, Pallas kernels for 19% -> 20%
where the time goes in v5:
time: 47.9 us; the launch traced here: 47.8 us
  starting transfers between devices  20.2 us (42%)
  waiting for transfers between devices  14.8 us (31%)
  Pallas kernels  12.6 us (26%)
    ppermute x17, starting transfers between devices, hop(): return lax.ppermute(y, 'seq', [(i, i ^ k) for i in range(n_seq)])  15.7 us
    ppermute x17, waiting for transfers between devices, hop(): return lax.ppermute(y, 'seq', [(i, i ^ k) for i in range(n_seq)])  13.7 us
    pallas_call x18, Pallas kernels, call(): pl.pallas_call(kernel, out_shape=out_shape, in_specs=specs, out_specs=jax...  12.6 us
    ppermute x1, starting transfers between devices, body(): lax.ppermute(x, 'res', [(i, (i + k) % n_res) for i in range(n_res)])  3 us
    ppermute x1, starting transfers between devices, body(): came.append(lax.ppermute(both, 'seq', pairs))  1.56 us
    ppermute x1, waiting for transfers between devices, body(): lax.ppermute(x, 'res', [(i, (i + k) % n_res) for i in range(n_res)])  1.03 us
  transfers between devices with their start and end apart: 19, of which 13 were waited for; matrix products, arithmetic and copies ran while one was open for 0% of the time, Pallas kernels for 20%

profile of v5, /device:TPU:0, one launch (start us, length us, event | category | flops | bytes accessed | tf_op | source)
XLA Modules:
  0.0 47.8 jit_solution(2060280149953037159)
XLA Ops:
  0.0 3.0 %collective-permute-start = (bf16[3,128,768]{2,1,0:T(8,128)(2,1)}, bf16[3,128,768]{2,1,0:T(8,128)(2,1)S(1)}, u32[]{:S(2)}, u32[]{:S(2)}) collective-permute-start(bf16[3,128,768]{2,1,0:T(8,128)(2,1)} %x_hbm.1), channel_id=1, source_target_pairs={{0,1},{1,0},{2,3},{3,2},{4,5},{5,4},{6,7},{7,6},{8,9},{9,8},{10,11... | collective-permute-start | bytes 1769480 | tf_op jit(solution)/shard_map/ppermute | solution.py:468
  3.0 2.8 %shard_map.64 = (bf16[384,768]{1,0:T(8,128)(2,1)S(1)}, bf16[3,256,384]{2,1,0:T(8,128)(2,1)S(1)}, f32[4,6,32,128]{3,2,1,0:T(8,128)S(1)}, bf16[768,384]{1,0:T(8,128)(2,1)S(1)}, bf16[768,384]{1,0:T(8,128)(2,1)S(1)}) custom-call(bf16[3,128,768]{2,1,0:T(8,128)(2,1)} %x_hbm.1, f32[768]{0:T(1024)} %gain_ref.1, bf16[768,768]{1,0:T(8,128)(2,1)} %wk_ref.3, ...), custom_call_target="tpu_custom_call" | custom-call | flops 490733568 | tf_op jit(solution)/shard_map/pallas_call | solution.py:424
  5.8 1.0 %shard_map.65 = (bf16[3,256,384]{2,1,0:T(8,128)(2,1)S(1)}, f32[4,6,32,128]{3,2,1,0:T(8,128)S(1)}) custom-call(bf16[384,768]{1,0:T(8,128)(2,1)S(1)} %get-tuple-element.41.rows_ref, bf16[768,384]{1,0:T(8,128)(2,1)S(1)} %get-tuple-element.42.wk_ref, bf16[768,384]{1,0:T(8,128)(2,1)S(1)} %get-tuple-element.43.wq_ref, ...), custom_call_target="tpu_custom_call" | custom-call | flops 490733568 | bytes 1769472 | tf_op jit(solution)/shard_map/pallas_call | solution.py:424
  7.9 2.6 %collective-permute-start.2 = (bf16[7,32,128]{2,1,0:T(8,128)(2,1)S(1)}, bf16[7,32,128]{2,1,0:T(8,128)(2,1)S(1)}, u32[]{:S(2)}, u32[]{:S(2)}) collective-permute-start(bf16[7,32,128]{2,1,0:T(8,128)(2,1)S(1)} %get-tuple-element.47), channel_id=1, source_target_pairs={{0,12},{2,14},{4,8},{6,10},{8,4},{10,6},{12,0},{14,2},{16,28},{18,... | collective-permute-start | bytes 172040 | tf_op jit(solution)/shard_map/ppermute | solution.py:458
  11.5 2.0 %shard_map.67 = (bf16[6,128,384]{2,1,0:T(8,128)(2,1)S(1)}, bf16[768,768]{1,0:T(8,128)(2,1)S(1)}, bf16[768,768]{1,0:T(8,128)(2,1)S(1)}) custom-call(bf16[384,768]{1,0:T(8,128)(2,1)S(1)} %get-tuple-element.41.rows_ref, bf16[768,768]{1,0:T(8,128)(2,1)} %wv_hbm.1, bf16[768,768]{1,0:T(8,128)(2,1)} %wf_hbm.1, f32[6,32,128]{2,1,0:T(8,128)S(1)} %get-tuple-element.46.after_ref.own_ref), custom_call_target="tpu_custom_call" | custom-call | flops 452984832 | bytes 589824 | tf_op jit(solution)/shard_map/pallas_call | solution.py:424
  13.5 1.2 %collective-permute-done.3.refs_1_ = bf16[7,32,128]{2,1,0:T(8,128)(2,1)S(1)} collective-permute-done((bf16[7,32,128]{2,1,0:T(8,128)(2,1)S(1)}, bf16[7,32,128]{2,1,0:T(8,128)(2,1)S(1)}, u32[]{:S(2)}, u32[]{:S(2)}) %collective-permute-start.3) | collective-permute-done | bytes 57376 | tf_op jit(solution)/shard_map/ppermute | solution.py:458
  15.5 1.0 %collective-permute-done.x_ref = bf16[3,128,768]{2,1,0:T(8,128)(2,1)S(1)} collective-permute-done((bf16[3,128,768]{2,1,0:T(8,128)(2,1)}, bf16[3,128,768]{2,1,0:T(8,128)(2,1)S(1)}, u32[]{:S(2)}, u32[]{:S(2)}) %collective-permute-start) | collective-permute-done | bytes 589856 | tf_op jit(solution)/shard_map/ppermute | solution.py:468
  16.5 1.0 %shard_map.69 = (bf16[384,768]{1,0:T(8,128)(2,1)S(1)}, f32[4,6,32,128]{3,2,1,0:T(8,128)S(1)}) custom-call(bf16[3,128,768]{2,1,0:T(8,128)(2,1)S(1)} %collective-permute-done.x_ref, f32[768]{0:T(1024)S(1)} %copy-done.1, bf16[768,768]{1,0:T(8,128)(2,1)S(1)} %copy-done, bf16[3,256,384]{2,1,0:T(8,128)(2,1)S(1)} %get-tuple-element.40.q_ref, ...), custom_call_target="tpu_custom_call" | custom-call | flops 264241152 | bytes 2362368 | tf_op jit(solution)/shard_map/pallas_call | solution.py:424
  17.7 2.9 %collective-permute-start.10 = (bf16[7,32,128]{2,1,0:T(8,128)(2,1)S(1)}, bf16[7,32,128]{2,1,0:T(8,128)(2,1)S(1)}, u32[]{:S(2)}, u32[]{:S(2)}) collective-permute-start(bf16[7,32,128]{2,1,0:T(8,128)(2,1)S(1)} %get-tuple-element.69), channel_id=1, source_target_pairs={{0,16},{2,18},{4,20},{6,22},{8,24},{10,26},{12,28},{14,30},{16,0},... | collective-permute-start | bytes 172040 | tf_op jit(solution)/shard_map/ppermute | solution.py:458
  20.5 0.7 %shard_map.70.keep_ref = f32[4,6,32,128]{3,2,1,0:T(8,128)S(1)} custom-call(bf16[384,768]{1,0:T(8,128)(2,1)S(1)} %get-tuple-element.52.rows_ref, bf16[768,768]{1,0:T(8,128)(2,1)S(1)} %copy-done, bf16[3,256,384]{2,1,0:T(8,128)(2,1)S(1)} %get-tuple-element.53.q_ref, f32[4,6,32,128]{3,2,1,0:T(8,128)S(1)} %get-tuple-element.54.after_ref), custom_call_target="tpu_custom_call" | custom-call | flops 264241152 | bytes 2359296 | tf_op jit(solution)/shard_map/pallas_call | solution.py:424
  21.5 2.6 %collective-permute-start.6 = (bf16[6,32,128]{2,1,0:T(8,128)(2,1)S(1)}, bf16[6,32,128]{2,1,0:T(8,128)(2,1)S(1)}, u32[]{:S(2)}, u32[]{:S(2)}) collective-permute-start(bf16[6,32,128]{2,1,0:T(8,128)(2,1)S(1)} %get-tuple-element.58), channel_id=1, source_target_pairs={{0,12},{2,14},{4,8},{6,10},{8,4},{10,6},{12,0},{14,2},{16,28},{18,... | collective-permute-start | bytes 147464 | tf_op jit(solution)/shard_map/ppermute | solution.py:458
  25.7 0.9 %collective-permute-done.6.refs_0_ = bf16[6,32,128]{2,1,0:T(8,128)(2,1)S(1)} collective-permute-done((bf16[6,32,128]{2,1,0:T(8,128)(2,1)S(1)}, bf16[6,32,128]{2,1,0:T(8,128)(2,1)S(1)}, u32[]{:S(2)}, u32[]{:S(2)}) %collective-permute-start.6) | collective-permute-done | bytes 49184 | tf_op jit(solution)/shard_map/ppermute | solution.py:458
  26.5 1.6 %collective-permute-done.7.refs_1_ = bf16[6,32,128]{2,1,0:T(8,128)(2,1)S(1)} collective-permute-done((bf16[6,32,128]{2,1,0:T(8,128)(2,1)S(1)}, bf16[6,32,128]{2,1,0:T(8,128)(2,1)S(1)}, u32[]{:S(2)}, u32[]{:S(2)}) %collective-permute-start.7) | collective-permute-done | bytes 49184 | tf_op jit(solution)/shard_map/ppermute | solution.py:458
  29.2 1.2 %collective-permute-done.14.got_ref = bf16[6,32,128]{2,1,0:T(8,128)(2,1)S(1)} collective-permute-done((bf16[6,32,128]{2,1,0:T(8,128)(2,1)S(1)}, bf16[6,32,128]{2,1,0:T(8,128)(2,1)S(1)}, u32[]{:S(2)}, u32[]{:S(2)}) %collective-permute-start.14) | collective-permute-done | bytes 49184 | tf_op jit(solution)/shard_map/ppermute | solution.py:458
  30.4 1.6 %collective-permute-start.15 = (bf16[2,6,32,128]{3,2,1,0:T(8,128)(2,1)S(1)}, bf16[2,6,32,128]{3,2,1,0:T(8,128)(2,1)S(1)}, u32[]{:S(2)}, u32[]{:S(2)}) collective-permute-start(bf16[2,6,32,128]{3,2,1,0:T(8,128)(2,1)S(1)} %shard_map.76.share_ref), channel_id=1, source_target_pairs={{0,4},{2,10},{4,0},{6,14},{8,12},{10,2},{12,8},{14,6},{16,20},{18,... | collective-permute-start | bytes 294920 | tf_op jit(solution)/shard_map/ppermute | solution.py:574
  32.0 0.9 %collective-permute-start.9 = (bf16[6,32,128]{2,1,0:T(8,128)(2,1)S(1)}, bf16[6,32,128]{2,1,0:T(8,128)(2,1)S(1)}, u32[]{:S(2)}, u32[]{:S(2)}) collective-permute-start(bf16[6,32,128]{2,1,0:T(8,128)(2,1)S(1)} %get-tuple-element.68), channel_id=1, source_target_pairs={{0,16},{2,18},{4,20},{6,22},{8,24},{10,26},{12,28},{14,30},{16,0},... | collective-permute-start | bytes 147464 | tf_op jit(solution)/shard_map/ppermute | solution.py:458
  32.8 0.9 %collective-permute-start.16 = (bf16[6,32,128]{2,1,0:T(8,128)(2,1)S(1)}, bf16[6,32,128]{2,1,0:T(8,128)(2,1)S(1)}, u32[]{:S(2)}, u32[]{:S(2)}) collective-permute-start(bf16[6,32,128]{2,1,0:T(8,128)(2,1)S(1)} %get-tuple-element.73.mine_ref), channel_id=1, source_target_pairs={{0,12},{2,14},{4,8},{6,10},{8,4},{10,6},{12,0},{14,2},{16,28},{18,... | collective-permute-start | bytes 147464 | tf_op jit(solution)/shard_map/ppermute | solution.py:458
  33.8 3.7 %collective-permute-done.9.refs_1_ = bf16[6,32,128]{2,1,0:T(8,128)(2,1)S(1)} collective-permute-done((bf16[6,32,128]{2,1,0:T(8,128)(2,1)S(1)}, bf16[6,32,128]{2,1,0:T(8,128)(2,1)S(1)}, u32[]{:S(2)}, u32[]{:S(2)}) %collective-permute-start.9) | collective-permute-done | bytes 49184 | tf_op jit(solution)/shard_map/ppermute | solution.py:458
  38.4 1.2 %collective-permute-start.12 = (bf16[7,32,128]{2,1,0:T(8,128)(2,1)S(1)}, bf16[7,32,128]{2,1,0:T(8,128)(2,1)S(1)}, u32[]{:S(2)}, u32[]{:S(2)}) collective-permute-start(bf16[7,32,128]{2,1,0:T(8,128)(2,1)S(1)} %shard_map.75.refs_2_.refs_0_), channel_id=1, source_target_pairs={{0,4},{2,6},{4,0},{6,2},{8,12},{10,14},{12,8},{14,10},{16,20},{18,... | collective-permute-start | bytes 172040 | tf_op jit(solution)/shard_map/ppermute | solution.py:458
  39.6 2.3 %collective-permute-start.11 = (bf16[7,32,128]{2,1,0:T(8,128)(2,1)S(1)}, bf16[7,32,128]{2,1,0:T(8,128)(2,1)S(1)}, u32[]{:S(2)}, u32[]{:S(2)}) collective-permute-start(bf16[7,32,128]{2,1,0:T(8,128)(2,1)S(1)} %shard_map.75.refs_2_.refs_0_), channel_id=1, source_target_pairs={{0,12},{2,14},{4,8},{6,10},{8,4},{10,6},{12,0},{14,2},{16,28},{18,... | collective-permute-start | bytes 172040 | tf_op jit(solution)/shard_map/ppermute | solution.py:458
  42.7 2.0 %collective-permute-done.11.refs_1_ = bf16[7,32,128]{2,1,0:T(8,128)(2,1)S(1)} collective-permute-done((bf16[7,32,128]{2,1,0:T(8,128)(2,1)S(1)}, bf16[7,32,128]{2,1,0:T(8,128)(2,1)S(1)}, u32[]{:S(2)}, u32[]{:S(2)}) %collective-permute-start.11) | collective-permute-done | bytes 57376 | tf_op jit(solution)/shard_map/ppermute | solution.py:458
  44.8 0.7 %shard_map.80.refs_2_ = f32[384,768]{1,0:T(8,128)S(1)} custom-call(bf16[4,7,32,128]{3,2,1,0:T(8,128)(2,1)S(1)} %shard_map.79.p_ref, bf16[6,128,384]{2,1,0:T(8,128)(2,1)S(1)} %shard_map.72.refs_8_.refs_0_, f32[6,128,384]{2,1,0:T(8,128)S(1)} %shard_map.78.refs_4_.refs_1_, bf16[768,768]{1,0:T(8,128)(2,1)S(1)} %get-tuple-element.74.refs_2_.refs_3_), custom_call_target="tpu_custom_call" | custom-call | flops 301989888 | bytes 3178496 | tf_op jit(solution)/shard_map/pallas_call | solution.py:424
  45.5 0.7 %collective-permute-done.18.p_ref = bf16[4,7,32,128]{3,2,1,0:T(8,128)(2,1)S(1)} collective-permute-done((bf16[4,7,32,128]{3,2,1,0:T(8,128)(2,1)S(1)}, bf16[4,7,32,128]{3,2,1,0:T(8,128)(2,1)S(1)}, u32[]{:S(2)}, u32[]{:S(2)}) %collective-permute-start.18) | collective-permute-done | bytes 229408 | tf_op jit(solution)/shard_map/ppermute | solution.py:458
  46.3 1.5 %shard_map.81 = bf16[3,128,768]{2,1,0:T(8,128)(2,1)} custom-call(bf16[4,7,32,128]{3,2,1,0:T(8,128)(2,1)S(1)} %collective-permute-done.18.p_ref, bf16[6,128,384]{2,1,0:T(8,128)(2,1)S(1)} %shard_map.72.refs_8_.refs_0_, f32[6,128,384]{2,1,0:T(8,128)S(1)} %shard_map.78.refs_4_.refs_1_, f32[384,768]{1,0:T(8,128)S(1)} %shard_map.80.refs_2_, ...), custom_call_target="tpu_custom_call" | custom-call | flops 301989888 | bytes 4358144 | tf_op jit(solution)/shard_map/pallas_call | solution.py:424
  (36 shorter events, 7.7 us)
Async XLA Ops:
  0.0 16.5 %collective-permute-start = (bf16[3,128,768]{2,1,0:T(8,128)(2,1)}, bf16[3,128,768]{2,1,0:T(8,128)(2,1)S(1)}, u32[]{:S(2)}, u32[]{:S(2)}) collective-permute-start(bf16[3,128,768]{2,1,0:T(8,128)(2,1)} %x_hbm.1), channel_id=1, source_target_pairs={{0,1},{1,0},{2,3},{3,2},{4,5},{5,4},{6,7},{7,6},{8,9},{9,8},{10,11... | collective-permute-start | bytes 1769480 | tf_op jit(solution)/shard_map/ppermute | solution.py:468
  5.8 1.8 %collective-permute-start.1 = (f32[4,6,32,128]{3,2,1,0:T(8,128)S(1)}, f32[4,6,32,128]{3,2,1,0:T(8,128)S(1)}, u32[]{:S(2)}, u32[]{:S(2)}) collective-permute-start(f32[4,6,32,128]{3,2,1,0:T(8,128)S(1)} %get-tuple-element.44.after_ref), channel_id=1, source_target_pairs={{0,2},{2,0},{4,6},{6,4},{8,10},{10,8},{12,14},{14,12},{16,18},{18,... | collective-permute-start | bytes 1179656 | tf_op jit(solution)/shard_map/ppermute | solution.py:458
  7.9 5.6 %collective-permute-start.2 = (bf16[7,32,128]{2,1,0:T(8,128)(2,1)S(1)}, bf16[7,32,128]{2,1,0:T(8,128)(2,1)S(1)}, u32[]{:S(2)}, u32[]{:S(2)}) collective-permute-start(bf16[7,32,128]{2,1,0:T(8,128)(2,1)S(1)} %get-tuple-element.47), channel_id=1, source_target_pairs={{0,12},{2,14},{4,8},{6,10},{8,4},{10,6},{12,0},{14,2},{16,28},{18,... | collective-permute-start | bytes 172040 | tf_op jit(solution)/shard_map/ppermute | solution.py:458
  10.5 4.2 %collective-permute-start.3 = (bf16[7,32,128]{2,1,0:T(8,128)(2,1)S(1)}, bf16[7,32,128]{2,1,0:T(8,128)(2,1)S(1)}, u32[]{:S(2)}, u32[]{:S(2)}) collective-permute-start(bf16[7,32,128]{2,1,0:T(8,128)(2,1)S(1)} %get-tuple-element.48), channel_id=1, source_target_pairs={{0,4},{2,6},{4,0},{6,2},{8,12},{10,14},{12,8},{14,10},{16,20},{18,... | collective-permute-start | bytes 172040 | tf_op jit(solution)/shard_map/ppermute | solution.py:458
  11.0 4.2 %collective-permute-start.4 = (bf16[7,32,128]{2,1,0:T(8,128)(2,1)S(1)}, bf16[7,32,128]{2,1,0:T(8,128)(2,1)S(1)}, u32[]{:S(2)}, u32[]{:S(2)}) collective-permute-start(bf16[7,32,128]{2,1,0:T(8,128)(2,1)S(1)} %get-tuple-element.49), channel_id=1, source_target_pairs={{0,8},{2,10},{4,12},{6,14},{8,0},{10,2},{12,4},{14,6},{16,24},{18,... | collective-permute-start | bytes 172040 | tf_op jit(solution)/shard_map/ppermute | solution.py:458
  11.5 5.1 %copy-start = (bf16[768,768]{1,0:T(8,128)(2,1)S(1)}, bf16[768,768]{1,0:T(8,128)(2,1)}, u32[]{:S(2)}) copy-start(bf16[768,768]{1,0:T(8,128)(2,1)} %wk_ref.3) | copy-start | bytes 3538948
  11.5 5.1 %copy-start.1 = (f32[768]{0:T(1024)S(1)}, f32[768]{0:T(1024)}, u32[]{:S(2)}) copy-start(f32[768]{0:T(1024)} %gain_ref.1) | copy-start | bytes 9220
  17.6 3.7 %collective-permute-start.5 = (f32[4,6,32,128]{3,2,1,0:T(8,128)S(1)}, f32[4,6,32,128]{3,2,1,0:T(8,128)S(1)}, u32[]{:S(2)}, u32[]{:S(2)}) collective-permute-start(f32[4,6,32,128]{3,2,1,0:T(8,128)S(1)} %get-tuple-element.54.after_ref), channel_id=1, source_target_pairs={{0,2},{2,0},{4,6},{6,4},{8,10},{10,8},{12,14},{14,12},{16,18},{18,... | collective-permute-start | bytes 1179656 | tf_op jit(solution)/shard_map/ppermute | solution.py:458
  17.7 11.2 %collective-permute-start.10 = (bf16[7,32,128]{2,1,0:T(8,128)(2,1)S(1)}, bf16[7,32,128]{2,1,0:T(8,128)(2,1)S(1)}, u32[]{:S(2)}, u32[]{:S(2)}) collective-permute-start(bf16[7,32,128]{2,1,0:T(8,128)(2,1)S(1)} %get-tuple-element.69), channel_id=1, source_target_pairs={{0,16},{2,18},{4,20},{6,22},{8,24},{10,26},{12,28},{14,30},{16,0},... | collective-permute-start | bytes 172040 | tf_op jit(solution)/shard_map/ppermute | solution.py:458
  21.5 5.1 %collective-permute-start.6 = (bf16[6,32,128]{2,1,0:T(8,128)(2,1)S(1)}, bf16[6,32,128]{2,1,0:T(8,128)(2,1)S(1)}, u32[]{:S(2)}, u32[]{:S(2)}) collective-permute-start(bf16[6,32,128]{2,1,0:T(8,128)(2,1)S(1)} %get-tuple-element.58), channel_id=1, source_target_pairs={{0,12},{2,14},{4,8},{6,10},{8,4},{10,6},{12,0},{14,2},{16,28},{18,... | collective-permute-start | bytes 147464 | tf_op jit(solution)/shard_map/ppermute | solution.py:458
  24.0 4.1 %collective-permute-start.7 = (bf16[6,32,128]{2,1,0:T(8,128)(2,1)S(1)}, bf16[6,32,128]{2,1,0:T(8,128)(2,1)S(1)}, u32[]{:S(2)}, u32[]{:S(2)}) collective-permute-start(bf16[6,32,128]{2,1,0:T(8,128)(2,1)S(1)} %get-tuple-element.59), channel_id=1, source_target_pairs={{0,4},{2,6},{4,0},{6,2},{8,12},{10,14},{12,8},{14,10},{16,20},{18,... | collective-permute-start | bytes 147464 | tf_op jit(solution)/shard_map/ppermute | solution.py:458
  24.6 4.1 %collective-permute-start.8 = (bf16[6,32,128]{2,1,0:T(8,128)(2,1)S(1)}, bf16[6,32,128]{2,1,0:T(8,128)(2,1)S(1)}, u32[]{:S(2)}, u32[]{:S(2)}) collective-permute-start(bf16[6,32,128]{2,1,0:T(8,128)(2,1)S(1)} %get-tuple-element.60), channel_id=1, source_target_pairs={{0,8},{2,10},{4,12},{6,14},{8,0},{10,2},{12,4},{14,6},{16,24},{18,... | collective-permute-start | bytes 147464 | tf_op jit(solution)/shard_map/ppermute | solution.py:458
  29.1 1.3 %collective-permute-start.14 = (bf16[6,32,128]{2,1,0:T(8,128)(2,1)S(1)}, bf16[6,32,128]{2,1,0:T(8,128)(2,1)S(1)}, u32[]{:S(2)}, u32[]{:S(2)}) collective-permute-start(bf16[6,32,128]{2,1,0:T(8,128)(2,1)S(1)} %get-tuple-element.73.mine_ref), channel_id=1, source_target_pairs={{0,2},{2,0},{4,6},{6,4},{8,10},{10,8},{12,14},{14,12},{16,18},{18,... | collective-permute-start | bytes 147464 | tf_op jit(solution)/shard_map/ppermute | solution.py:458
  30.4 7.8 %collective-permute-start.15 = (bf16[2,6,32,128]{3,2,1,0:T(8,128)(2,1)S(1)}, bf16[2,6,32,128]{3,2,1,0:T(8,128)(2,1)S(1)}, u32[]{:S(2)}, u32[]{:S(2)}) collective-permute-start(bf16[2,6,32,128]{3,2,1,0:T(8,128)(2,1)S(1)} %shard_map.76.share_ref), channel_id=1, source_target_pairs={{0,4},{2,10},{4,0},{6,14},{8,12},{10,2},{12,8},{14,6},{16,20},{18,... | collective-permute-start | bytes 294920 | tf_op jit(solution)/shard_map/ppermute | solution.py:574
  32.0 5.5 %collective-permute-start.9 = (bf16[6,32,128]{2,1,0:T(8,128)(2,1)S(1)}, bf16[6,32,128]{2,1,0:T(8,128)(2,1)S(1)}, u32[]{:S(2)}, u32[]{:S(2)}) collective-permute-start(bf16[6,32,128]{2,1,0:T(8,128)(2,1)S(1)} %get-tuple-element.68), channel_id=1, source_target_pairs={{0,16},{2,18},{4,20},{6,22},{8,24},{10,26},{12,28},{14,30},{16,0},... | collective-permute-start | bytes 147464 | tf_op jit(solution)/shard_map/ppermute | solution.py:458
  32.8 5.4 %collective-permute-start.16 = (bf16[6,32,128]{2,1,0:T(8,128)(2,1)S(1)}, bf16[6,32,128]{2,1,0:T(8,128)(2,1)S(1)}, u32[]{:S(2)}, u32[]{:S(2)}) collective-permute-start(bf16[6,32,128]{2,1,0:T(8,128)(2,1)S(1)} %get-tuple-element.73.mine_ref), channel_id=1, source_target_pairs={{0,12},{2,14},{4,8},{6,10},{8,4},{10,6},{12,0},{14,2},{16,28},{18,... | collective-permute-start | bytes 147464 | tf_op jit(solution)/shard_map/ppermute | solution.py:458
  38.3 3.6 %collective-permute-start.17 = (bf16[3,6,32,128]{3,2,1,0:T(8,128)(2,1)S(1)}, bf16[3,6,32,128]{3,2,1,0:T(8,128)(2,1)S(1)}, u32[]{:S(2)}, u32[]{:S(2)}) collective-permute-start(bf16[3,6,32,128]{3,2,1,0:T(8,128)(2,1)S(1)} %shard_map.77), channel_id=1, source_target_pairs={{0,2},{2,0},{4,6},{6,4},{8,10},{10,8},{12,14},{14,12},{16,18},{18,... | collective-permute-start | bytes 442376 | tf_op jit(solution)/shard_map/ppermute | solution.py:458
  38.4 4.4 %collective-permute-start.13 = (bf16[7,32,128]{2,1,0:T(8,128)(2,1)S(1)}, bf16[7,32,128]{2,1,0:T(8,128)(2,1)S(1)}, u32[]{:S(2)}, u32[]{:S(2)}) collective-permute-start(bf16[7,32,128]{2,1,0:T(8,128)(2,1)S(1)} %shard_map.75.refs_2_.refs_0_), channel_id=1, source_target_pairs={{0,8},{2,10},{4,12},{6,14},{8,0},{10,2},{12,4},{14,6},{16,24},{18,... | collective-permute-start | bytes 172040 | tf_op jit(solution)/shard_map/ppermute | solution.py:458
  38.4 4.3 %collective-permute-start.12 = (bf16[7,32,128]{2,1,0:T(8,128)(2,1)S(1)}, bf16[7,32,128]{2,1,0:T(8,128)(2,1)S(1)}, u32[]{:S(2)}, u32[]{:S(2)}) collective-permute-start(bf16[7,32,128]{2,1,0:T(8,128)(2,1)S(1)} %shard_map.75.refs_2_.refs_0_), channel_id=1, source_target_pairs={{0,4},{2,6},{4,0},{6,2},{8,12},{10,14},{12,8},{14,10},{16,20},{18,... | collective-permute-start | bytes 172040 | tf_op jit(solution)/shard_map/ppermute | solution.py:458
  39.6 5.1 %collective-permute-start.11 = (bf16[7,32,128]{2,1,0:T(8,128)(2,1)S(1)}, bf16[7,32,128]{2,1,0:T(8,128)(2,1)S(1)}, u32[]{:S(2)}, u32[]{:S(2)}) collective-permute-start(bf16[7,32,128]{2,1,0:T(8,128)(2,1)S(1)} %shard_map.75.refs_2_.refs_0_), channel_id=1, source_target_pairs={{0,12},{2,14},{4,8},{6,10},{8,4},{10,6},{12,0},{14,2},{16,28},{18,... | collective-permute-start | bytes 172040 | tf_op jit(solution)/shard_map/ppermute | solution.py:458
  44.7 1.6 %collective-permute-start.18 = (bf16[4,7,32,128]{3,2,1,0:T(8,128)(2,1)S(1)}, bf16[4,7,32,128]{3,2,1,0:T(8,128)(2,1)S(1)}, u32[]{:S(2)}, u32[]{:S(2)}) collective-permute-start(bf16[4,7,32,128]{3,2,1,0:T(8,128)(2,1)S(1)} %shard_map.79.p_ref), channel_id=1, source_target_pairs={{0,2},{2,0},{4,6},{6,4},{8,10},{10,8},{12,14},{14,12},{16,18},{18,... | collective-permute-start | bytes 688136 | tf_op jit(solution)/shard_map/ppermute | solution.py:458
